TPU v7x, 512 devices: a whole 4x8x8 slice. The times are simulated.
512 devices in a mesh: layer: 4 (over z_hi), facet: 128 (over y, z_lo, x, core).
Axes of the slice: x: 4, y: 8, z: 8 (z_hi: 4, z_lo: 2; z = z_hi * 2 + z_lo), core: 2. Of those that a mesh axis runs over, the one named last changes fastest.
Arguments:
- model_strip: bfloat16 [128, 2, 64, 8192], P('facet', None, None, 'layer'), may hold values from -6 to 6
- screen_angle: bfloat16 [4, 128, 64, 8192], P('layer', 'facet'), may hold values from -3.140625 to 3.140625
- facet_window: float32 [128, 8192], P('facet'), may hold values from 0.04 to 0.16
- facet_shift: int32 [128], P('facet'), may hold values from 0 to 8191
- kernel_taps: float32 [7], replicated, may hold values from 0.2 to 0.6
- plane_angle: float32 [4, 8], P('layer'), may hold values from -3.140625 to 3.140625
- u_cell: int32 [4, 128, 512], P('layer', 'facet'), may hold values from 0 to 63
- v_cell: int32 [4, 128, 512], P('layer', 'facet'), may hold values from 0 to 63
- w_plane: int32 [4, 128, 512], P('layer', 'facet'), may hold values from 0 to 7
- observed: float32 [4, 128, 2, 512], P('layer', 'facet'), may hold values from -6 to 6
Outputs:
- residual: float32 [4, 128, 2, 512], P('layer', 'facet')
- gradient: float32 [128, 2, 64, 8192], P('facet', None, None, 'layer')
All inputs are finite; a program needn't handle non-finite values.
Results may differ from a plain program's by a relative error of at most 0.009.
Values may be sent and summed in bfloat16 or wider, within the bound.
No kernel may reach another device: no remote copies, remote signals or barrier semaphores. Data moves between devices by JAX's collectives and lax.ppermute only.
A program may use at most 64 MiB of HBM per device.

v0:
```python
import math

import jax
import jax.numpy as jnp
import numpy as np
from jax import lax
from jax.experimental import pallas as pl
from jax.experimental.pallas import tpu as pltpu
from jax.sharding import PartitionSpec as P

STRIP_LEN = 8192
SUB_ROWS = 64
STRIP_COLS = 64
PLANES = 8
SUBGRIDS = 128
LAYERS = 4
COLS = STRIP_COLS // LAYERS
QUARTER = STRIP_LEN // LAYERS
LANES = 128
BLOCKS = QUARTER // LANES

back_gain = 8.0

Y, Z, X, CORE = 8, 2, 4, 2
ZX = Z * X
FACET_INDEX = np.arange(SUBGRIDS).reshape(Y, Z, X, CORE)
STAGE_ORDER = FACET_INDEX.transpose(3, 1, 2, 0).reshape(-1)
PLANE_GROUPS = FACET_INDEX.transpose(0, 3, 1, 2).reshape(-1, ZX).tolist()
GLOBAL_INDEX = np.arange(LAYERS * SUBGRIDS).reshape(LAYERS, Y, Z, X, CORE)
LINE_GROUPS = GLOBAL_INDEX.transpose(2, 3, 4, 1, 0).reshape(-1, Y * LAYERS).tolist()
CORE_SWAP = [(i, i ^ 1) for i in range(SUBGRIDS)]

VMEM_LIMIT = 48 * 1024 * 1024


def even_series(function, degree):
    series = np.polynomial.chebyshev.Chebyshev.interpolate(
        lambda t: function(np.sqrt(np.maximum((t + 1.0) * 0.5, 0.0)) * math.pi), degree
    )
    return [float(value) for value in np.polynomial.chebyshev.cheb2poly(series.coef)]


COSINE_SERIES = even_series(np.cos, 8)
SINE_SERIES = even_series(lambda x: np.sinc(x / math.pi), 8)


def phase_parts(angle):
    t = angle * angle * (2.0 / (math.pi * math.pi)) - 1.0
    cosine = jnp.full_like(t, COSINE_SERIES[-1])
    sine = jnp.full_like(t, SINE_SERIES[-1])
    for value in COSINE_SERIES[-2::-1]:
        cosine = cosine * t + value
    for value in SINE_SERIES[-2::-1]:
        sine = sine * t + value
    return cosine, sine * angle


def fourier_table(rows, length):
    turn_count = rows[:, None] * np.arange(length)[None, :] % length
    angles = 2.0 * math.pi / length * turn_count
    table = np.stack([np.cos(angles), -np.sin(angles)]) / math.sqrt(length)
    return table.astype(np.float32).astype(jnp.bfloat16)


def twiddle():
    turn_count = np.arange(SUB_ROWS)[:, None] * np.arange(LANES)[None, :] % STRIP_LEN
    angles = 2.0 * math.pi / STRIP_LEN * turn_count
    return (np.cos(angles).astype(np.float32), (-np.sin(angles)).astype(np.float32))


def first_tables():
    real, imag = fourier_table(np.arange(SUB_ROWS), SUB_ROWS)
    ahead = np.block([[real, -imag], [imag, real]])
    back = np.block([[real.T, imag.T], [-imag.T, real.T]])
    return (ahead, back)


def second_tables(order):
    real, imag = fourier_table(order, SUBGRIDS)
    ahead = np.block([[real.T, imag.T], [-imag.T, real.T]])
    back = np.block([[real, -imag], [imag, real]])
    return (ahead, back)


def pack_table():
    table = np.zeros((4, 2, LAYERS, COLS, LAYERS, 4, 2, COLS), np.float32)
    for r in range(4):
        for p in range(2):
            for layer in range(LAYERS):
                for c in range(COLS):
                    table[r, p, layer, c, layer, r, p, c] = 1.0
    return table.reshape(4 * LANES, 4 * LANES).astype(jnp.bfloat16)


def facet_factor(window, shift_cells, swapped):
    def staged(values):
        ordered = values.reshape(Y, Z, X, CORE, SUB_ROWS).transpose(4, 3, 1, 2, 0)
        mine = ordered.reshape(SUB_ROWS, CORE, SUBGRIDS // CORE)
        return jnp.where(swapped, mine[:, ::-1], mine).reshape(SUB_ROWS, SUBGRIDS)

    positions = jnp.arange(STRIP_LEN, dtype=jnp.int32)
    turn_count = positions * shift_cells % STRIP_LEN
    angles = 2.0 * math.pi / STRIP_LEN * turn_count.astype(jnp.float32)
    return (staged(window * jnp.cos(angles)), staged(-window * jnp.sin(angles)))


def forward_kernel(
    layer_ref, p0, p1, p2, p3, twist_real, twist_imag, first, second, factor_real, factor_imag,
    mine_ref, other_ref, screened, half,
):
    pieces = (p0, p1, p2, p3)
    q = layer_ref[0]
    table = first[...]
    for j in range(LAYERS):
        layer = (q + LAYERS - j) & 3

        def screen_block(t, carry, j=j):
            lanes = pl.ds(pl.multiple_of(t * LANES, LANES), LANES)
            for i in range(LAYERS):
                nq = (q + LAYERS - i) & 3
                cosine, sine = phase_parts(pieces[j][2 + nq, :, lanes].astype(jnp.float32))
                real = pieces[i][0, :, lanes].astype(jnp.float32)
                imag = pieces[i][1, :, lanes].astype(jnp.float32)
                rows = pl.ds(pl.multiple_of((nq * BLOCKS + t) * COLS, COLS), COLS)
                screened[0, rows, :] = real * cosine - imag * sine
                screened[1, rows, :] = real * sine + imag * cosine
            return carry

        lax.fori_loop(0, BLOCKS, screen_block, 0)

        def first_block(pair, carry, layer=layer):
            def column(part, c):
                return screened[part, pl.ds(c, SUB_ROWS, stride=COLS), :]

            c = pair * 2
            data = jnp.concatenate(
                [
                    jnp.concatenate([column(0, c), column(1, c)], axis=0),
                    jnp.concatenate([column(0, c + 1), column(1, c + 1)], axis=0),
                ],
                axis=1,
            ).astype(jnp.bfloat16)
            mixed = jnp.dot(table, data, preferred_element_type=jnp.float32)
            for h in range(2):
                real = mixed[:SUB_ROWS, h * LANES : (h + 1) * LANES]
                imag = mixed[SUB_ROWS:, h * LANES : (h + 1) * LANES]
                rows = pl.ds(layer * COLS + c + h, SUB_ROWS, stride=STRIP_COLS)
                half[0, rows, :] = real * twist_real[...] - imag * twist_imag[...]
                half[1, rows, :] = real * twist_imag[...] + imag * twist_real[...]
            return carry

        lax.fori_loop(0, COLS // 2, first_block, 0)

    weights = second[...]

    def second_block(pair, carry):
        rows = pl.ds(pl.multiple_of(pair * 2 * STRIP_COLS, 2 * STRIP_COLS), 2 * STRIP_COLS)
        data = jnp.concatenate([half[0, rows, :], half[1, rows, :]], axis=1).astype(jnp.bfloat16)
        spectrum = jnp.dot(data, weights, preferred_element_type=jnp.float32)
        blocks = []
        for h in range(2):
            real = spectrum[h * STRIP_COLS : (h + 1) * STRIP_COLS, :LANES]
            imag = spectrum[h * STRIP_COLS : (h + 1) * STRIP_COLS, LANES:]
            fr = factor_real[pl.ds(pair * 2 + h, 1), :]
            fi = factor_imag[pl.ds(pair * 2 + h, 1), :]
            turned = jnp.concatenate([real * fr - imag * fi, real * fi + imag * fr], axis=0).T
            blocks.append(turned.reshape(CORE * ZX, Y, LANES))
        both = jnp.concatenate(blocks, axis=1).astype(jnp.bfloat16)
        place = pl.ds(pl.multiple_of(pair * 2 * Y, 2 * Y), 2 * Y)
        mine_ref[:, place, :] = both[:ZX]
        other_ref[:, place, :] = both[ZX:]
        return carry

    lax.fori_loop(0, SUB_ROWS // 2, second_block, 0, unroll=2)


def pack_kernel(pieces, table, out_ref, total):
    total[...] = jnp.sum(pieces[...].astype(jnp.float32), axis=0)
    rows = []
    for y in range(Y):
        block = total[pl.ds(y, SUB_ROWS, stride=Y), :]
        rows.append(jnp.concatenate([block[r * 16 : (r + 1) * 16] for r in range(4)], axis=1))
    data = jnp.concatenate(rows, axis=0).astype(jnp.bfloat16)
    packed = jnp.dot(data, table[...], preferred_element_type=jnp.float32).astype(jnp.bfloat16)
    for y in range(Y):
        for layer in range(LAYERS):
            out_ref[y * LAYERS + layer] = packed[
                y * 16 : (y + 1) * 16, layer * LANES : (layer + 1) * LANES
            ]


def unpack_kernel(line, table, out_ref, total):
    data = jnp.concatenate(
        [
            jnp.concatenate([line[y * LAYERS + layer] for layer in range(LAYERS)], axis=1)
            for y in range(Y)
        ],
        axis=0,
    )
    grids = lax.dot_general(
        data, table[...], (((1,), (1,)), ((), ())), preferred_element_type=jnp.float32
    )
    for y in range(Y):
        for r in range(4):
            total[pl.ds(r * 16 * Y + y, 16, stride=Y), :] = grids[
                y * 16 : (y + 1) * 16, r * LANES : (r + 1) * LANES
            ]
    block = total[...].astype(jnp.bfloat16)
    for copy in range(ZX):
        out_ref[copy] = block


def backward_kernel(
    layer_ref, mine, other, p0, p1, p2, p3, twist_real, twist_imag, first, second, factor_real,
    factor_imag, o0, o1, o2, o3, half, phases, total,
):
    pieces = (p0, p1, p2, p3)
    q = layer_ref[0]
    rows_of = SUB_ROWS * COLS
    for j in range(LAYERS):

        def phase_block(t, carry, j=j):
            lanes = pl.ds(pl.multiple_of(t * LANES, LANES), LANES)
            for nq in range(LAYERS):
                cosine, sine = phase_parts(pieces[j][2 + nq, :, lanes].astype(jnp.float32))
                rows = pl.ds(
                    pl.multiple_of(j * rows_of + (nq * BLOCKS + t) * COLS, COLS), COLS
                )
                phases[0, rows, :] = cosine
                phases[1, rows, :] = sine
            return carry

        lax.fori_loop(0, BLOCKS, phase_block, 0)

    weights = second[...]

    def second_block(pair, carry):
        place = pl.ds(pl.multiple_of(pair * 2 * Y, 2 * Y), 2 * Y)
        both = jnp.concatenate([mine[:, place, :], other[:, place, :]], axis=0).astype(jnp.float32)
        data = []
        for h in range(2):
            turned = both[:, h * Y : (h + 1) * Y, :].reshape(SUBGRIDS, LANES).T
            real = turned[:STRIP_COLS]
            imag = turned[STRIP_COLS:]
            fr = factor_real[pl.ds(pair * 2 + h, 1), :]
            fi = factor_imag[pl.ds(pair * 2 + h, 1), :]
            data.append(
                jnp.concatenate([real * fr + imag * fi, imag * fr - real * fi], axis=1)
            )
        data = jnp.concatenate(data, axis=0).astype(jnp.bfloat16)
        mixed = jnp.dot(data, weights, preferred_element_type=jnp.float32)
        for h in range(2):
            real = mixed[h * STRIP_COLS : (h + 1) * STRIP_COLS, :LANES]
            imag = mixed[h * STRIP_COLS : (h + 1) * STRIP_COLS, LANES:]
            tr = twist_real[pl.ds(pair * 2 + h, 1), :]
            ti = twist_imag[pl.ds(pair * 2 + h, 1), :]
            rows = pl.ds(pair * 2 + h, STRIP_COLS, stride=SUB_ROWS)
            half[0, rows, :] = real * tr + imag * ti
            half[1, rows, :] = imag * tr - real * ti
        return carry

    lax.fori_loop(0, SUB_ROWS // 2, second_block, 0, unroll=2)

    table = first[...]

    def first_block(pair, carry):
        c = pair * 2
        sums = [None] * 4
        for j in range(LAYERS):
            layer = (q + LAYERS - j) & 3

            def column(part, h):
                start = (layer * COLS + c + h) * SUB_ROWS
                return half[part, pl.ds(pl.multiple_of(start, SUB_ROWS), SUB_ROWS), :]

            data = jnp.concatenate(
                [
                    jnp.concatenate([column(0, 0), column(1, 0)], axis=0),
                    jnp.concatenate([column(0, 1), column(1, 1)], axis=0),
                ],
                axis=1,
            ).astype(jnp.bfloat16)
            image = jnp.dot(table, data, preferred_element_type=jnp.float32)
            for h in range(2):
                real = image[:SUB_ROWS, h * LANES : (h + 1) * LANES]
                imag = image[SUB_ROWS:, h * LANES : (h + 1) * LANES]
                rows = pl.ds(j * rows_of + c + h, SUB_ROWS, stride=COLS)
                cosine = phases[0, rows, :]
                sine = phases[1, rows, :]
                for part, term in enumerate(
                    (real * cosine + imag * sine, imag * cosine - real * sine)
                ):
                    place = 2 * h + part
                    sums[place] = term if j == 0 else sums[place] + term
        for h in range(2):
            for part in range(2):
                total[part, pl.ds(c + h, SUB_ROWS, stride=COLS), :] = back_gain * sums[2 * h + part]
        return carry

    lax.fori_loop(0, COLS // 2, first_block, 0)

    def leave_block(t, carry):
        lanes = pl.ds(pl.multiple_of(t * LANES, LANES), LANES)
        for i, out_ref in enumerate((o0, o1, o2, o3)):
            nq = (q + i) & 3
            rows = pl.ds(pl.multiple_of((nq * BLOCKS + t) * COLS, COLS), COLS)
            for part in range(2):
                out_ref[part, :, lanes] = total[part, rows, :].astype(out_ref.dtype)
        return carry

    lax.fori_loop(0, BLOCKS, leave_block, 0)


def join_kernel(layer_ref, r0, r1, r2, r3, out_ref):
    q = layer_ref[0]
    for i, piece in enumerate((r0, r1, r2, r3)):
        source = (q + LAYERS - i) & 3
        rows = pl.ds(pl.multiple_of(source * COLS, COLS), COLS)
        for part in range(2):
            out_ref[part, rows, :] = piece[part].astype(jnp.float32)


def on_core(kernel, name, out_shape, scratch=(), scalars=0, inputs=1):
    specs = [pl.BlockSpec(memory_space=pltpu.SMEM)] * scalars
    specs += [pl.BlockSpec(memory_space=pltpu.VMEM)] * inputs
    is_list = isinstance(out_shape, (list, tuple))
    one = pl.BlockSpec(memory_space=pltpu.VMEM)
    return pl.pallas_call(
        kernel,
        name=name,
        out_shape=out_shape,
        in_specs=specs,
        out_specs=[one] * len(out_shape) if is_list else one,
        scratch_shapes=list(scratch),
        compiler_params=pltpu.CompilerParams(vmem_limit_bytes=VMEM_LIMIT),
    )


def shaped(shape, kind):
    return jax.ShapeDtypeStruct(shape, kind)


def forward(layer, pieces, factor_real, factor_imag, second):
    blocks = shaped((ZX, SUB_ROWS * Y, LANES), jnp.bfloat16)
    twist_real, twist_imag = twiddle()
    return on_core(
        forward_kernel,
        "ahead",
        [blocks, blocks],
        (
            pltpu.VMEM((2, SUB_ROWS * COLS, LANES), jnp.float32),
            pltpu.VMEM((2, SUB_ROWS * STRIP_COLS, LANES), jnp.float32),
        ),
        1,
        10,
    )(layer, *pieces, twist_real, twist_imag, first_tables()[0], second, factor_real, factor_imag)


def backward(layer, mine, other, pieces, factor_real, factor_imag, second):
    twist_real, twist_imag = twiddle()
    piece = (2, COLS, QUARTER)
    return on_core(
        backward_kernel,
        "back",
        [shaped(piece, jnp.float32)] + [shaped(piece, jnp.bfloat16)] * 3,
        (
            pltpu.VMEM((2, SUB_ROWS * STRIP_COLS, LANES), jnp.float32),
            pltpu.VMEM((2, LAYERS * SUB_ROWS * COLS, LANES), jnp.float32),
            pltpu.VMEM((2, SUB_ROWS * COLS, LANES), jnp.float32),
        ),
        1,
        12,
    )(
        layer, mine, other, *pieces, twist_real, twist_imag, first_tables()[1], second,
        factor_real, factor_imag,
    )


def spread(cell_index, length, kernel_taps):
    tap_count = kernel_taps.shape[0]
    offset = (jnp.arange(length, dtype=jnp.int32)[None, :] - cell_index[:, None]) % length
    wanted = (jnp.arange(tap_count, dtype=jnp.int32) - tap_count // 2) % length
    matches = (offset[:, :, None] == wanted[None, None, :]).astype(jnp.float32)
    return jnp.sum(matches * kernel_taps, axis=2)


def degrid(subgrid, row_cells, column_cells, plane, observed_vis, angle_table, kernel_taps):
    row_weights = spread(row_cells, SUB_ROWS, kernel_taps)
    column_weights = spread(column_cells, STRIP_COLS, kernel_taps)
    kernel_rows = jnp.dot(row_weights, subgrid, precision=lax.Precision.HIGHEST)
    model_real = jnp.sum(kernel_rows[:, :STRIP_COLS] * column_weights, axis=1)
    model_imag = jnp.sum(kernel_rows[:, STRIP_COLS:] * column_weights, axis=1)
    plane_pick = (plane[:, None] == jnp.arange(PLANES, dtype=jnp.int32)[None, :]).astype(
        jnp.float32
    )
    phase_angle = jnp.sum(plane_pick * angle_table[None, :], axis=1)
    cosine = jnp.cos(phase_angle)
    sine_part = jnp.sin(phase_angle)
    residual_real = observed_vis[0] - (model_real * cosine - model_imag * sine_part)
    residual_imag = observed_vis[1] - (model_real * sine_part + model_imag * cosine)
    weighted_real = residual_real * cosine + residual_imag * sine_part
    weighted_imag = residual_imag * cosine - residual_real * sine_part
    spread_cols = jnp.concatenate(
        [weighted_real[:, None] * column_weights, weighted_imag[:, None] * column_weights], axis=1
    )
    adjoint = jnp.dot(row_weights.T, spread_cols, precision=lax.Precision.HIGHEST)
    return (jnp.stack([residual_real, residual_imag]), adjoint)


def exchange(blocks, axes, groups=None):
    return lax.all_to_all(
        blocks, axes, split_axis=0, concat_axis=0, tiled=True, axis_index_groups=groups
    )


def local(
    model_strip,
    screen_angle,
    facet_window,
    facet_shift,
    kernel_taps,
    plane_angle,
    u_cell,
    v_cell,
    w_plane,
    observed,
):
    layer = lax.axis_index("layer").astype(jnp.int32)
    swapped = lax.axis_index("facet") % CORE == 1
    layer_of = layer.reshape(1)

    joined = jnp.concatenate(
        [
            model_strip[0].reshape(2, LAYERS, COLS, QUARTER).transpose(1, 0, 2, 3),
            screen_angle[0, 0].reshape(LAYERS, COLS, LAYERS, QUARTER).transpose(0, 2, 1, 3),
        ],
        axis=1,
    )
    pieces = []
    for shift in range(LAYERS):
        piece = lax.dynamic_index_in_dim(joined, (layer + shift) % LAYERS, 0, keepdims=False)
        if shift:
            piece = lax.ppermute(piece, "layer", [(i, (i + shift) % LAYERS) for i in range(LAYERS)])
        pieces.append(piece)

    factor_real, factor_imag = facet_factor(facet_window[0], facet_shift[0], swapped)
    plain = second_tables(STAGE_ORDER)
    crossed = second_tables(np.roll(STAGE_ORDER, SUBGRIDS // CORE))
    second_ahead = jnp.where(swapped, crossed[0], plain[0])
    second_back = jnp.where(swapped, crossed[1], plain[1])
    mine, other = forward(layer_of, pieces, factor_real, factor_imag, second_ahead)

    arrived = lax.ppermute(other, "facet", CORE_SWAP)
    pair_sum = (mine.astype(jnp.float32) + arrived.astype(jnp.float32)).astype(jnp.bfloat16)
    plane_terms = exchange(pair_sum, "facet", PLANE_GROUPS)
    table = pack_table()
    piece = (SUB_ROWS // 4, 2 * STRIP_COLS)
    packed = on_core(
        pack_kernel,
        "pack",
        shaped((Y * LAYERS, *piece), jnp.bfloat16),
        (pltpu.VMEM((SUB_ROWS * Y, LANES), jnp.float32),),
        0,
        2,
    )(plane_terms, table)
    line_sum = jnp.sum(
        exchange(packed, ("layer", "facet"), LINE_GROUPS)
        .reshape(Y, LAYERS, *piece)
        .astype(jnp.float32),
        axis=0,
    )
    subgrid = (
        line_sum.reshape(LAYERS, SUB_ROWS // 4, 4, 2, COLS)
        .transpose(2, 1, 3, 0, 4)
        .reshape(SUB_ROWS, 2 * STRIP_COLS)
    )

    residual, adjoint = degrid(
        subgrid, u_cell[0, 0], v_cell[0, 0], w_plane[0, 0], observed[0, 0], plane_angle[0], kernel_taps
    )

    sent = (
        adjoint.astype(jnp.bfloat16)
        .reshape(4, SUB_ROWS // 4, 2, LAYERS, COLS)
        .transpose(3, 1, 0, 2, 4)
        .reshape(1, LAYERS, *piece)
    )
    line = exchange(
        jnp.broadcast_to(sent, (Y, LAYERS, *piece)).reshape(Y * LAYERS, *piece),
        ("layer", "facet"),
        LINE_GROUPS,
    )
    copies = on_core(
        unpack_kernel,
        "unpack",
        shaped((ZX, SUB_ROWS * Y, LANES), jnp.bfloat16),
        (pltpu.VMEM((SUB_ROWS * Y, LANES), jnp.float32),),
        0,
        2,
    )(line, table)
    mine_grids = exchange(copies, "facet", PLANE_GROUPS)
    other_grids = lax.ppermute(mine_grids, "facet", CORE_SWAP)
    leaving = backward(
        layer_of, mine_grids, other_grids, pieces, factor_real, factor_imag, second_back
    )
    arriving = [leaving[0]]
    for shift in range(1, LAYERS):
        arriving.append(
            lax.ppermute(
                leaving[shift], "layer", [(i, (i + shift) % LAYERS) for i in range(LAYERS)]
            )
        )
    gradient = on_core(
        join_kernel, "join", shaped((2, STRIP_COLS, QUARTER), jnp.float32), (), 1, 4
    )(layer_of, *arriving)
    return (residual[None, None], gradient[None])


def solution(mesh):
    return jax.shard_map(
        local,
        mesh=mesh,
        in_specs=(
            P("facet", None, None, "layer"),
            P("layer", "facet", None, None),
            P("facet", None),
            P("facet"),
            P(),
            P("layer", None),
            P("layer", "facet", None),
            P("layer", "facet", None),
            P("layer", "facet", None),
            P("layer", "facet", None, None),
        ),
        out_specs=(P("layer", "facet", None, None), P("facet", None, None, "layer")),
        check_vma=False,
    )
```

profile of v0, /device:TPU:1, one launch (start us, length us, event | category | flops | bytes accessed | tf_op | source)
XLA Modules:
  0.0 198.7 jit_solution(2853118130612918973)
XLA Ops:
  0.7 1.8 reshape_squeeze.7
  3.9 6.8 %collective-permute-start = (bf16[6,16,2048]{2,1,0:T(8,128)(2,1)S(1)}, bf16[6,16,2048]{2,1,0:T(8,128)(2,1)S(1)}, u32[]{:S(2)}, u32[]{:S(2)}) collective-permute-start(bf16[6,16,2048]{2,1,0:T(8,128)(2,1)S(1)} %get-tuple-element.23), channel_id=1, source_target_pairs={{0,128},{128,256},{256,384},{384,0},{1,129},{129,257},{257,385},{3... | collective-permute-start | bytes 1179656 | tf_op jit(solution)/shard_map/ppermute | solution.py:443
  10.7 8.8 %collective-permute-start.1 = (bf16[6,16,2048]{2,1,0:T(8,128)(2,1)S(1)}, bf16[6,16,2048]{2,1,0:T(8,128)(2,1)S(1)}, u32[]{:S(2)}, u32[]{:S(2)}) collective-permute-start(bf16[6,16,2048]{2,1,0:T(8,128)(2,1)S(1)} %get-tuple-element.24), channel_id=1, source_target_pairs={{0,256},{128,384},{256,0},{384,128},{1,257},{129,385},{257,1},{385... | collective-permute-start | bytes 1179656 | tf_op jit(solution)/shard_map/ppermute | solution.py:443
  19.5 3.4 %collective-permute-start.2 = (bf16[6,16,2048]{2,1,0:T(8,128)(2,1)S(1)}, bf16[6,16,2048]{2,1,0:T(8,128)(2,1)S(1)}, u32[]{:S(2)}, u32[]{:S(2)}) collective-permute-start(bf16[6,16,2048]{2,1,0:T(8,128)(2,1)S(1)} %get-tuple-element.21), channel_id=1, source_target_pairs={{0,384},{128,0},{256,128},{384,256},{1,385},{129,1},{257,129},{385... | collective-permute-start | bytes 1179656 | tf_op jit(solution)/shard_map/ppermute | solution.py:443
  26.3 8.9 %collective-permute-done.1.p2 = bf16[6,16,2048]{2,1,0:T(8,128)(2,1)S(1)} collective-permute-done((bf16[6,16,2048]{2,1,0:T(8,128)(2,1)S(1)}, bf16[6,16,2048]{2,1,0:T(8,128)(2,1)S(1)}, u32[]{:S(2)}, u32[]{:S(2)}) %collective-permute-start.1) | collective-permute-done | bytes 393248 | tf_op jit(solution)/shard_map/ppermute | solution.py:443
  35.3 20.2 %collective-permute-done.2.p3 = bf16[6,16,2048]{2,1,0:T(8,128)(2,1)S(1)} collective-permute-done((bf16[6,16,2048]{2,1,0:T(8,128)(2,1)S(1)}, bf16[6,16,2048]{2,1,0:T(8,128)(2,1)S(1)}, u32[]{:S(2)}, u32[]{:S(2)}) %collective-permute-start.2) | collective-permute-done | bytes 393248 | tf_op jit(solution)/shard_map/ppermute | solution.py:443
  55.5 17.0 %ahead.1 = (bf16[8,512,128]{2,1,0:T(8,128)(2,1)S(1)}, bf16[8,512,128]{2,1,0:T(8,128)(2,1)S(1)}) custom-call(s32[1]{0:T(128)} %bitcast.2.layer_ref, bf16[6,16,2048]{2,1,0:T(8,128)(2,1)S(1)} %get-tuple-element.22.p0, bf16[6,16,2048]{2,1,0:T(8,128)(2,1)S(1)} %collective-permute-done.p1, bf16[6,16,2048]{2,1,0:T(8,128)(2,1)S(1)} %collective-permute-done.1.p2, ...), custom_call_target="tpu_custom_call" | custom-call | tf_op jit(solution)/shard_map/ahead/pallas_call | solution.py:346
  72.5 2.5 %collective-permute-start.3 = (bf16[8,512,128]{2,1,0:T(8,128)(2,1)S(1)}, bf16[8,512,128]{2,1,0:T(8,128)(2,1)S(1)}, u32[]{:S(2)}, u32[]{:S(2)}) collective-permute-start(bf16[8,512,128]{2,1,0:T(8,128)(2,1)S(1)} %get-tuple-element.9), channel_id=1, source_target_pairs={{0,1},{1,0},{2,3},{3,2},{4,5},{5,4},{6,7},{7,6},{8,9},{9,8},{10,11... | collective-permute-start | bytes 3145736 | tf_op jit(solution)/shard_map/ppermute | solution.py:453
  75.0 2.3 %collective-permute-done.3 = bf16[8,512,128]{2,1,0:T(8,128)(2,1)S(1)} collective-permute-done((bf16[8,512,128]{2,1,0:T(8,128)(2,1)S(1)}, bf16[8,512,128]{2,1,0:T(8,128)(2,1)S(1)}, u32[]{:S(2)}, u32[]{:S(2)}) %collective-permute-start.3) | collective-permute-done | bytes 1048608 | tf_op jit(solution)/shard_map/ppermute | solution.py:453
  77.2 1.2 add_convert_fusion
  78.5 4.2 %all-to-all-start = ((bf16[8,512,128]{2,1,0:T(8,128)(2,1)}), bf16[8,512,128]{2,1,0:T(8,128)(2,1)S(1)}, u32[]{:S(2)}, u32[]{:S(2)}) async-start(bf16[8,512,128]{2,1,0:T(8,128)(2,1)} %add_convert_fusion), calls=%async_computation | async-start | bytes 2097152 | tf_op jit(solution)/shard_map/all_to_all | solution.py:411
  83.5 14.1 %all-to-all-done.pieces = bf16[8,512,128]{2,1,0:T(8,128)(2,1)S(1)} async-done(((bf16[8,512,128]{2,1,0:T(8,128)(2,1)}), bf16[8,512,128]{2,1,0:T(8,128)(2,1)S(1)}, u32[]{:S(2)}, u32[]{:S(2)}) %all-to-all-start) | async-done | bytes 1048608 | tf_op jit(solution)/shard_map/all_to_all | solution.py:411
  98.7 10.4 %all-to-all-start.1 = ((bf16[32,16,128]{2,1,0:T(8,128)(2,1)}), bf16[32,16,128]{2,1,0:T(8,128)(2,1)S(1)}, u32[]{:S(2)}, u32[]{:S(2)}) async-start(bf16[32,16,128]{2,1,0:T(8,128)(2,1)} %pack.1), calls=%async_computation.1 | async-start | bytes 262144 | tf_op jit(solution)/shard_map/all_to_all | solution.py:411
  110.0 10.4 %all-to-all-done.1 = bf16[32,16,128]{2,1,0:T(8,128)(2,1)S(1)} async-done(((bf16[32,16,128]{2,1,0:T(8,128)(2,1)}), bf16[32,16,128]{2,1,0:T(8,128)(2,1)S(1)}, u32[]{:S(2)}, u32[]{:S(2)}) %all-to-all-start.1) | async-done | bytes 131104 | tf_op jit(solution)/shard_map/all_to_all | solution.py:411
  122.6 14.5 %all_to_all.20.line = bf16[32,16,128]{2,1,0:T(8,128)(2,1)S(1)} all-to-all(bf16[32,16,128]{2,1,0:T(8,128)(2,1)S(1)} %bitcast.60), channel_id=1, replica_groups={{0,128,256,384,16,144,272,400,32,160,288,416,48,176,304,432,64,192,320,..., dimensions={0} | all-to-all | bytes 262144 | tf_op jit(solution)/shard_map/all_to_all | solution.py:411
  137.5 16.7 %all_to_all.21.mine = bf16[8,512,128]{2,1,0:T(8,128)(2,1)S(1)} all-to-all(bf16[8,512,128]{2,1,0:T(8,128)(2,1)S(1)} %unpack.1), channel_id=1, replica_groups={{0,2,4,6,8,10,12,14},{1,3,5,7,9,11,13,15},{16,18,20,22,24,26,28,30},{17..., dimensions={0} | all-to-all | bytes 2097152 | tf_op jit(solution)/shard_map/all_to_all | solution.py:411
  154.2 6.1 %collective-permute-start.4 = (bf16[8,512,128]{2,1,0:T(8,128)(2,1)S(1)}, bf16[8,512,128]{2,1,0:T(8,128)(2,1)S(1)}, u32[]{:S(2)}, u32[]{:S(2)}) collective-permute-start(bf16[8,512,128]{2,1,0:T(8,128)(2,1)S(1)} %all_to_all.21.mine), channel_id=1, source_target_pairs={{0,1},{1,0},{2,3},{3,2},{4,5},{5,4},{6,7},{7,6},{8,9},{9,8},{10,11... | collective-permute-start | bytes 3145736 | tf_op jit(solution)/shard_map/ppermute | solution.py:502
  160.3 2.2 %collective-permute-done.4.other = bf16[8,512,128]{2,1,0:T(8,128)(2,1)S(1)} collective-permute-done((bf16[8,512,128]{2,1,0:T(8,128)(2,1)S(1)}, bf16[8,512,128]{2,1,0:T(8,128)(2,1)S(1)}, u32[]{:S(2)}, u32[]{:S(2)}) %collective-permute-start.4) | collective-permute-done | bytes 1048608 | tf_op jit(solution)/shard_map/ppermute | solution.py:502
  162.5 13.2 %back.1 = (f32[2,16,2048]{2,1,0:T(8,128)S(1)}, bf16[2,16,2048]{2,1,0:T(8,128)(2,1)S(1)}, bf16[2,16,2048]{2,1,0:T(8,128)(2,1)S(1)}, bf16[2,16,2048]{2,1,0:T(8,128)(2,1)S(1)}) custom-call(s32[1]{0:T(128)} %bitcast.2.layer_ref, bf16[8,512,128]{2,1,0:T(8,128)(2,1)S(1)} %all_to_all.21.mine, bf16[8,512,128]{2,1,0:T(8,128)(2,1)S(1)} %collective-permute-done.4.other, ...), custom_call_target="tpu_custom_call" | custom-call | tf_op jit(solution)/shard_map/back/pallas_call | solution.py:362
  175.7 2.7 %collective-permute-start.5 = (bf16[2,16,2048]{2,1,0:T(8,128)(2,1)S(1)}, bf16[2,16,2048]{2,1,0:T(8,128)(2,1)S(1)}, u32[]{:S(2)}, u32[]{:S(2)}) collective-permute-start(bf16[2,16,2048]{2,1,0:T(8,128)(2,1)S(1)} %get-tuple-element.11), channel_id=1, source_target_pairs={{0,128},{128,256},{256,384},{384,0},{1,129},{129,257},{257,385},{3... | collective-permute-start | bytes 393224 | tf_op jit(solution)/shard_map/ppermute | solution.py:509
  178.4 4.1 %collective-permute-start.6 = (bf16[2,16,2048]{2,1,0:T(8,128)(2,1)S(1)}, bf16[2,16,2048]{2,1,0:T(8,128)(2,1)S(1)}, u32[]{:S(2)}, u32[]{:S(2)}) collective-permute-start(bf16[2,16,2048]{2,1,0:T(8,128)(2,1)S(1)} %get-tuple-element.12), channel_id=1, source_target_pairs={{0,256},{128,384},{256,0},{384,128},{1,257},{129,385},{257,1},{385... | collective-permute-start | bytes 393224 | tf_op jit(solution)/shard_map/ppermute | solution.py:509
  182.5 4.2 %collective-permute-start.7 = (bf16[2,16,2048]{2,1,0:T(8,128)(2,1)S(1)}, bf16[2,16,2048]{2,1,0:T(8,128)(2,1)S(1)}, u32[]{:S(2)}, u32[]{:S(2)}) collective-permute-start(bf16[2,16,2048]{2,1,0:T(8,128)(2,1)S(1)} %get-tuple-element.13), channel_id=1, source_target_pairs={{0,384},{128,0},{256,128},{384,256},{1,385},{129,1},{257,129},{385... | collective-permute-start | bytes 393224 | tf_op jit(solution)/shard_map/ppermute | solution.py:509
  187.4 3.5 %collective-permute-done.6.r2 = bf16[2,16,2048]{2,1,0:T(8,128)(2,1)S(1)} collective-permute-done((bf16[2,16,2048]{2,1,0:T(8,128)(2,1)S(1)}, bf16[2,16,2048]{2,1,0:T(8,128)(2,1)S(1)}, u32[]{:S(2)}, u32[]{:S(2)}) %collective-permute-start.6) | collective-permute-done | bytes 131104 | tf_op jit(solution)/shard_map/ppermute | solution.py:509
  190.9 6.7 %collective-permute-done.7.r3 = bf16[2,16,2048]{2,1,0:T(8,128)(2,1)S(1)} collective-permute-done((bf16[2,16,2048]{2,1,0:T(8,128)(2,1)S(1)}, bf16[2,16,2048]{2,1,0:T(8,128)(2,1)S(1)}, u32[]{:S(2)}, u32[]{:S(2)}) %collective-permute-start.7) | collective-permute-done | bytes 131104 | tf_op jit(solution)/shard_map/ppermute | solution.py:509
  (75 shorter events, 10.9 us)
Async XLA Ops:
  3.7 19.8 %copy-start.10 = (f32[1,8192]{1,0:T(1,128)S(1)}, f32[1,8192]{1,0:T(1,128)}, u32[]{:S(2)}) copy-start(f32[1,8192]{1,0:T(1,128)} %param.23) | copy-start | bytes 98308
  3.8 22.5 %copy-start.8 = (bf16[256,256]{1,0:T(8,128)(2,1)S(1)}, bf16[256,256]{1,0:T(8,128)(2,1)}, u32[]{:S(2)}) copy-start(bf16[256,256]{1,0:T(8,128)(2,1)} %constant.139.clone) | copy-start | bytes 393220
  3.8 22.5 %copy-start.9 = (bf16[256,256]{1,0:T(8,128)(2,1)S(1)}, bf16[256,256]{1,0:T(8,128)(2,1)}, u32[]{:S(2)}) copy-start(bf16[256,256]{1,0:T(8,128)(2,1)} %constant.140.clone) | copy-start | bytes 393220
  3.8 51.6 %copy-start.1 = (f32[64,128]{1,0:T(8,128)S(1)}, f32[64,128]{1,0:T(8,128)}, u32[]{:S(2)}) copy-start(f32[64,128]{1,0:T(8,128)} %constant.143.clone.twist_real) | copy-start | bytes 98308
  3.9 51.6 %copy-start.2 = (f32[64,128]{1,0:T(8,128)S(1)}, f32[64,128]{1,0:T(8,128)}, u32[]{:S(2)}) copy-start(f32[64,128]{1,0:T(8,128)} %constant.144.clone.twist_imag) | copy-start | bytes 98308
  3.9 51.6 %copy-start.4 = (bf16[128,128]{1,0:T(8,128)(2,1)S(1)}, bf16[128,128]{1,0:T(8,128)(2,1)}, u32[]{:S(2)}) copy-start(bf16[128,128]{1,0:T(8,128)(2,1)} %constant.145.clone.first) | copy-start | bytes 98308
  3.9 22.4 %collective-permute-start = (bf16[6,16,2048]{2,1,0:T(8,128)(2,1)S(1)}, bf16[6,16,2048]{2,1,0:T(8,128)(2,1)S(1)}, u32[]{:S(2)}, u32[]{:S(2)}) collective-permute-start(bf16[6,16,2048]{2,1,0:T(8,128)(2,1)S(1)} %get-tuple-element.23), channel_id=1, source_target_pairs={{0,128},{128,256},{256,384},{384,0},{1,129},{129,257},{257,385},{3... | collective-permute-start | bytes 1179656 | tf_op jit(solution)/shard_map/ppermute | solution.py:443
  10.7 24.6 %collective-permute-start.1 = (bf16[6,16,2048]{2,1,0:T(8,128)(2,1)S(1)}, bf16[6,16,2048]{2,1,0:T(8,128)(2,1)S(1)}, u32[]{:S(2)}, u32[]{:S(2)}) collective-permute-start(bf16[6,16,2048]{2,1,0:T(8,128)(2,1)S(1)} %get-tuple-element.24), channel_id=1, source_target_pairs={{0,256},{128,384},{256,0},{384,128},{1,257},{129,385},{257,1},{385... | collective-permute-start | bytes 1179656 | tf_op jit(solution)/shard_map/ppermute | solution.py:443
  19.5 35.9 %collective-permute-start.2 = (bf16[6,16,2048]{2,1,0:T(8,128)(2,1)S(1)}, bf16[6,16,2048]{2,1,0:T(8,128)(2,1)S(1)}, u32[]{:S(2)}, u32[]{:S(2)}) collective-permute-start(bf16[6,16,2048]{2,1,0:T(8,128)(2,1)S(1)} %get-tuple-element.21), channel_id=1, source_target_pairs={{0,384},{128,0},{256,128},{384,256},{1,385},{129,1},{257,129},{385... | collective-permute-start | bytes 1179656 | tf_op jit(solution)/shard_map/ppermute | solution.py:443
  72.5 4.7 %collective-permute-start.3 = (bf16[8,512,128]{2,1,0:T(8,128)(2,1)S(1)}, bf16[8,512,128]{2,1,0:T(8,128)(2,1)S(1)}, u32[]{:S(2)}, u32[]{:S(2)}) collective-permute-start(bf16[8,512,128]{2,1,0:T(8,128)(2,1)S(1)} %get-tuple-element.9), channel_id=1, source_target_pairs={{0,1},{1,0},{2,3},{3,2},{4,5},{5,4},{6,7},{7,6},{8,9},{9,8},{10,11... | collective-permute-start | bytes 3145736 | tf_op jit(solution)/shard_map/ppermute | solution.py:453
  78.5 4.8 %copy-start.12 = (s32[1,1,512]{2,1,0:T(1,128)S(1)}, s32[1,1,512]{2,1,0:T(1,128)}, u32[]{:S(2)}) copy-start(s32[1,1,512]{2,1,0:T(1,128)} %param.28) | copy-start | bytes 6148
  78.5 4.8 %copy-start.13 = (s32[1,1,512]{2,1,0:T(1,128)S(1)}, s32[1,1,512]{2,1,0:T(1,128)}, u32[]{:S(2)}) copy-start(s32[1,1,512]{2,1,0:T(1,128)} %param.27) | copy-start | bytes 6148
  78.5 19.1 %copy-start = (bf16[512,512]{1,0:T(8,128)(2,1)S(1)}, bf16[512,512]{1,0:T(8,128)(2,1)}, u32[]{:S(2)}) copy-start(bf16[512,512]{1,0:T(8,128)(2,1)} %constant.146.clone.table) | copy-start | bytes 1572868
  78.5 19.1 %all-to-all-start = ((bf16[8,512,128]{2,1,0:T(8,128)(2,1)}), bf16[8,512,128]{2,1,0:T(8,128)(2,1)S(1)}, u32[]{:S(2)}, u32[]{:S(2)}) async-start(bf16[8,512,128]{2,1,0:T(8,128)(2,1)} %add_convert_fusion), calls=%async_computation | async-start | bytes 2097152 | tf_op jit(solution)/shard_map/all_to_all | solution.py:411
  83.5 25.6 %copy-start.16 = (f32[7]{0:T(128)S(1)}, f32[7]{0:T(128)}, u32[]{:S(2)}) copy-start(f32[7]{0:T(128)} %param.25) | copy-start | bytes 88
  83.5 26.5 %copy-start.11 = (f32[1,1,2,512]{3,2,1,0:T(2,128)S(1)}, f32[1,1,2,512]{3,2,1,0:T(2,128)}, u32[]{:S(2)}) copy-start(f32[1,1,2,512]{3,2,1,0:T(2,128)} %param.30) | copy-start | bytes 12292
  98.7 21.8 %all-to-all-start.1 = ((bf16[32,16,128]{2,1,0:T(8,128)(2,1)}), bf16[32,16,128]{2,1,0:T(8,128)(2,1)S(1)}, u32[]{:S(2)}, u32[]{:S(2)}) async-start(bf16[32,16,128]{2,1,0:T(8,128)(2,1)} %pack.1), calls=%async_computation.1 | async-start | bytes 262144 | tf_op jit(solution)/shard_map/all_to_all | solution.py:411
  137.5 22.8 %copy-start.6 = (bf16[256,256]{1,0:T(8,128)(2,1)S(1)}, bf16[256,256]{1,0:T(8,128)(2,1)}, u32[]{:S(2)}) copy-start(bf16[256,256]{1,0:T(8,128)(2,1)} %constant.141.clone) | copy-start | bytes 393220
  137.5 22.8 %copy-start.7 = (bf16[256,256]{1,0:T(8,128)(2,1)S(1)}, bf16[256,256]{1,0:T(8,128)(2,1)}, u32[]{:S(2)}) copy-start(bf16[256,256]{1,0:T(8,128)(2,1)} %constant.142.clone) | copy-start | bytes 393220
  137.5 25.1 %copy-start.3 = (bf16[128,128]{1,0:T(8,128)(2,1)S(1)}, bf16[128,128]{1,0:T(8,128)(2,1)}, u32[]{:S(2)}) copy-start(bf16[128,128]{1,0:T(8,128)(2,1)} %constant.147.clone.first) | copy-start | bytes 98308
  154.2 8.3 %collective-permute-start.4 = (bf16[8,512,128]{2,1,0:T(8,128)(2,1)S(1)}, bf16[8,512,128]{2,1,0:T(8,128)(2,1)S(1)}, u32[]{:S(2)}, u32[]{:S(2)}) collective-permute-start(bf16[8,512,128]{2,1,0:T(8,128)(2,1)S(1)} %all_to_all.21.mine), channel_id=1, source_target_pairs={{0,1},{1,0},{2,3},{3,2},{4,5},{5,4},{6,7},{7,6},{8,9},{9,8},{10,11... | collective-permute-start | bytes 3145736 | tf_op jit(solution)/shard_map/ppermute | solution.py:502
  175.7 11.7 %collective-permute-start.5 = (bf16[2,16,2048]{2,1,0:T(8,128)(2,1)S(1)}, bf16[2,16,2048]{2,1,0:T(8,128)(2,1)S(1)}, u32[]{:S(2)}, u32[]{:S(2)}) collective-permute-start(bf16[2,16,2048]{2,1,0:T(8,128)(2,1)S(1)} %get-tuple-element.11), channel_id=1, source_target_pairs={{0,128},{128,256},{256,384},{384,0},{1,129},{129,257},{257,385},{3... | collective-permute-start | bytes 393224 | tf_op jit(solution)/shard_map/ppermute | solution.py:509
  178.4 12.5 %collective-permute-start.6 = (bf16[2,16,2048]{2,1,0:T(8,128)(2,1)S(1)}, bf16[2,16,2048]{2,1,0:T(8,128)(2,1)S(1)}, u32[]{:S(2)}, u32[]{:S(2)}) collective-permute-start(bf16[2,16,2048]{2,1,0:T(8,128)(2,1)S(1)} %get-tuple-element.12), channel_id=1, source_target_pairs={{0,256},{128,384},{256,0},{384,128},{1,257},{129,385},{257,1},{385... | collective-permute-start | bytes 393224 | tf_op jit(solution)/shard_map/ppermute | solution.py:509
  182.5 15.1 %collective-permute-start.7 = (bf16[2,16,2048]{2,1,0:T(8,128)(2,1)S(1)}, bf16[2,16,2048]{2,1,0:T(8,128)(2,1)S(1)}, u32[]{:S(2)}, u32[]{:S(2)}) collective-permute-start(bf16[2,16,2048]{2,1,0:T(8,128)(2,1)S(1)} %get-tuple-element.13), channel_id=1, source_target_pairs={{0,384},{128,0},{256,128},{384,256},{1,385},{129,1},{257,129},{385... | collective-permute-start | bytes 393224 | tf_op jit(solution)/shard_map/ppermute | solution.py:509
  (3 other events, 10.5 us)
where the time goes:
time: 199 us
  waiting for transfers between devices  68.4 us (34%)
  starting transfers between devices  53.1 us (27%)
  Pallas kernels  32.7 us (16%)
  blocking collectives  31.2 us (16%)
  other arithmetic  5.64 us (3%)
  local copies, waits for them, and re-layouts  5.01 us (3%)
    all_to_all x2, blocking collectives, exchange(): lax.all_to_all(blocks, axes, split_axis=0, concat_axis=0, tiled=True, axi...  31.2 us
    ppermute x3, waiting for transfers between devices, local(): lax.ppermute(piece, 'layer', [(i, (i + shift) % LAYERS) for i in range(LA...  29.1 us
    all_to_all x2, waiting for transfers between devices, exchange(): lax.all_to_all(blocks, axes, split_axis=0, concat_axis=0, tiled=True, axi...  24.6 us
    ppermute x3, starting transfers between devices, local(): lax.ppermute(piece, 'layer', [(i, (i + shift) % LAYERS) for i in range(LA...  19 us
    pallas_call x1, Pallas kernels, forward(): on_core(forward_kernel, 'ahead', [blocks, blocks], (pltpu.VMEM((2, SUB_RO...  17 us
    all_to_all x2, starting transfers between devices, exchange(): lax.all_to_all(blocks, axes, split_axis=0, concat_axis=0, tiled=True, axi...  14.5 us
    pallas_call x1, Pallas kernels, backward(): on_core(backward_kernel, 'back', [shaped(piece, jnp.float32)] + [shaped(p...  13.2 us
    ppermute x3, starting transfers between devices, local(): lax.ppermute(leaving[shift], 'layer', [(i, (i + shift) % LAYERS) for i in...  11 us
  transfers between devices with their start and end apart: 10, of which 8 were waited for; matrix products, arithmetic and copies ran while one was open for 3% of the time, Pallas kernels for 0%

commit v1 on v0

--- a/solution.py
+++ b/solution.py
@@ -30,7 +30,11 @@
 LINE_GROUPS = GLOBAL_INDEX.transpose(2, 3, 4, 1, 0).reshape(-1, Y * LAYERS).tolist()
 CORE_SWAP = [(i, i ^ 1) for i in range(SUBGRIDS)]
 
-VMEM_LIMIT = 48 * 1024 * 1024
+VMEM_LIMIT = 32 * 1024 * 1024
+
+COL_PITCH = 24
+LINE_PITCH = 72
+PHASE_ROWS = SUB_ROWS * COL_PITCH
 
 
 def even_series(function, degree):
@@ -105,57 +109,68 @@
 
 
 def forward_kernel(
-    layer_ref, p0, p1, p2, p3, twist_real, twist_imag, first, second, factor_real, factor_imag,
-    mine_ref, other_ref, screened, half,
+    pieces, twist_real, twist_imag, first, second, factor_real, factor_imag,
+    mine_ref, other_ref, phases, strip, half,
 ):
-    pieces = (p0, p1, p2, p3)
-    q = layer_ref[0]
     table = first[...]
-    for j in range(LAYERS):
-        layer = (q + LAYERS - j) & 3
-
-        def screen_block(t, carry, j=j):
+
+    def strip_block(t, carry):
+        lanes = pl.ds(pl.multiple_of(t * LANES, LANES), LANES)
+        for nq in range(LAYERS):
+            rows = pl.ds(pl.multiple_of((nq * BLOCKS + t) * COL_PITCH, 8), COLS)
+            for part in range(2):
+                strip[part, rows, :] = pieces[nq, part, :, lanes].astype(jnp.float32)
+        return carry
+
+    lax.fori_loop(0, BLOCKS, strip_block, 0, unroll=2)
+    for layer in range(LAYERS):
+
+        def phase_block(t, carry, layer=layer):
             lanes = pl.ds(pl.multiple_of(t * LANES, LANES), LANES)
-            for i in range(LAYERS):
-                nq = (q + LAYERS - i) & 3
-                cosine, sine = phase_parts(pieces[j][2 + nq, :, lanes].astype(jnp.float32))
-                real = pieces[i][0, :, lanes].astype(jnp.float32)
-                imag = pieces[i][1, :, lanes].astype(jnp.float32)
-                rows = pl.ds(pl.multiple_of((nq * BLOCKS + t) * COLS, COLS), COLS)
-                screened[0, rows, :] = real * cosine - imag * sine
-                screened[1, rows, :] = real * sine + imag * cosine
+            for nq in range(LAYERS):
+                cosine, sine = phase_parts(pieces[layer, 2 + nq, :, lanes].astype(jnp.float32))
+                rows = pl.ds(
+                    pl.multiple_of(layer * PHASE_ROWS + (nq * BLOCKS + t) * COL_PITCH, 8), COLS
+                )
+                phases[0, rows, :] = cosine
+                phases[1, rows, :] = sine
             return carry
 
-        lax.fori_loop(0, BLOCKS, screen_block, 0)
+        lax.fori_loop(0, BLOCKS, phase_block, 0, unroll=4)
 
         def first_block(pair, carry, layer=layer):
-            def column(part, c):
-                return screened[part, pl.ds(c, SUB_ROWS, stride=COLS), :]
-
             c = pair * 2
-            data = jnp.concatenate(
-                [
-                    jnp.concatenate([column(0, c), column(1, c)], axis=0),
-                    jnp.concatenate([column(0, c + 1), column(1, c + 1)], axis=0),
-                ],
-                axis=1,
-            ).astype(jnp.bfloat16)
+            data = []
+            for h in range(2):
+                column = pl.ds(c + h, SUB_ROWS, stride=COL_PITCH)
+                turn = pl.ds(layer * PHASE_ROWS + c + h, SUB_ROWS, stride=COL_PITCH)
+                real, imag = strip[0, column, :], strip[1, column, :]
+                cosine, sine = phases[0, turn, :], phases[1, turn, :]
+                data.append(
+                    jnp.concatenate(
+                        [real * cosine - imag * sine, real * sine + imag * cosine], axis=0
+                    )
+                )
+            data = jnp.concatenate(data, axis=1).astype(jnp.bfloat16)
             mixed = jnp.dot(table, data, preferred_element_type=jnp.float32)
             for h in range(2):
                 real = mixed[:SUB_ROWS, h * LANES : (h + 1) * LANES]
                 imag = mixed[SUB_ROWS:, h * LANES : (h + 1) * LANES]
-                rows = pl.ds(layer * COLS + c + h, SUB_ROWS, stride=STRIP_COLS)
+                rows = pl.ds(layer * COLS + c + h, SUB_ROWS, stride=LINE_PITCH)
                 half[0, rows, :] = real * twist_real[...] - imag * twist_imag[...]
                 half[1, rows, :] = real * twist_imag[...] + imag * twist_real[...]
             return carry
 
-        lax.fori_loop(0, COLS // 2, first_block, 0)
+        lax.fori_loop(0, COLS // 2, first_block, 0, unroll=4)
 
     weights = second[...]
 
     def second_block(pair, carry):
-        rows = pl.ds(pl.multiple_of(pair * 2 * STRIP_COLS, 2 * STRIP_COLS), 2 * STRIP_COLS)
-        data = jnp.concatenate([half[0, rows, :], half[1, rows, :]], axis=1).astype(jnp.bfloat16)
+        data = []
+        for h in range(2):
+            rows = pl.ds(pl.multiple_of((pair * 2 + h) * LINE_PITCH, 8), STRIP_COLS)
+            data.append(jnp.concatenate([half[0, rows, :], half[1, rows, :]], axis=1))
+        data = jnp.concatenate(data, axis=0).astype(jnp.bfloat16)
         spectrum = jnp.dot(data, weights, preferred_element_type=jnp.float32)
         blocks = []
         for h in range(2):
@@ -171,7 +186,7 @@
         other_ref[:, place, :] = both[ZX:]
         return carry
 
-    lax.fori_loop(0, SUB_ROWS // 2, second_block, 0, unroll=2)
+    lax.fori_loop(0, SUB_ROWS // 2, second_block, 0, unroll=8)
 
 
 def pack_kernel(pieces, table, out_ref, total):
@@ -211,27 +226,9 @@
 
 
 def backward_kernel(
-    layer_ref, mine, other, p0, p1, p2, p3, twist_real, twist_imag, first, second, factor_real,
-    factor_imag, o0, o1, o2, o3, half, phases, total,
+    mine, other, phases, twist_real, twist_imag, first, second, factor_real, factor_imag,
+    out_ref, half, total,
 ):
-    pieces = (p0, p1, p2, p3)
-    q = layer_ref[0]
-    rows_of = SUB_ROWS * COLS
-    for j in range(LAYERS):
-
-        def phase_block(t, carry, j=j):
-            lanes = pl.ds(pl.multiple_of(t * LANES, LANES), LANES)
-            for nq in range(LAYERS):
-                cosine, sine = phase_parts(pieces[j][2 + nq, :, lanes].astype(jnp.float32))
-                rows = pl.ds(
-                    pl.multiple_of(j * rows_of + (nq * BLOCKS + t) * COLS, COLS), COLS
-                )
-                phases[0, rows, :] = cosine
-                phases[1, rows, :] = sine
-            return carry
-
-        lax.fori_loop(0, BLOCKS, phase_block, 0)
-
     weights = second[...]
 
     def second_block(pair, carry):
@@ -254,12 +251,12 @@
             imag = mixed[h * STRIP_COLS : (h + 1) * STRIP_COLS, LANES:]
             tr = twist_real[pl.ds(pair * 2 + h, 1), :]
             ti = twist_imag[pl.ds(pair * 2 + h, 1), :]
-            rows = pl.ds(pair * 2 + h, STRIP_COLS, stride=SUB_ROWS)
+            rows = pl.ds(pair * 2 + h, STRIP_COLS, stride=LINE_PITCH)
             half[0, rows, :] = real * tr + imag * ti
             half[1, rows, :] = imag * tr - real * ti
         return carry
 
-    lax.fori_loop(0, SUB_ROWS // 2, second_block, 0, unroll=2)
+    lax.fori_loop(0, SUB_ROWS // 2, second_block, 0, unroll=8)
 
     table = first[...]
 
@@ -267,11 +264,10 @@
         c = pair * 2
         sums = [None] * 4
         for j in range(LAYERS):
-            layer = (q + LAYERS - j) & 3
-
-            def column(part, h):
-                start = (layer * COLS + c + h) * SUB_ROWS
-                return half[part, pl.ds(pl.multiple_of(start, SUB_ROWS), SUB_ROWS), :]
+
+            def column(part, h, j=j):
+                start = (j * COLS + c + h) * LINE_PITCH
+                return half[part, pl.ds(pl.multiple_of(start, 8), SUB_ROWS), :]
 
             data = jnp.concatenate(
                 [
@@ -284,7 +280,7 @@
             for h in range(2):
                 real = image[:SUB_ROWS, h * LANES : (h + 1) * LANES]
                 imag = image[SUB_ROWS:, h * LANES : (h + 1) * LANES]
-                rows = pl.ds(j * rows_of + c + h, SUB_ROWS, stride=COLS)
+                rows = pl.ds(j * PHASE_ROWS + c + h, SUB_ROWS, stride=COL_PITCH)
                 cosine = phases[0, rows, :]
                 sine = phases[1, rows, :]
                 for part, term in enumerate(
@@ -294,42 +290,30 @@
                     sums[place] = term if j == 0 else sums[place] + term
         for h in range(2):
             for part in range(2):
-                total[part, pl.ds(c + h, SUB_ROWS, stride=COLS), :] = back_gain * sums[2 * h + part]
+                total[part, pl.ds(c + h, SUB_ROWS, stride=COL_PITCH), :] = back_gain * sums[2 * h + part]
         return carry
 
-    lax.fori_loop(0, COLS // 2, first_block, 0)
+    lax.fori_loop(0, COLS // 2, first_block, 0, unroll=4)
 
     def leave_block(t, carry):
         lanes = pl.ds(pl.multiple_of(t * LANES, LANES), LANES)
-        for i, out_ref in enumerate((o0, o1, o2, o3)):
-            nq = (q + i) & 3
-            rows = pl.ds(pl.multiple_of((nq * BLOCKS + t) * COLS, COLS), COLS)
+        for nq in range(LAYERS):
+            rows = pl.ds(pl.multiple_of((nq * BLOCKS + t) * COL_PITCH, 8), COLS)
             for part in range(2):
-                out_ref[part, :, lanes] = total[part, rows, :].astype(out_ref.dtype)
+                out_ref[nq, part, :, lanes] = total[part, rows, :].astype(jnp.bfloat16)
         return carry
 
-    lax.fori_loop(0, BLOCKS, leave_block, 0)
-
-
-def join_kernel(layer_ref, r0, r1, r2, r3, out_ref):
-    q = layer_ref[0]
-    for i, piece in enumerate((r0, r1, r2, r3)):
-        source = (q + LAYERS - i) & 3
-        rows = pl.ds(pl.multiple_of(source * COLS, COLS), COLS)
-        for part in range(2):
-            out_ref[part, rows, :] = piece[part].astype(jnp.float32)
-
-
-def on_core(kernel, name, out_shape, scratch=(), scalars=0, inputs=1):
-    specs = [pl.BlockSpec(memory_space=pltpu.SMEM)] * scalars
-    specs += [pl.BlockSpec(memory_space=pltpu.VMEM)] * inputs
+    lax.fori_loop(0, BLOCKS, leave_block, 0, unroll=2)
+
+
+def on_core(kernel, name, out_shape, scratch, inputs):
     is_list = isinstance(out_shape, (list, tuple))
     one = pl.BlockSpec(memory_space=pltpu.VMEM)
     return pl.pallas_call(
         kernel,
         name=name,
         out_shape=out_shape,
-        in_specs=specs,
+        in_specs=[one] * inputs,
         out_specs=[one] * len(out_shape) if is_list else one,
         scratch_shapes=list(scratch),
         compiler_params=pltpu.CompilerParams(vmem_limit_bytes=VMEM_LIMIT),
@@ -340,38 +324,34 @@
     return jax.ShapeDtypeStruct(shape, kind)
 
 
-def forward(layer, pieces, factor_real, factor_imag, second):
+def forward(pieces, factor_real, factor_imag, second):
     blocks = shaped((ZX, SUB_ROWS * Y, LANES), jnp.bfloat16)
     twist_real, twist_imag = twiddle()
     return on_core(
         forward_kernel,
         "ahead",
-        [blocks, blocks],
+        [blocks, blocks, shaped((2, LAYERS * PHASE_ROWS, LANES), jnp.float32)],
         (
-            pltpu.VMEM((2, SUB_ROWS * COLS, LANES), jnp.float32),
-            pltpu.VMEM((2, SUB_ROWS * STRIP_COLS, LANES), jnp.float32),
+            pltpu.VMEM((2, PHASE_ROWS, LANES), jnp.float32),
+            pltpu.VMEM((2, SUB_ROWS * LINE_PITCH, LANES), jnp.float32),
         ),
-        1,
-        10,
-    )(layer, *pieces, twist_real, twist_imag, first_tables()[0], second, factor_real, factor_imag)
-
-
-def backward(layer, mine, other, pieces, factor_real, factor_imag, second):
+        7,
+    )(pieces, twist_real, twist_imag, first_tables()[0], second, factor_real, factor_imag)
+
+
+def backward(mine, other, phases, factor_real, factor_imag, second):
     twist_real, twist_imag = twiddle()
-    piece = (2, COLS, QUARTER)
     return on_core(
         backward_kernel,
         "back",
-        [shaped(piece, jnp.float32)] + [shaped(piece, jnp.bfloat16)] * 3,
+        shaped((LAYERS, 2, COLS, QUARTER), jnp.bfloat16),
         (
-            pltpu.VMEM((2, SUB_ROWS * STRIP_COLS, LANES), jnp.float32),
-            pltpu.VMEM((2, LAYERS * SUB_ROWS * COLS, LANES), jnp.float32),
-            pltpu.VMEM((2, SUB_ROWS * COLS, LANES), jnp.float32),
+            pltpu.VMEM((2, STRIP_COLS * LINE_PITCH, LANES), jnp.float32),
+            pltpu.VMEM((2, PHASE_ROWS, LANES), jnp.float32),
         ),
-        1,
-        12,
+        9,
     )(
-        layer, mine, other, *pieces, twist_real, twist_imag, first_tables()[1], second,
+        mine, other, phases, twist_real, twist_imag, first_tables()[1], second,
         factor_real, factor_imag,
     )
 
@@ -425,9 +405,7 @@
     w_plane,
     observed,
 ):
-    layer = lax.axis_index("layer").astype(jnp.int32)
     swapped = lax.axis_index("facet") % CORE == 1
-    layer_of = layer.reshape(1)
 
     joined = jnp.concatenate(
         [
@@ -436,19 +414,14 @@
         ],
         axis=1,
     )
-    pieces = []
-    for shift in range(LAYERS):
-        piece = lax.dynamic_index_in_dim(joined, (layer + shift) % LAYERS, 0, keepdims=False)
-        if shift:
-            piece = lax.ppermute(piece, "layer", [(i, (i + shift) % LAYERS) for i in range(LAYERS)])
-        pieces.append(piece)
+    pieces = exchange(joined, "layer")
 
     factor_real, factor_imag = facet_factor(facet_window[0], facet_shift[0], swapped)
     plain = second_tables(STAGE_ORDER)
     crossed = second_tables(np.roll(STAGE_ORDER, SUBGRIDS // CORE))
     second_ahead = jnp.where(swapped, crossed[0], plain[0])
     second_back = jnp.where(swapped, crossed[1], plain[1])
-    mine, other = forward(layer_of, pieces, factor_real, factor_imag, second_ahead)
+    mine, other, phases = forward(pieces, factor_real, factor_imag, second_ahead)
 
     arrived = lax.ppermute(other, "facet", CORE_SWAP)
     pair_sum = (mine.astype(jnp.float32) + arrived.astype(jnp.float32)).astype(jnp.bfloat16)
@@ -460,7 +433,6 @@
         "pack",
         shaped((Y * LAYERS, *piece), jnp.bfloat16),
         (pltpu.VMEM((SUB_ROWS * Y, LANES), jnp.float32),),
-        0,
         2,
     )(plane_terms, table)
     line_sum = jnp.sum(
@@ -495,25 +467,18 @@
         "unpack",
         shaped((ZX, SUB_ROWS * Y, LANES), jnp.bfloat16),
         (pltpu.VMEM((SUB_ROWS * Y, LANES), jnp.float32),),
-        0,
         2,
     )(line, table)
     mine_grids = exchange(copies, "facet", PLANE_GROUPS)
     other_grids = lax.ppermute(mine_grids, "facet", CORE_SWAP)
-    leaving = backward(
-        layer_of, mine_grids, other_grids, pieces, factor_real, factor_imag, second_back
-    )
-    arriving = [leaving[0]]
-    for shift in range(1, LAYERS):
-        arriving.append(
-            lax.ppermute(
-                leaving[shift], "layer", [(i, (i + shift) % LAYERS) for i in range(LAYERS)]
-            )
-        )
-    gradient = on_core(
-        join_kernel, "join", shaped((2, STRIP_COLS, QUARTER), jnp.float32), (), 1, 4
-    )(layer_of, *arriving)
-    return (residual[None, None], gradient[None])
+    leaving = backward(mine_grids, other_grids, phases, factor_real, factor_imag, second_back)
+    gradient = (
+        exchange(leaving, "layer")
+        .transpose(1, 0, 2, 3)
+        .reshape(1, 2, STRIP_COLS, QUARTER)
+        .astype(jnp.float32)
+    )
+    return (residual[None, None], gradient)
 
 
 def solution(mesh):

time: 199 us -> 182 us (0.915)
  Pallas kernels: 32.7 us -> 13.7 us
  local copies, waits for them, and re-layouts: 5.01 us -> 11.5 us
  starting transfers between devices: 53.1 us -> 50.2 us
  waiting for transfers between devices: 68.4 us -> 65.7 us
    ppermute x6 -> x0, waiting for transfers between devices: 39.4 us -> none  [the longest x3 29.1 us: local(): lax.ppermute(piece, 'layer', [(i, (i + shift) % LAYERS) for i in range(LA...]
    all_to_all x2 -> x4, waiting for transfers between devices: 24.6 us -> 61.2 us  [exchange(): lax.all_to_all(blocks, axes, split_axis=0, concat_axis=0, tiled=True, axi...]
    ppermute x6 -> x0, starting transfers between devices: 30 us -> none  [the longest x3 19 us: local(): lax.ppermute(piece, 'layer', [(i, (i + shift) % LAYERS) for i in range(LA...]
    all_to_all x2 -> x4, starting transfers between devices: 14.5 us -> 39.4 us  [exchange(): lax.all_to_all(blocks, axes, split_axis=0, concat_axis=0, tiled=True, axi...]
    pallas_call x3 -> x2, Pallas kernels: 31.3 us -> 12.3 us  [the longest x1 7.56 us: forward(): on_core(forward_kernel, 'ahead', [blocks, blocks, shaped((2, LAYERS * PHA...]
    unnamed x35 -> x39, local copies, waits for them, and re-layouts: 1.07 us -> 6.5 us
    ppermute x1, starting transfers between devices: 2.45 us -> 4.79 us  [local(): arrived = lax.ppermute(other, 'facet', CORE_SWAP)]
  transfers between devices with their start and end apart: 10 -> 6, of which waited for: 8 -> 6; matrix products, arithmetic and copies ran while one was open for 3% -> 2% of each run, Pallas kernels for 0% -> 0%
where the time goes in v1:
time: 182 us; the launch traced here: 180 us
  waiting for transfers between devices  65.7 us (36%)
  starting transfers between devices  50.2 us (28%)
  blocking collectives  31.1 us (17%)
  Pallas kernels  13.7 us (8%)
  local copies, waits for them, and re-layouts  11.5 us (6%)
  other arithmetic  5.73 us (3%)
    all_to_all x4, waiting for transfers between devices, exchange(): lax.all_to_all(blocks, axes, split_axis=0, concat_axis=0, tiled=True, axi...  61.2 us
    all_to_all x4, starting transfers between devices, exchange(): lax.all_to_all(blocks, axes, split_axis=0, concat_axis=0, tiled=True, axi...  39.4 us
    all_to_all x2, blocking collectives, exchange(): lax.all_to_all(blocks, axes, split_axis=0, concat_axis=0, tiled=True, axi...  31.1 us
    pallas_call x1, Pallas kernels, forward(): on_core(forward_kernel, 'ahead', [blocks, blocks, shaped((2, LAYERS * PHA...  7.56 us
    unnamed x39, local copies, waits for them, and re-layouts  6.5 us
    ppermute x1, starting transfers between devices, local(): other_grids = lax.ppermute(mine_grids, 'facet', CORE_SWAP)  6.04 us
    ppermute x1, starting transfers between devices, local(): arrived = lax.ppermute(other, 'facet', CORE_SWAP)  4.79 us
    pallas_call x1, Pallas kernels, backward(): on_core(backward_kernel, 'back', shaped((LAYERS, 2, COLS, QUARTER), jnp.b...  4.75 us
  transfers between devices with their start and end apart: 6, of which 6 were waited for; matrix products, arithmetic and copies ran while one was open for 2% of the time, Pallas kernels for 0%

profile of v1, /device:TPU:1, one launch (start us, length us, event | category | flops | bytes accessed | tf_op | source)
XLA Modules:
  0.0 180.4 jit_solution(9794363548667083096)
XLA Ops:
  0.6 1.8 %reshape_squeeze.7 = bf16[4,16,4,2048]{3,2,1,0:T(4,128)(2,1)S(1)} reshape(bf16[1,1,64,8192]{3,2,1,0:T(8,128)(2,1)} %param.22) | data formatting | bytes 2097152 | tf_op jit(solution)/shard_map/reshape;squeeze | solution.py:413
  3.6 1.3 pad_maximum_fusion
  4.9 11.0 %all-to-all-start = ((bf16[4,6,16,2048]{3,2,1,0:T(8,128)(2,1)}), bf16[4,6,16,2048]{3,2,1,0:T(8,128)(2,1)S(1)}, u32[]{:S(2)}, u32[]{:S(2)}) async-start(bf16[4,6,16,2048]{3,2,1,0:T(8,128)(2,1)} %pad_maximum_fusion), calls=%async_computation | async-start | bytes 3145728 | tf_op jit(solution)/shard_map/all_to_all | solution.py:391
  17.9 1.1 multiply_bitcast_fusion
  19.3 22.0 %all-to-all-done.pieces = bf16[4,6,16,2048]{3,2,1,0:T(8,128)(2,1)S(1)} async-done(((bf16[4,6,16,2048]{3,2,1,0:T(8,128)(2,1)}), bf16[4,6,16,2048]{3,2,1,0:T(8,128)(2,1)S(1)}, u32[]{:S(2)}, u32[]{:S(2)}) %all-to-all-start) | async-done | bytes 1572896 | tf_op jit(solution)/shard_map/all_to_all | solution.py:391
  41.3 7.6 %ahead.1 = (bf16[8,512,128]{2,1,0:T(8,128)(2,1)S(1)}, bf16[8,512,128]{2,1,0:T(8,128)(2,1)S(1)}, f32[2,6144,128]{2,1,0:T(8,128)S(1)}) custom-call(bf16[4,6,16,2048]{3,2,1,0:T(8,128)(2,1)S(1)} %all-to-all-done.pieces, f32[64,128]{1,0:T(8,128)S(1)} %copy-done.3, f32[64,128]{1,0:T(8,128)S(1)} %copy-done.4, bf16[128,128]{1,0:T(8,128)(2,1)S(1)} %copy-done.6, ...), custom_call_target="tpu_custom_call" | custom-call | tf_op jit(solution)/shard_map/ahead/pallas_call | solution.py:330
  48.9 2.7 %copy-done = f32[2,6144,128]{2,1,0:T(8,128)} copy-done((f32[2,6144,128]{2,1,0:T(8,128)}, f32[2,6144,128]{2,1,0:T(8,128)S(1)}, u32[]{:S(2)}) %copy-start) | copy-done | bytes 6291480
  51.6 4.8 %collective-permute-start = (bf16[8,512,128]{2,1,0:T(8,128)(2,1)S(1)}, bf16[8,512,128]{2,1,0:T(8,128)(2,1)S(1)}, u32[]{:S(2)}, u32[]{:S(2)}) collective-permute-start(bf16[8,512,128]{2,1,0:T(8,128)(2,1)S(1)} %get-tuple-element.6), channel_id=1, source_target_pairs={{0,1},{1,0},{2,3},{3,2},{4,5},{5,4},{6,7},{7,6},{8,9},{9,8},{10,11... | collective-permute-start | bytes 3145736 | tf_op jit(solution)/shard_map/ppermute | solution.py:426
  56.4 2.3 %collective-permute-done = bf16[8,512,128]{2,1,0:T(8,128)(2,1)S(1)} collective-permute-done((bf16[8,512,128]{2,1,0:T(8,128)(2,1)S(1)}, bf16[8,512,128]{2,1,0:T(8,128)(2,1)S(1)}, u32[]{:S(2)}, u32[]{:S(2)}) %collective-permute-start) | collective-permute-done | bytes 1048608 | tf_op jit(solution)/shard_map/ppermute | solution.py:426
  58.6 1.2 add_convert_fusion
  59.9 16.8 %all-to-all-start.1 = ((bf16[8,512,128]{2,1,0:T(8,128)(2,1)}), bf16[8,512,128]{2,1,0:T(8,128)(2,1)S(1)}, u32[]{:S(2)}, u32[]{:S(2)}) async-start(bf16[8,512,128]{2,1,0:T(8,128)(2,1)} %add_convert_fusion), calls=%async_computation.1 | async-start | bytes 2097152 | tf_op jit(solution)/shard_map/all_to_all | solution.py:391
  77.0 14.6 %all-to-all-done.1.pieces = bf16[8,512,128]{2,1,0:T(8,128)(2,1)S(1)} async-done(((bf16[8,512,128]{2,1,0:T(8,128)(2,1)}), bf16[8,512,128]{2,1,0:T(8,128)(2,1)S(1)}, u32[]{:S(2)}, u32[]{:S(2)}) %all-to-all-start.1) | async-done | bytes 1048608 | tf_op jit(solution)/shard_map/all_to_all | solution.py:391
  91.7 1.0 pack.1
  92.7 8.1 %all-to-all-start.2 = ((bf16[32,16,128]{2,1,0:T(8,128)(2,1)}), bf16[32,16,128]{2,1,0:T(8,128)(2,1)S(1)}, u32[]{:S(2)}, u32[]{:S(2)}) async-start(bf16[32,16,128]{2,1,0:T(8,128)(2,1)} %pack.1), calls=%async_computation.2 | async-start | bytes 262144 | tf_op jit(solution)/shard_map/all_to_all | solution.py:391
  101.1 11.1 %all-to-all-done.2 = bf16[32,16,128]{2,1,0:T(8,128)(2,1)S(1)} async-done(((bf16[32,16,128]{2,1,0:T(8,128)(2,1)}), bf16[32,16,128]{2,1,0:T(8,128)(2,1)S(1)}, u32[]{:S(2)}, u32[]{:S(2)}) %all-to-all-start.2) | async-done | bytes 131104 | tf_op jit(solution)/shard_map/all_to_all | solution.py:391
  114.3 14.5 %all_to_all.30.line = bf16[32,16,128]{2,1,0:T(8,128)(2,1)S(1)} all-to-all(bf16[32,16,128]{2,1,0:T(8,128)(2,1)S(1)} %bitcast.53), channel_id=1, replica_groups={{0,128,256,384,16,144,272,400,32,160,288,416,48,176,304,432,64,192,320,..., dimensions={0} | all-to-all | bytes 262144 | tf_op jit(solution)/shard_map/all_to_all | solution.py:391
  129.2 16.6 %all_to_all.31.mine = bf16[8,512,128]{2,1,0:T(8,128)(2,1)S(1)} all-to-all(bf16[8,512,128]{2,1,0:T(8,128)(2,1)S(1)} %unpack.1), channel_id=1, replica_groups={{0,2,4,6,8,10,12,14},{1,3,5,7,9,11,13,15},{16,18,20,22,24,26,28,30},{17..., dimensions={0} | all-to-all | bytes 2097152 | tf_op jit(solution)/shard_map/all_to_all | solution.py:391
  145.8 6.0 %collective-permute-start.1 = (bf16[8,512,128]{2,1,0:T(8,128)(2,1)S(1)}, bf16[8,512,128]{2,1,0:T(8,128)(2,1)S(1)}, u32[]{:S(2)}, u32[]{:S(2)}) collective-permute-start(bf16[8,512,128]{2,1,0:T(8,128)(2,1)S(1)} %all_to_all.31.mine), channel_id=1, source_target_pairs={{0,1},{1,0},{2,3},{3,2},{4,5},{5,4},{6,7},{7,6},{8,9},{9,8},{10,11... | collective-permute-start | bytes 3145736 | tf_op jit(solution)/shard_map/ppermute | solution.py:473
  151.9 2.2 %collective-permute-done.1.other = bf16[8,512,128]{2,1,0:T(8,128)(2,1)S(1)} collective-permute-done((bf16[8,512,128]{2,1,0:T(8,128)(2,1)S(1)}, bf16[8,512,128]{2,1,0:T(8,128)(2,1)S(1)}, u32[]{:S(2)}, u32[]{:S(2)}) %collective-permute-start.1) | collective-permute-done | bytes 1048608 | tf_op jit(solution)/shard_map/ppermute | solution.py:473
  154.1 2.8 %copy-done.1 = f32[2,6144,128]{2,1,0:T(8,128)S(1)} copy-done((f32[2,6144,128]{2,1,0:T(8,128)S(1)}, f32[2,6144,128]{2,1,0:T(8,128)}, u32[]{:S(2)}) %copy-start.1) | copy-done | bytes 6291480
  156.9 4.7 %back.1 = bf16[4,2,16,2048]{3,2,1,0:T(8,128)(2,1)} custom-call(bf16[8,512,128]{2,1,0:T(8,128)(2,1)S(1)} %all_to_all.31.mine, bf16[8,512,128]{2,1,0:T(8,128)(2,1)S(1)} %collective-permute-done.1.other, f32[2,6144,128]{2,1,0:T(8,128)S(1)} %copy-done.1, f32[64,128]{1,0:T(8,128)S(1)} %copy-done.3, f32[64,128]{1,0:T(8,128)S(1)} %copy-done.4, ...), custom_call_target="tpu_custom_call" | custom-call | tf_op jit(solution)/shard_map/back/pallas_call | solution.py:344
  161.7 3.5 %all-to-all-start.5 = ((bf16[4,2,16,2048]{3,2,1,0:T(8,128)(2,1)}), bf16[4,2,16,2048]{3,2,1,0:T(8,128)(2,1)S(1)}, u32[]{:S(2)}, u32[]{:S(2)}) async-start(bf16[4,2,16,2048]{3,2,1,0:T(8,128)(2,1)} %back.1), calls=%async_computation.5 | async-start | bytes 1048576 | tf_op jit(solution)/shard_map/all_to_all | solution.py:391
  165.8 13.5 %all-to-all-done.5 = bf16[4,2,16,2048]{3,2,1,0:T(8,128)(2,1)S(1)} async-done(((bf16[4,2,16,2048]{3,2,1,0:T(8,128)(2,1)}), bf16[4,2,16,2048]{3,2,1,0:T(8,128)(2,1)S(1)}, u32[]{:S(2)}, u32[]{:S(2)}) %all-to-all-start.5) | async-done | bytes 524320 | tf_op jit(solution)/shard_map/all_to_all | solution.py:391
  179.4 1.1 copy.48
  (72 shorter events, 6.4 us)
Async XLA Ops:
  4.9 11.5 %copy-start.12 = (f32[1,8192]{1,0:T(1,128)S(1)}, f32[1,8192]{1,0:T(1,128)}, u32[]{:S(2)}) copy-start(f32[1,8192]{1,0:T(1,128)} %param.23) | copy-start | bytes 98308
  4.9 14.4 %copy-start.10 = (bf16[256,256]{1,0:T(8,128)(2,1)S(1)}, bf16[256,256]{1,0:T(8,128)(2,1)}, u32[]{:S(2)}) copy-start(bf16[256,256]{1,0:T(8,128)(2,1)} %constant.101.clone) | copy-start | bytes 393220
  4.9 14.4 %copy-start.11 = (bf16[256,256]{1,0:T(8,128)(2,1)S(1)}, bf16[256,256]{1,0:T(8,128)(2,1)}, u32[]{:S(2)}) copy-start(bf16[256,256]{1,0:T(8,128)(2,1)} %constant.102.clone) | copy-start | bytes 393220
  4.9 36.4 %copy-start.3 = (f32[64,128]{1,0:T(8,128)S(1)}, f32[64,128]{1,0:T(8,128)}, u32[]{:S(2)}) copy-start(f32[64,128]{1,0:T(8,128)} %constant.105.clone.twist_real) | copy-start | bytes 98308
  4.9 36.4 %copy-start.4 = (f32[64,128]{1,0:T(8,128)S(1)}, f32[64,128]{1,0:T(8,128)}, u32[]{:S(2)}) copy-start(f32[64,128]{1,0:T(8,128)} %constant.106.clone.twist_imag) | copy-start | bytes 98308
  4.9 36.4 %copy-start.6 = (bf16[128,128]{1,0:T(8,128)(2,1)S(1)}, bf16[128,128]{1,0:T(8,128)(2,1)}, u32[]{:S(2)}) copy-start(bf16[128,128]{1,0:T(8,128)(2,1)} %constant.107.clone.first) | copy-start | bytes 98308
  4.9 36.4 %all-to-all-start = ((bf16[4,6,16,2048]{3,2,1,0:T(8,128)(2,1)}), bf16[4,6,16,2048]{3,2,1,0:T(8,128)(2,1)S(1)}, u32[]{:S(2)}, u32[]{:S(2)}) async-start(bf16[4,6,16,2048]{3,2,1,0:T(8,128)(2,1)} %pad_maximum_fusion), calls=%async_computation | async-start | bytes 3145728 | tf_op jit(solution)/shard_map/all_to_all | solution.py:391
  48.9 2.7 %copy-start = (f32[2,6144,128]{2,1,0:T(8,128)}, f32[2,6144,128]{2,1,0:T(8,128)S(1)}, u32[]{:S(2)}) copy-start(f32[2,6144,128]{2,1,0:T(8,128)S(1)} %get-tuple-element.7.phases) | copy-start | bytes 18874372
  51.6 7.1 %collective-permute-start = (bf16[8,512,128]{2,1,0:T(8,128)(2,1)S(1)}, bf16[8,512,128]{2,1,0:T(8,128)(2,1)S(1)}, u32[]{:S(2)}, u32[]{:S(2)}) collective-permute-start(bf16[8,512,128]{2,1,0:T(8,128)(2,1)S(1)} %get-tuple-element.6), channel_id=1, source_target_pairs={{0,1},{1,0},{2,3},{3,2},{4,5},{5,4},{6,7},{7,6},{8,9},{9,8},{10,11... | collective-permute-start | bytes 3145736 | tf_op jit(solution)/shard_map/ppermute | solution.py:426
  59.9 16.9 %copy-start.16 = (s32[1,1,512]{2,1,0:T(1,128)S(1)}, s32[1,1,512]{2,1,0:T(1,128)}, u32[]{:S(2)}) copy-start(s32[1,1,512]{2,1,0:T(1,128)} %param.29) | copy-start | bytes 6148
  59.9 16.9 %copy-start.17 = (f32[1,8]{1,0:T(1,128)S(1)}, f32[1,8]{1,0:T(1,128)}, u32[]{:S(2)}) copy-start(f32[1,8]{1,0:T(1,128)} %param.26) | copy-start | bytes 100
  59.9 17.0 %copy-start.14 = (s32[1,1,512]{2,1,0:T(1,128)S(1)}, s32[1,1,512]{2,1,0:T(1,128)}, u32[]{:S(2)}) copy-start(s32[1,1,512]{2,1,0:T(1,128)} %param.28) | copy-start | bytes 6148
  59.9 17.0 %copy-start.15 = (s32[1,1,512]{2,1,0:T(1,128)S(1)}, s32[1,1,512]{2,1,0:T(1,128)}, u32[]{:S(2)}) copy-start(s32[1,1,512]{2,1,0:T(1,128)} %param.27) | copy-start | bytes 6148
  59.9 31.8 %copy-start.2 = (bf16[512,512]{1,0:T(8,128)(2,1)S(1)}, bf16[512,512]{1,0:T(8,128)(2,1)}, u32[]{:S(2)}) copy-start(bf16[512,512]{1,0:T(8,128)(2,1)} %constant.108.clone.table) | copy-start | bytes 1572868
  59.9 31.7 %all-to-all-start.1 = ((bf16[8,512,128]{2,1,0:T(8,128)(2,1)}), bf16[8,512,128]{2,1,0:T(8,128)(2,1)S(1)}, u32[]{:S(2)}, u32[]{:S(2)}) async-start(bf16[8,512,128]{2,1,0:T(8,128)(2,1)} %add_convert_fusion), calls=%async_computation.1 | async-start | bytes 2097152 | tf_op jit(solution)/shard_map/all_to_all | solution.py:391
  76.7 24.1 %copy-start.18 = (f32[7]{0:T(128)S(1)}, f32[7]{0:T(128)}, u32[]{:S(2)}) copy-start(f32[7]{0:T(128)} %param.25) | copy-start | bytes 88
  76.7 24.4 %copy-start.13 = (f32[1,1,2,512]{3,2,1,0:T(2,128)S(1)}, f32[1,1,2,512]{3,2,1,0:T(2,128)}, u32[]{:S(2)}) copy-start(f32[1,1,2,512]{3,2,1,0:T(2,128)} %param.30) | copy-start | bytes 12292
  92.7 19.5 %all-to-all-start.2 = ((bf16[32,16,128]{2,1,0:T(8,128)(2,1)}), bf16[32,16,128]{2,1,0:T(8,128)(2,1)S(1)}, u32[]{:S(2)}, u32[]{:S(2)}) async-start(bf16[32,16,128]{2,1,0:T(8,128)(2,1)} %pack.1), calls=%async_computation.2 | async-start | bytes 262144 | tf_op jit(solution)/shard_map/all_to_all | solution.py:391
  128.8 23.1 %copy-start.8 = (bf16[256,256]{1,0:T(8,128)(2,1)S(1)}, bf16[256,256]{1,0:T(8,128)(2,1)}, u32[]{:S(2)}) copy-start(bf16[256,256]{1,0:T(8,128)(2,1)} %constant.103.clone) | copy-start | bytes 393220
  128.8 23.1 %copy-start.9 = (bf16[256,256]{1,0:T(8,128)(2,1)S(1)}, bf16[256,256]{1,0:T(8,128)(2,1)}, u32[]{:S(2)}) copy-start(bf16[256,256]{1,0:T(8,128)(2,1)} %constant.104.clone) | copy-start | bytes 393220
  129.2 24.9 %copy-start.5 = (bf16[128,128]{1,0:T(8,128)(2,1)S(1)}, bf16[128,128]{1,0:T(8,128)(2,1)}, u32[]{:S(2)}) copy-start(bf16[128,128]{1,0:T(8,128)(2,1)} %constant.109.clone.first) | copy-start | bytes 98308
  145.8 8.3 %collective-permute-start.1 = (bf16[8,512,128]{2,1,0:T(8,128)(2,1)S(1)}, bf16[8,512,128]{2,1,0:T(8,128)(2,1)S(1)}, u32[]{:S(2)}, u32[]{:S(2)}) collective-permute-start(bf16[8,512,128]{2,1,0:T(8,128)(2,1)S(1)} %all_to_all.31.mine), channel_id=1, source_target_pairs={{0,1},{1,0},{2,3},{3,2},{4,5},{5,4},{6,7},{7,6},{8,9},{9,8},{10,11... | collective-permute-start | bytes 3145736 | tf_op jit(solution)/shard_map/ppermute | solution.py:473
  154.1 2.8 %copy-start.1 = (f32[2,6144,128]{2,1,0:T(8,128)S(1)}, f32[2,6144,128]{2,1,0:T(8,128)}, u32[]{:S(2)}) copy-start(f32[2,6144,128]{2,1,0:T(8,128)} %copy-done) | copy-start | bytes 18874372
  161.7 17.6 %all-to-all-start.5 = ((bf16[4,2,16,2048]{3,2,1,0:T(8,128)(2,1)}), bf16[4,2,16,2048]{3,2,1,0:T(8,128)(2,1)S(1)}, u32[]{:S(2)}, u32[]{:S(2)}) async-start(bf16[4,2,16,2048]{3,2,1,0:T(8,128)(2,1)} %back.1), calls=%async_computation.5 | async-start | bytes 1048576 | tf_op jit(solution)/shard_map/all_to_all | solution.py:391
  (1 other events, 1.0 us)

commit v2 on v1

--- a/solution.py
+++ b/solution.py
@@ -30,7 +30,7 @@
 LINE_GROUPS = GLOBAL_INDEX.transpose(2, 3, 4, 1, 0).reshape(-1, Y * LAYERS).tolist()
 CORE_SWAP = [(i, i ^ 1) for i in range(SUBGRIDS)]
 
-VMEM_LIMIT = 32 * 1024 * 1024
+VMEM_LIMIT = 24 * 1024 * 1024
 
 COL_PITCH = 24
 LINE_PITCH = 72
@@ -44,8 +44,8 @@
     return [float(value) for value in np.polynomial.chebyshev.cheb2poly(series.coef)]
 
 
-COSINE_SERIES = even_series(np.cos, 8)
-SINE_SERIES = even_series(lambda x: np.sinc(x / math.pi), 8)
+COSINE_SERIES = even_series(np.cos, 6)
+SINE_SERIES = even_series(lambda x: np.sinc(x / math.pi), 6)
 
 
 def phase_parts(angle):
@@ -108,9 +108,32 @@
     return (staged(window * jnp.cos(angles)), staged(-window * jnp.sin(angles)))
 
 
+def gather_kernel(strip, screen, out_ref, sems):
+    copies = []
+    for cq in range(LAYERS):
+        rows = pl.ds(cq * COLS, COLS)
+        pairs = [(strip.at[part, rows, :], part) for part in range(2)]
+        pairs += [
+            (screen.at[rows, pl.ds(nq * QUARTER, QUARTER)], 2 + nq) for nq in range(LAYERS)
+        ]
+        for source, place in pairs:
+            copies.append(
+                pltpu.make_async_copy(source, out_ref.at[cq, place], sems.at[len(copies)])
+            )
+    for copy in copies:
+        copy.start()
+    for copy in copies:
+        copy.wait()
+
+
+def phase_copy(source, target, sems, layer):
+    rows = pl.ds(layer * PHASE_ROWS, PHASE_ROWS)
+    return pltpu.make_async_copy(source.at[:, rows, :], target.at[:, rows, :], sems.at[layer])
+
+
 def forward_kernel(
     pieces, twist_real, twist_imag, first, second, factor_real, factor_imag,
-    mine_ref, other_ref, phases, strip, half,
+    mine_ref, other_ref, phases_out, phases, strip, half, sems,
 ):
     table = first[...]
 
@@ -137,6 +160,7 @@
             return carry
 
         lax.fori_loop(0, BLOCKS, phase_block, 0, unroll=4)
+        phase_copy(phases, phases_out, sems, layer).start()
 
         def first_block(pair, carry, layer=layer):
             c = pair * 2
@@ -187,6 +211,8 @@
         return carry
 
     lax.fori_loop(0, SUB_ROWS // 2, second_block, 0, unroll=8)
+    for layer in range(LAYERS):
+        phase_copy(phases, phases_out, sems, layer).wait()
 
 
 def pack_kernel(pieces, table, out_ref, total):
@@ -226,9 +252,11 @@
 
 
 def backward_kernel(
-    mine, other, phases, twist_real, twist_imag, first, second, factor_real, factor_imag,
-    out_ref, half, total,
+    mine, other, phases_in, twist_real, twist_imag, first, second, factor_real, factor_imag,
+    out_ref, phases, half, total, sems,
 ):
+    for layer in range(LAYERS):
+        phase_copy(phases_in, phases, sems, layer).start()
     weights = second[...]
 
     def second_block(pair, carry):
@@ -258,6 +286,8 @@
 
     lax.fori_loop(0, SUB_ROWS // 2, second_block, 0, unroll=8)
 
+    for layer in range(LAYERS):
+        phase_copy(phases_in, phases, sems, layer).wait()
     table = first[...]
 
     def first_block(pair, carry):
@@ -306,15 +336,14 @@
     lax.fori_loop(0, BLOCKS, leave_block, 0, unroll=2)
 
 
-def on_core(kernel, name, out_shape, scratch, inputs):
-    is_list = isinstance(out_shape, (list, tuple))
-    one = pl.BlockSpec(memory_space=pltpu.VMEM)
+def on_core(kernel, name, out_shape, scratch, inputs, far_in=(), far_out=()):
+    near, far = pl.BlockSpec(memory_space=pltpu.VMEM), pl.BlockSpec(memory_space=pltpu.HBM)
     return pl.pallas_call(
         kernel,
         name=name,
         out_shape=out_shape,
-        in_specs=[one] * inputs,
-        out_specs=[one] * len(out_shape) if is_list else one,
+        in_specs=[far if i in far_in else near for i in range(inputs)],
+        out_specs=[far if i in far_out else near for i in range(len(out_shape))],
         scratch_shapes=list(scratch),
         compiler_params=pltpu.CompilerParams(vmem_limit_bytes=VMEM_LIMIT),
     )
@@ -324,18 +353,34 @@
     return jax.ShapeDtypeStruct(shape, kind)
 
 
+def far(values):
+    return pltpu.with_memory_space_constraint(values, pltpu.HBM)
+
+
+def gather(strip, screen):
+    blocks = shaped((LAYERS, 2 + LAYERS, COLS, QUARTER), jnp.bfloat16)
+    sems = pltpu.SemaphoreType.DMA((LAYERS * (2 + LAYERS),))
+    return on_core(gather_kernel, "gather", [blocks], (sems,), 2, (0, 1), (0,))(
+        far(strip), far(screen)
+    )[0]
+
+
 def forward(pieces, factor_real, factor_imag, second):
     blocks = shaped((ZX, SUB_ROWS * Y, LANES), jnp.bfloat16)
+    phases = (2, LAYERS * PHASE_ROWS, LANES)
     twist_real, twist_imag = twiddle()
     return on_core(
         forward_kernel,
         "ahead",
-        [blocks, blocks, shaped((2, LAYERS * PHASE_ROWS, LANES), jnp.float32)],
+        [blocks, blocks, pltpu.HBM(phases, jnp.float32)],
         (
+            pltpu.VMEM(phases, jnp.float32),
             pltpu.VMEM((2, PHASE_ROWS, LANES), jnp.float32),
             pltpu.VMEM((2, SUB_ROWS * LINE_PITCH, LANES), jnp.float32),
+            pltpu.SemaphoreType.DMA((LAYERS,)),
         ),
         7,
+        far_out=(2,),
     )(pieces, twist_real, twist_imag, first_tables()[0], second, factor_real, factor_imag)
 
 
@@ -344,16 +389,19 @@
     return on_core(
         backward_kernel,
         "back",
-        shaped((LAYERS, 2, COLS, QUARTER), jnp.bfloat16),
+        [shaped((LAYERS, 2, COLS, QUARTER), jnp.bfloat16)],
         (
+            pltpu.VMEM((2, LAYERS * PHASE_ROWS, LANES), jnp.float32),
             pltpu.VMEM((2, STRIP_COLS * LINE_PITCH, LANES), jnp.float32),
             pltpu.VMEM((2, PHASE_ROWS, LANES), jnp.float32),
+            pltpu.SemaphoreType.DMA((LAYERS,)),
         ),
         9,
+        far_in=(2,),
     )(
-        mine, other, phases, twist_real, twist_imag, first_tables()[1], second,
+        mine, other, far(phases), twist_real, twist_imag, first_tables()[1], second,
         factor_real, factor_imag,
-    )
+    )[0]
 
 
 def spread(cell_index, length, kernel_taps):
@@ -407,14 +455,7 @@
 ):
     swapped = lax.axis_index("facet") % CORE == 1
 
-    joined = jnp.concatenate(
-        [
-            model_strip[0].reshape(2, LAYERS, COLS, QUARTER).transpose(1, 0, 2, 3),
-            screen_angle[0, 0].reshape(LAYERS, COLS, LAYERS, QUARTER).transpose(0, 2, 1, 3),
-        ],
-        axis=1,
-    )
-    pieces = exchange(joined, "layer")
+    pieces = exchange(gather(model_strip[0], screen_angle[0, 0]), "layer")
 
     factor_real, factor_imag = facet_factor(facet_window[0], facet_shift[0], swapped)
     plain = second_tables(STAGE_ORDER)
@@ -431,10 +472,10 @@
     packed = on_core(
         pack_kernel,
         "pack",
-        shaped((Y * LAYERS, *piece), jnp.bfloat16),
+        [shaped((Y * LAYERS, *piece), jnp.bfloat16)],
         (pltpu.VMEM((SUB_ROWS * Y, LANES), jnp.float32),),
         2,
-    )(plane_terms, table)
+    )(plane_terms, table)[0]
     line_sum = jnp.sum(
         exchange(packed, ("layer", "facet"), LINE_GROUPS)
         .reshape(Y, LAYERS, *piece)
@@ -465,10 +506,10 @@
     copies = on_core(
         unpack_kernel,
         "unpack",
-        shaped((ZX, SUB_ROWS * Y, LANES), jnp.bfloat16),
+        [shaped((ZX, SUB_ROWS * Y, LANES), jnp.bfloat16)],
         (pltpu.VMEM((SUB_ROWS * Y, LANES), jnp.float32),),
         2,
-    )(line, table)
+    )(line, table)[0]
     mine_grids = exchange(copies, "facet", PLANE_GROUPS)
     other_grids = lax.ppermute(mine_grids, "facet", CORE_SWAP)
     leaving = backward(mine_grids, other_grids, phases, factor_real, factor_imag, second_back)

time: 182 us -> 221 us (1.21)
  Pallas kernels: 13.7 us -> 63.1 us
  local copies, waits for them, and re-layouts: 11.5 us -> 3.13 us
    pallas_call x4 -> x5, Pallas kernels: 13.7 us -> 63.1 us  [the longest x1 49 us: gather(): on_core(gather_kernel, 'gather', [blocks], (sems,), 2, (0, 1), (0,))]
    unnamed x39 -> x33, local copies, waits for them, and re-layouts: 6.5 us -> 0.61 us
    another operation x3 -> x0, local copies, waits for them, and re-layouts: 2.46 us -> none  [the longest x2 2.43 us: local(): screen_angle[0, 0].reshape(LAYERS, COLS, LAYERS, QUARTER)]
where the time goes in v2:
time: 221 us; the launch traced here: 220 us
  waiting for transfers between devices  65.7 us (30%)
  Pallas kernels  63.1 us (29%)
  starting transfers between devices  50.2 us (23%)
  blocking collectives  31.2 us (14%)
  other arithmetic  4.42 us (2%)
  local copies, waits for them, and re-layouts  3.13 us (1%)
    all_to_all x4, waiting for transfers between devices, exchange(): lax.all_to_all(blocks, axes, split_axis=0, concat_axis=0, tiled=True, axi...  61.2 us
    pallas_call x1, Pallas kernels, gather(): on_core(gather_kernel, 'gather', [blocks], (sems,), 2, (0, 1), (0,))  49 us
    all_to_all x4, starting transfers between devices, exchange(): lax.all_to_all(blocks, axes, split_axis=0, concat_axis=0, tiled=True, axi...  39.4 us
    all_to_all x2, blocking collectives, exchange(): lax.all_to_all(blocks, axes, split_axis=0, concat_axis=0, tiled=True, axi...  31.2 us
    pallas_call x1, Pallas kernels, forward(): on_core(forward_kernel, 'ahead', [blocks, blocks, pltpu.HBM(phases, jnp.f...  7.06 us
    ppermute x1, starting transfers between devices, local(): other_grids = lax.ppermute(mine_grids, 'facet', CORE_SWAP)  6.05 us
    pallas_call x1, Pallas kernels, backward(): on_core(backward_kernel, 'back', [shaped((LAYERS, 2, COLS, QUARTER), jnp....  5.63 us
    ppermute x1, starting transfers between devices, local(): arrived = lax.ppermute(other, 'facet', CORE_SWAP)  4.8 us
  transfers between devices with their start and end apart: 6, of which 6 were waited for; matrix products, arithmetic and copies ran while one was open for 2% of the time, Pallas kernels for 0%

profile of v2, /device:TPU:1, one launch (start us, length us, event | category | flops | bytes accessed | tf_op | source)
XLA Modules:
  0.0 220.3 jit_solution(1803387078160015461)
XLA Ops:
  0.6 49.0 %gather.1 = bf16[4,6,16,2048]{3,2,1,0:T(8,128)(2,1)} custom-call(bf16[2,64,2048]{2,1,0:T(8,128)(2,1)} %bitcast.45, bf16[64,8192]{1,0:T(8,128)(2,1)} %bitcast.39), custom_call_target="tpu_custom_call" | custom-call | tf_op jit(solution)/shard_map/gather/pallas_call | solution.py:363
  49.7 11.0 %all-to-all-start = ((bf16[4,6,16,2048]{3,2,1,0:T(8,128)(2,1)}), bf16[4,6,16,2048]{3,2,1,0:T(8,128)(2,1)S(1)}, u32[]{:S(2)}, u32[]{:S(2)}) async-start(bf16[4,6,16,2048]{3,2,1,0:T(8,128)(2,1)} %gather.1), calls=%async_computation | async-start | bytes 3145728 | tf_op jit(solution)/shard_map/all_to_all | solution.py:439
  60.7 0.5 broadcast.165
  61.2 0.7 reduce.3
  62.7 1.1 multiply_bitcast_fusion
  64.1 22.0 %all-to-all-done.pieces = bf16[4,6,16,2048]{3,2,1,0:T(8,128)(2,1)S(1)} async-done(((bf16[4,6,16,2048]{3,2,1,0:T(8,128)(2,1)}), bf16[4,6,16,2048]{3,2,1,0:T(8,128)(2,1)S(1)}, u32[]{:S(2)}, u32[]{:S(2)}) %all-to-all-start) | async-done | bytes 1572896 | tf_op jit(solution)/shard_map/all_to_all | solution.py:439
  86.1 7.1 %ahead.1 = (bf16[8,512,128]{2,1,0:T(8,128)(2,1)S(1)}, bf16[8,512,128]{2,1,0:T(8,128)(2,1)S(1)}, f32[2,6144,128]{2,1,0:T(8,128)}) custom-call(bf16[4,6,16,2048]{3,2,1,0:T(8,128)(2,1)S(1)} %all-to-all-done.pieces, f32[64,128]{1,0:T(8,128)S(1)} %copy-done.1, f32[64,128]{1,0:T(8,128)S(1)} %copy-done.2, bf16[128,128]{1,0:T(8,128)(2,1)S(1)} %copy-done.4, ...), custom_call_target="tpu_custom_call" | custom-call | tf_op jit(solution)/shard_map/ahead/pallas_call | solution.py:372
  93.1 4.8 %collective-permute-start = (bf16[8,512,128]{2,1,0:T(8,128)(2,1)S(1)}, bf16[8,512,128]{2,1,0:T(8,128)(2,1)S(1)}, u32[]{:S(2)}, u32[]{:S(2)}) collective-permute-start(bf16[8,512,128]{2,1,0:T(8,128)(2,1)S(1)} %get-tuple-element.6), channel_id=1, source_target_pairs={{0,1},{1,0},{2,3},{3,2},{4,5},{5,4},{6,7},{7,6},{8,9},{9,8},{10,11... | collective-permute-start | bytes 3145736 | tf_op jit(solution)/shard_map/ppermute | solution.py:467
  98.0 2.3 %collective-permute-done = bf16[8,512,128]{2,1,0:T(8,128)(2,1)S(1)} collective-permute-done((bf16[8,512,128]{2,1,0:T(8,128)(2,1)S(1)}, bf16[8,512,128]{2,1,0:T(8,128)(2,1)S(1)}, u32[]{:S(2)}, u32[]{:S(2)}) %collective-permute-start) | collective-permute-done | bytes 1048608 | tf_op jit(solution)/shard_map/ppermute | solution.py:467
  100.2 1.2 add_convert_fusion
  101.5 16.8 %all-to-all-start.1 = ((bf16[8,512,128]{2,1,0:T(8,128)(2,1)}), bf16[8,512,128]{2,1,0:T(8,128)(2,1)S(1)}, u32[]{:S(2)}, u32[]{:S(2)}) async-start(bf16[8,512,128]{2,1,0:T(8,128)(2,1)} %add_convert_fusion), calls=%async_computation.1 | async-start | bytes 2097152 | tf_op jit(solution)/shard_map/all_to_all | solution.py:439
  118.6 14.7 %all-to-all-done.1.pieces = bf16[8,512,128]{2,1,0:T(8,128)(2,1)S(1)} async-done(((bf16[8,512,128]{2,1,0:T(8,128)(2,1)}), bf16[8,512,128]{2,1,0:T(8,128)(2,1)S(1)}, u32[]{:S(2)}, u32[]{:S(2)}) %all-to-all-start.1) | async-done | bytes 1048608 | tf_op jit(solution)/shard_map/all_to_all | solution.py:439
  133.2 1.0 pack.1
  134.3 8.1 %all-to-all-start.2 = ((bf16[32,16,128]{2,1,0:T(8,128)(2,1)}), bf16[32,16,128]{2,1,0:T(8,128)(2,1)S(1)}, u32[]{:S(2)}, u32[]{:S(2)}) async-start(bf16[32,16,128]{2,1,0:T(8,128)(2,1)} %pack.1), calls=%async_computation.2 | async-start | bytes 262144 | tf_op jit(solution)/shard_map/all_to_all | solution.py:439
  142.7 11.1 %all-to-all-done.2 = bf16[32,16,128]{2,1,0:T(8,128)(2,1)S(1)} async-done(((bf16[32,16,128]{2,1,0:T(8,128)(2,1)}), bf16[32,16,128]{2,1,0:T(8,128)(2,1)S(1)}, u32[]{:S(2)}, u32[]{:S(2)}) %all-to-all-start.2) | async-done | bytes 131104 | tf_op jit(solution)/shard_map/all_to_all | solution.py:439
  155.9 14.6 %all_to_all.30.line = bf16[32,16,128]{2,1,0:T(8,128)(2,1)S(1)} all-to-all(bf16[32,16,128]{2,1,0:T(8,128)(2,1)S(1)} %bitcast.44), channel_id=1, replica_groups={{0,128,256,384,16,144,272,400,32,160,288,416,48,176,304,432,64,192,320,..., dimensions={0} | all-to-all | bytes 262144 | tf_op jit(solution)/shard_map/all_to_all | solution.py:439
  170.9 16.6 %all_to_all.31.mine = bf16[8,512,128]{2,1,0:T(8,128)(2,1)S(1)} all-to-all(bf16[8,512,128]{2,1,0:T(8,128)(2,1)S(1)} %unpack.1), channel_id=1, replica_groups={{0,2,4,6,8,10,12,14},{1,3,5,7,9,11,13,15},{16,18,20,22,24,26,28,30},{17..., dimensions={0} | all-to-all | bytes 2097152 | tf_op jit(solution)/shard_map/all_to_all | solution.py:439
  187.5 6.1 %collective-permute-start.1 = (bf16[8,512,128]{2,1,0:T(8,128)(2,1)S(1)}, bf16[8,512,128]{2,1,0:T(8,128)(2,1)S(1)}, u32[]{:S(2)}, u32[]{:S(2)}) collective-permute-start(bf16[8,512,128]{2,1,0:T(8,128)(2,1)S(1)} %all_to_all.31.mine), channel_id=1, source_target_pairs={{0,1},{1,0},{2,3},{3,2},{4,5},{5,4},{6,7},{7,6},{8,9},{9,8},{10,11... | collective-permute-start | bytes 3145736 | tf_op jit(solution)/shard_map/ppermute | solution.py:514
  193.6 2.2 %collective-permute-done.1.other = bf16[8,512,128]{2,1,0:T(8,128)(2,1)S(1)} collective-permute-done((bf16[8,512,128]{2,1,0:T(8,128)(2,1)S(1)}, bf16[8,512,128]{2,1,0:T(8,128)(2,1)S(1)}, u32[]{:S(2)}, u32[]{:S(2)}) %collective-permute-start.1) | collective-permute-done | bytes 1048608 | tf_op jit(solution)/shard_map/ppermute | solution.py:514
  195.8 5.6 %back.1 = bf16[4,2,16,2048]{3,2,1,0:T(8,128)(2,1)} custom-call(bf16[8,512,128]{2,1,0:T(8,128)(2,1)S(1)} %all_to_all.31.mine, bf16[8,512,128]{2,1,0:T(8,128)(2,1)S(1)} %collective-permute-done.1.other, f32[2,6144,128]{2,1,0:T(8,128)} %get-tuple-element.7.phases_in, f32[64,128]{1,0:T(8,128)S(1)} %copy-done.1, f32[64,128]{1,0:T(8,128)S(1)} %copy-done.2, ...), custom_call_target="tpu_custom_call" | custom-call | tf_op jit(solution)/shard_map/back/pallas_call | solution.py:389
  201.5 3.5 %all-to-all-start.5 = ((bf16[4,2,16,2048]{3,2,1,0:T(8,128)(2,1)}), bf16[4,2,16,2048]{3,2,1,0:T(8,128)(2,1)S(1)}, u32[]{:S(2)}, u32[]{:S(2)}) async-start(bf16[4,2,16,2048]{3,2,1,0:T(8,128)(2,1)} %back.1), calls=%async_computation.5 | async-start | bytes 1048576 | tf_op jit(solution)/shard_map/all_to_all | solution.py:439
  205.0 0.6 maximum_bitcast_fusion
  205.6 13.5 %all-to-all-done.5 = bf16[4,2,16,2048]{3,2,1,0:T(8,128)(2,1)S(1)} async-done(((bf16[4,2,16,2048]{3,2,1,0:T(8,128)(2,1)}), bf16[4,2,16,2048]{3,2,1,0:T(8,128)(2,1)S(1)}, u32[]{:S(2)}, u32[]{:S(2)}) %all-to-all-start.5) | async-done | bytes 524320 | tf_op jit(solution)/shard_map/all_to_all | solution.py:439
  219.2 1.1 copy.42
  (63 shorter events, 3.5 us)
Async XLA Ops:
  49.6 11.6 %copy-start.9 = (f32[1,8192]{1,0:T(1,128)S(1)}, f32[1,8192]{1,0:T(1,128)}, u32[]{:S(2)}) copy-start(f32[1,8192]{1,0:T(1,128)} %param.23) | copy-start | bytes 98308
  49.6 14.4 %copy-start.7 = (bf16[256,256]{1,0:T(8,128)(2,1)S(1)}, bf16[256,256]{1,0:T(8,128)(2,1)}, u32[]{:S(2)}) copy-start(bf16[256,256]{1,0:T(8,128)(2,1)} %constant.101.clone) | copy-start | bytes 393220
  49.6 14.4 %copy-start.8 = (bf16[256,256]{1,0:T(8,128)(2,1)S(1)}, bf16[256,256]{1,0:T(8,128)(2,1)}, u32[]{:S(2)}) copy-start(bf16[256,256]{1,0:T(8,128)(2,1)} %constant.102.clone) | copy-start | bytes 393220
  49.6 36.4 %copy-start.1 = (f32[64,128]{1,0:T(8,128)S(1)}, f32[64,128]{1,0:T(8,128)}, u32[]{:S(2)}) copy-start(f32[64,128]{1,0:T(8,128)} %constant.105.clone.twist_real) | copy-start | bytes 98308
  49.6 36.4 %copy-start.2 = (f32[64,128]{1,0:T(8,128)S(1)}, f32[64,128]{1,0:T(8,128)}, u32[]{:S(2)}) copy-start(f32[64,128]{1,0:T(8,128)} %constant.106.clone.twist_imag) | copy-start | bytes 98308
  49.7 36.4 %copy-start.4 = (bf16[128,128]{1,0:T(8,128)(2,1)S(1)}, bf16[128,128]{1,0:T(8,128)(2,1)}, u32[]{:S(2)}) copy-start(bf16[128,128]{1,0:T(8,128)(2,1)} %constant.107.clone.first) | copy-start | bytes 98308
  49.7 36.4 %all-to-all-start = ((bf16[4,6,16,2048]{3,2,1,0:T(8,128)(2,1)}), bf16[4,6,16,2048]{3,2,1,0:T(8,128)(2,1)S(1)}, u32[]{:S(2)}, u32[]{:S(2)}) async-start(bf16[4,6,16,2048]{3,2,1,0:T(8,128)(2,1)} %gather.1), calls=%async_computation | async-start | bytes 3145728 | tf_op jit(solution)/shard_map/all_to_all | solution.py:439
  93.1 7.1 %collective-permute-start = (bf16[8,512,128]{2,1,0:T(8,128)(2,1)S(1)}, bf16[8,512,128]{2,1,0:T(8,128)(2,1)S(1)}, u32[]{:S(2)}, u32[]{:S(2)}) collective-permute-start(bf16[8,512,128]{2,1,0:T(8,128)(2,1)S(1)} %get-tuple-element.6), channel_id=1, source_target_pairs={{0,1},{1,0},{2,3},{3,2},{4,5},{5,4},{6,7},{7,6},{8,9},{9,8},{10,11... | collective-permute-start | bytes 3145736 | tf_op jit(solution)/shard_map/ppermute | solution.py:467
  100.2 18.1 %copy-start.13 = (s32[1,1,512]{2,1,0:T(1,128)S(1)}, s32[1,1,512]{2,1,0:T(1,128)}, u32[]{:S(2)}) copy-start(s32[1,1,512]{2,1,0:T(1,128)} %param.29) | copy-start | bytes 6148
  100.2 18.1 %copy-start.14 = (f32[1,8]{1,0:T(1,128)S(1)}, f32[1,8]{1,0:T(1,128)}, u32[]{:S(2)}) copy-start(f32[1,8]{1,0:T(1,128)} %param.26) | copy-start | bytes 100
  100.2 18.2 %copy-start.11 = (s32[1,1,512]{2,1,0:T(1,128)S(1)}, s32[1,1,512]{2,1,0:T(1,128)}, u32[]{:S(2)}) copy-start(s32[1,1,512]{2,1,0:T(1,128)} %param.28) | copy-start | bytes 6148
  100.2 18.2 %copy-start.12 = (s32[1,1,512]{2,1,0:T(1,128)S(1)}, s32[1,1,512]{2,1,0:T(1,128)}, u32[]{:S(2)}) copy-start(s32[1,1,512]{2,1,0:T(1,128)} %param.27) | copy-start | bytes 6148
  100.2 33.0 %copy-start = (bf16[512,512]{1,0:T(8,128)(2,1)S(1)}, bf16[512,512]{1,0:T(8,128)(2,1)}, u32[]{:S(2)}) copy-start(bf16[512,512]{1,0:T(8,128)(2,1)} %constant.108.clone.table) | copy-start | bytes 1572868
  101.5 40.9 %copy-start.15 = (f32[7]{0:T(128)S(1)}, f32[7]{0:T(128)}, u32[]{:S(2)}) copy-start(f32[7]{0:T(128)} %param.25) | copy-start | bytes 88
  101.5 41.2 %copy-start.10 = (f32[1,1,2,512]{3,2,1,0:T(2,128)S(1)}, f32[1,1,2,512]{3,2,1,0:T(2,128)}, u32[]{:S(2)}) copy-start(f32[1,1,2,512]{3,2,1,0:T(2,128)} %param.30) | copy-start | bytes 12292
  101.5 31.7 %all-to-all-start.1 = ((bf16[8,512,128]{2,1,0:T(8,128)(2,1)}), bf16[8,512,128]{2,1,0:T(8,128)(2,1)S(1)}, u32[]{:S(2)}, u32[]{:S(2)}) async-start(bf16[8,512,128]{2,1,0:T(8,128)(2,1)} %add_convert_fusion), calls=%async_computation.1 | async-start | bytes 2097152 | tf_op jit(solution)/shard_map/all_to_all | solution.py:439
  134.3 19.5 %all-to-all-start.2 = ((bf16[32,16,128]{2,1,0:T(8,128)(2,1)}), bf16[32,16,128]{2,1,0:T(8,128)(2,1)S(1)}, u32[]{:S(2)}, u32[]{:S(2)}) async-start(bf16[32,16,128]{2,1,0:T(8,128)(2,1)} %pack.1), calls=%async_computation.2 | async-start | bytes 262144 | tf_op jit(solution)/shard_map/all_to_all | solution.py:439
  155.9 37.7 %copy-start.5 = (bf16[256,256]{1,0:T(8,128)(2,1)S(1)}, bf16[256,256]{1,0:T(8,128)(2,1)}, u32[]{:S(2)}) copy-start(bf16[256,256]{1,0:T(8,128)(2,1)} %constant.103.clone) | copy-start | bytes 393220
  155.9 37.7 %copy-start.6 = (bf16[256,256]{1,0:T(8,128)(2,1)S(1)}, bf16[256,256]{1,0:T(8,128)(2,1)}, u32[]{:S(2)}) copy-start(bf16[256,256]{1,0:T(8,128)(2,1)} %constant.104.clone) | copy-start | bytes 393220
  170.5 25.3 %copy-start.3 = (bf16[128,128]{1,0:T(8,128)(2,1)S(1)}, bf16[128,128]{1,0:T(8,128)(2,1)}, u32[]{:S(2)}) copy-start(bf16[128,128]{1,0:T(8,128)(2,1)} %constant.109.clone.first) | copy-start | bytes 98308
  187.5 8.3 %collective-permute-start.1 = (bf16[8,512,128]{2,1,0:T(8,128)(2,1)S(1)}, bf16[8,512,128]{2,1,0:T(8,128)(2,1)S(1)}, u32[]{:S(2)}, u32[]{:S(2)}) collective-permute-start(bf16[8,512,128]{2,1,0:T(8,128)(2,1)S(1)} %all_to_all.31.mine), channel_id=1, source_target_pairs={{0,1},{1,0},{2,3},{3,2},{4,5},{5,4},{6,7},{7,6},{8,9},{9,8},{10,11... | collective-permute-start | bytes 3145736 | tf_op jit(solution)/shard_map/ppermute | solution.py:514
  201.5 17.6 %all-to-all-start.5 = ((bf16[4,2,16,2048]{3,2,1,0:T(8,128)(2,1)}), bf16[4,2,16,2048]{3,2,1,0:T(8,128)(2,1)S(1)}, u32[]{:S(2)}, u32[]{:S(2)}) async-start(bf16[4,2,16,2048]{3,2,1,0:T(8,128)(2,1)} %back.1), calls=%async_computation.5 | async-start | bytes 1048576 | tf_op jit(solution)/shard_map/all_to_all | solution.py:439

commit v3 on v2

--- a/solution.py
+++ b/solution.py
@@ -108,22 +108,31 @@
     return (staged(window * jnp.cos(angles)), staged(-window * jnp.sin(angles)))
 
 
-def gather_kernel(strip, screen, out_ref, sems):
-    copies = []
+def gather_kernel(strip, screen, out_ref, blocks, in_sems, out_sems):
+    def arrivals(cq):
+        rows = pl.ds(cq * COLS, COLS)
+        pairs = [(strip.at[:, rows, :], blocks.at[cq, pl.ds(0, 2)])]
+        for nq in range(LAYERS):
+            pairs.append(
+                (screen.at[rows, pl.ds(nq * QUARTER, QUARTER)], blocks.at[cq, 2 + nq])
+            )
+        return [
+            pltpu.make_async_copy(source, target, in_sems.at[cq, i])
+            for i, (source, target) in enumerate(pairs)
+        ]
+
+    def departure(cq):
+        return pltpu.make_async_copy(blocks.at[cq], out_ref.at[cq], out_sems.at[cq])
+
     for cq in range(LAYERS):
-        rows = pl.ds(cq * COLS, COLS)
-        pairs = [(strip.at[part, rows, :], part) for part in range(2)]
-        pairs += [
-            (screen.at[rows, pl.ds(nq * QUARTER, QUARTER)], 2 + nq) for nq in range(LAYERS)
-        ]
-        for source, place in pairs:
-            copies.append(
-                pltpu.make_async_copy(source, out_ref.at[cq, place], sems.at[len(copies)])
-            )
-    for copy in copies:
-        copy.start()
-    for copy in copies:
-        copy.wait()
+        for copy in arrivals(cq):
+            copy.start()
+    for cq in range(LAYERS):
+        for copy in arrivals(cq):
+            copy.wait()
+        departure(cq).start()
+    for cq in range(LAYERS):
+        departure(cq).wait()
 
 
 def phase_copy(source, target, sems, layer):
@@ -358,11 +367,20 @@
 
 
 def gather(strip, screen):
-    blocks = shaped((LAYERS, 2 + LAYERS, COLS, QUARTER), jnp.bfloat16)
-    sems = pltpu.SemaphoreType.DMA((LAYERS * (2 + LAYERS),))
-    return on_core(gather_kernel, "gather", [blocks], (sems,), 2, (0, 1), (0,))(
-        far(strip), far(screen)
-    )[0]
+    blocks = (LAYERS, 2 + LAYERS, COLS, QUARTER)
+    return on_core(
+        gather_kernel,
+        "gather",
+        [pltpu.HBM(blocks, jnp.bfloat16)],
+        (
+            pltpu.VMEM(blocks, jnp.bfloat16),
+            pltpu.SemaphoreType.DMA((LAYERS, 1 + LAYERS)),
+            pltpu.SemaphoreType.DMA((LAYERS,)),
+        ),
+        2,
+        (0, 1),
+        (0,),
+    )(far(strip), far(screen))[0]
 
 
 def forward(pieces, factor_real, factor_imag, second):
@@ -412,18 +430,20 @@
     return jnp.sum(matches * kernel_taps, axis=2)
 
 
-def degrid(subgrid, row_cells, column_cells, plane, observed_vis, angle_table, kernel_taps):
+def prepare(row_cells, column_cells, plane, angle_table, kernel_taps):
     row_weights = spread(row_cells, SUB_ROWS, kernel_taps)
     column_weights = spread(column_cells, STRIP_COLS, kernel_taps)
+    plane_pick = (plane[:, None] == jnp.arange(PLANES, dtype=jnp.int32)[None, :]).astype(
+        jnp.float32
+    )
+    phase_angle = jnp.sum(plane_pick * angle_table[None, :], axis=1)
+    return (row_weights, column_weights, jnp.cos(phase_angle), jnp.sin(phase_angle))
+
+
+def degrid(subgrid, observed_vis, row_weights, column_weights, cosine, sine_part):
     kernel_rows = jnp.dot(row_weights, subgrid, precision=lax.Precision.HIGHEST)
     model_real = jnp.sum(kernel_rows[:, :STRIP_COLS] * column_weights, axis=1)
     model_imag = jnp.sum(kernel_rows[:, STRIP_COLS:] * column_weights, axis=1)
-    plane_pick = (plane[:, None] == jnp.arange(PLANES, dtype=jnp.int32)[None, :]).astype(
-        jnp.float32
-    )
-    phase_angle = jnp.sum(plane_pick * angle_table[None, :], axis=1)
-    cosine = jnp.cos(phase_angle)
-    sine_part = jnp.sin(phase_angle)
     residual_real = observed_vis[0] - (model_real * cosine - model_imag * sine_part)
     residual_imag = observed_vis[1] - (model_real * sine_part + model_imag * cosine)
     weighted_real = residual_real * cosine + residual_imag * sine_part
@@ -462,6 +482,13 @@
     crossed = second_tables(np.roll(STAGE_ORDER, SUBGRIDS // CORE))
     second_ahead = jnp.where(swapped, crossed[0], plain[0])
     second_back = jnp.where(swapped, crossed[1], plain[1])
+    prepared = prepare(u_cell[0, 0], v_cell[0, 0], w_plane[0, 0], plane_angle[0], kernel_taps)
+    observed_vis = (observed[0, 0, 0], observed[0, 0, 1])
+    (
+        pieces, factor_real, factor_imag, second_ahead, second_back, prepared, observed_vis
+    ) = lax.optimization_barrier(
+        (pieces, factor_real, factor_imag, second_ahead, second_back, prepared, observed_vis)
+    )
     mine, other, phases = forward(pieces, factor_real, factor_imag, second_ahead)
 
     arrived = lax.ppermute(other, "facet", CORE_SWAP)
@@ -488,13 +515,11 @@
         .reshape(SUB_ROWS, 2 * STRIP_COLS)
     )
 
-    residual, adjoint = degrid(
-        subgrid, u_cell[0, 0], v_cell[0, 0], w_plane[0, 0], observed[0, 0], plane_angle[0], kernel_taps
-    )
+    residual, adjoint = degrid(subgrid, observed_vis, *prepared)
+    residual, adjoint = lax.optimization_barrier((residual, adjoint.astype(jnp.bfloat16)))
 
     sent = (
-        adjoint.astype(jnp.bfloat16)
-        .reshape(4, SUB_ROWS // 4, 2, LAYERS, COLS)
+        adjoint.reshape(4, SUB_ROWS // 4, 2, LAYERS, COLS)
         .transpose(3, 1, 0, 2, 4)
         .reshape(1, LAYERS, *piece)
     )

time: 221 us -> 171 us (0.77)
  blocking collectives: 31.2 us -> 97.2 us
  Pallas kernels: 63.1 us -> 15.1 us
  waiting for transfers between devices: 65.7 us -> 25.9 us
  starting transfers between devices: 50.2 us -> 23.1 us
    all_to_all x2 -> x5, blocking collectives: 31.2 us -> 97.2 us  [exchange(): lax.all_to_all(blocks, axes, split_axis=0, concat_axis=0, tiled=True, axi...]
    pallas_call x1, Pallas kernels: 49 us -> 2.4 us  [gather(): on_core(gather_kernel, 'gather', [pltpu.HBM(blocks, jnp.bfloat16)], (pltp...]
    all_to_all x4 -> x1, waiting for transfers between devices: 61.2 us -> 21.3 us  [exchange(): lax.all_to_all(blocks, axes, split_axis=0, concat_axis=0, tiled=True, axi...]
    all_to_all x4 -> x1, starting transfers between devices: 39.4 us -> 11 us  [exchange(): lax.all_to_all(blocks, axes, split_axis=0, concat_axis=0, tiled=True, axi...]
  transfers between devices with their start and end apart: 6 -> 3, of which waited for: 6 -> 3; matrix products, arithmetic and copies ran while one was open for 2% -> 2% of each run, Pallas kernels for 0% -> 0%
where the time goes in v3:
time: 171 us; the launch traced here: 170 us
  blocking collectives  97.2 us (57%)
  waiting for transfers between devices  25.9 us (15%)
  starting transfers between devices  23.1 us (14%)
  Pallas kernels  15.1 us (9%)
  other arithmetic  3.44 us (2%)
  local copies, waits for them, and re-layouts  3.13 us (2%)
  between operations  1.71 us (1%)
    all_to_all x5, blocking collectives, exchange(): lax.all_to_all(blocks, axes, split_axis=0, concat_axis=0, tiled=True, axi...  97.2 us
    all_to_all x1, waiting for transfers between devices, exchange(): lax.all_to_all(blocks, axes, split_axis=0, concat_axis=0, tiled=True, axi...  21.3 us
    all_to_all x1, starting transfers between devices, exchange(): lax.all_to_all(blocks, axes, split_axis=0, concat_axis=0, tiled=True, axi...  11 us
    ppermute x1, starting transfers between devices, local(): other_grids = lax.ppermute(mine_grids, 'facet', CORE_SWAP)  7.29 us
    pallas_call x1, Pallas kernels, forward(): on_core(forward_kernel, 'ahead', [blocks, blocks, pltpu.HBM(phases, jnp.f...  7.06 us
    pallas_call x1, Pallas kernels, backward(): on_core(backward_kernel, 'back', [shaped((LAYERS, 2, COLS, QUARTER), jnp....  4.84 us
    ppermute x1, starting transfers between devices, local(): arrived = lax.ppermute(other, 'facet', CORE_SWAP)  4.78 us
  transfers between devices with their start and end apart: 3, of which 3 were waited for; matrix products, arithmetic and copies ran while one was open for 2% of the time, Pallas kernels for 0%

profile of v3, /device:TPU:1, one launch (start us, length us, event | category | flops | bytes accessed | tf_op | source)
XLA Modules:
  0.0 170.3 jit_solution(13202658148898087359)
XLA Ops:
  0.6 2.4 %gather.1 = bf16[4,6,16,2048]{3,2,1,0:T(8,128)(2,1)} custom-call(bf16[2,64,2048]{2,1,0:T(8,128)(2,1)} %bitcast.40, bf16[64,8192]{1,0:T(8,128)(2,1)} %bitcast.34), custom_call_target="tpu_custom_call" | custom-call | tf_op jit(solution)/shard_map/gather/pallas_call | solution.py:371
  3.2 11.0 %all-to-all-start = ((bf16[4,6,16,2048]{3,2,1,0:T(8,128)(2,1)}), bf16[4,6,16,2048]{3,2,1,0:T(8,128)(2,1)S(1)}, u32[]{:S(2)}, u32[]{:S(2)}) async-start(bf16[4,6,16,2048]{3,2,1,0:T(8,128)(2,1)} %gather.1), calls=%async_computation | async-start | bytes 3145728 | tf_op jit(solution)/shard_map/all_to_all | solution.py:459
  14.9 0.5 broadcast.167
  15.4 0.7 reduce.3
  16.2 1.1 multiply_bitcast_fusion
  18.2 21.3 %all-to-all-done.pieces = bf16[4,6,16,2048]{3,2,1,0:T(8,128)(2,1)S(1)} async-done(((bf16[4,6,16,2048]{3,2,1,0:T(8,128)(2,1)}), bf16[4,6,16,2048]{3,2,1,0:T(8,128)(2,1)S(1)}, u32[]{:S(2)}, u32[]{:S(2)}) %all-to-all-start) | async-done | bytes 1572896 | tf_op jit(solution)/shard_map/all_to_all | solution.py:459
  39.6 7.1 %ahead.1 = (bf16[8,512,128]{2,1,0:T(8,128)(2,1)S(1)}, bf16[8,512,128]{2,1,0:T(8,128)(2,1)S(1)}, f32[2,6144,128]{2,1,0:T(8,128)}) custom-call(bf16[4,6,16,2048]{3,2,1,0:T(8,128)(2,1)S(1)} %all-to-all-done.pieces, f32[64,128]{1,0:T(8,128)S(1)} %copy-done.2, f32[64,128]{1,0:T(8,128)S(1)} %copy-done.1, bf16[128,128]{1,0:T(8,128)(2,1)S(1)} %copy-done.4, ...), custom_call_target="tpu_custom_call" | custom-call | tf_op jit(solution)/shard_map/ahead/pallas_call | solution.py:390
  46.6 4.8 %collective-permute-start = (bf16[8,512,128]{2,1,0:T(8,128)(2,1)S(1)}, bf16[8,512,128]{2,1,0:T(8,128)(2,1)S(1)}, u32[]{:S(2)}, u32[]{:S(2)}) collective-permute-start(bf16[8,512,128]{2,1,0:T(8,128)(2,1)S(1)} %get-tuple-element.25), channel_id=1, source_target_pairs={{0,1},{1,0},{2,3},{3,2},{4,5},{5,4},{6,7},{7,6},{8,9},{9,8},{10,11... | collective-permute-start | bytes 3145736 | tf_op jit(solution)/shard_map/ppermute | solution.py:494
  51.4 2.3 %collective-permute-done = bf16[8,512,128]{2,1,0:T(8,128)(2,1)S(1)} collective-permute-done((bf16[8,512,128]{2,1,0:T(8,128)(2,1)S(1)}, bf16[8,512,128]{2,1,0:T(8,128)(2,1)S(1)}, u32[]{:S(2)}, u32[]{:S(2)}) %collective-permute-start) | collective-permute-done | bytes 1048608 | tf_op jit(solution)/shard_map/ppermute | solution.py:494
  54.0 30.9 %all_to_all.30.pieces = bf16[8,512,128]{2,1,0:T(8,128)(2,1)S(1)} all-to-all(bf16[8,512,128]{2,1,0:T(8,128)(2,1)S(1)} %add_convert_fusion), channel_id=1, replica_groups={{0,2,4,6,8,10,12,14},{1,3,5,7,9,11,13,15},{16,18,20,22,24,26,28,30},{17..., dimensions={0} | all-to-all | bytes 2097152 | tf_op jit(solution)/shard_map/all_to_all | solution.py:459
  84.9 0.4 pack.1
  85.3 19.2 %all_to_all.31 = bf16[32,16,128]{2,1,0:T(8,128)(2,1)S(1)} all-to-all(bf16[32,16,128]{2,1,0:T(8,128)(2,1)S(1)} %pack.1), channel_id=1, replica_groups={{0,128,256,384,16,144,272,400,32,160,288,416,48,176,304,432,64,192,320,..., dimensions={0} | all-to-all | bytes 262144 | tf_op jit(solution)/shard_map/all_to_all | solution.py:459
  104.5 0.4 reshape.147
  105.3 0.4 fusion.20
  105.8 0.6 pad_maximum_fusion
  106.4 0.4 convolution_convert_fusion
  107.2 14.5 %all_to_all.32.line = bf16[32,16,128]{2,1,0:T(8,128)(2,1)S(1)} all-to-all(bf16[32,16,128]{2,1,0:T(8,128)(2,1)S(1)} %bitcast.39), channel_id=1, replica_groups={{0,128,256,384,16,144,272,400,32,160,288,416,48,176,304,432,64,192,320,..., dimensions={0} | all-to-all | bytes 262144 | tf_op jit(solution)/shard_map/all_to_all | solution.py:459
  121.7 0.4 unpack.1
  122.1 14.7 %all_to_all.33.mine = bf16[8,512,128]{2,1,0:T(8,128)(2,1)S(1)} all-to-all(bf16[8,512,128]{2,1,0:T(8,128)(2,1)S(1)} %unpack.1), channel_id=1, replica_groups={{0,2,4,6,8,10,12,14},{1,3,5,7,9,11,13,15},{16,18,20,22,24,26,28,30},{17..., dimensions={0} | all-to-all | bytes 2097152 | tf_op jit(solution)/shard_map/all_to_all | solution.py:459
  136.7 7.3 %collective-permute-start.1 = (bf16[8,512,128]{2,1,0:T(8,128)(2,1)S(1)}, bf16[8,512,128]{2,1,0:T(8,128)(2,1)S(1)}, u32[]{:S(2)}, u32[]{:S(2)}) collective-permute-start(bf16[8,512,128]{2,1,0:T(8,128)(2,1)S(1)} %all_to_all.33.mine), channel_id=1, source_target_pairs={{0,1},{1,0},{2,3},{3,2},{4,5},{5,4},{6,7},{7,6},{8,9},{9,8},{10,11... | collective-permute-start | bytes 3145736 | tf_op jit(solution)/shard_map/ppermute | solution.py:539
  144.0 2.3 %collective-permute-done.1.other = bf16[8,512,128]{2,1,0:T(8,128)(2,1)S(1)} collective-permute-done((bf16[8,512,128]{2,1,0:T(8,128)(2,1)S(1)}, bf16[8,512,128]{2,1,0:T(8,128)(2,1)S(1)}, u32[]{:S(2)}, u32[]{:S(2)}) %collective-permute-start.1) | collective-permute-done | bytes 1048608 | tf_op jit(solution)/shard_map/ppermute | solution.py:539
  146.3 4.8 %back.1 = bf16[4,2,16,2048]{3,2,1,0:T(8,128)(2,1)S(1)} custom-call(bf16[8,512,128]{2,1,0:T(8,128)(2,1)S(1)} %all_to_all.33.mine, bf16[8,512,128]{2,1,0:T(8,128)(2,1)S(1)} %collective-permute-done.1.other, f32[2,6144,128]{2,1,0:T(8,128)} %get-tuple-element.32.phases_in, f32[64,128]{1,0:T(8,128)S(1)} %copy-done.2, f32[64,128]{1,0:T(8,128)S(1)} %copy-done.1, ...), custom_call_target="tpu_custom_call" | custom-call | tf_op jit(solution)/shard_map/back/pallas_call | solution.py:407
  151.1 18.0 %all_to_all.34 = bf16[4,2,16,2048]{3,2,1,0:T(8,128)(2,1)S(1)} all-to-all(bf16[4,2,16,2048]{3,2,1,0:T(8,128)(2,1)S(1)} %back.1), channel_id=1, replica_groups=mesh['layer'=4,'facet'=128] {'layer'}, dimensions={0} | all-to-all | bytes 1048576 | tf_op jit(solution)/shard_map/all_to_all | solution.py:459
  169.3 1.1 copy.42
  (58 shorter events, 2.2 us)
Async XLA Ops:
  3.0 12.3 %copy-start.9 = (f32[1,8192]{1,0:T(1,128)S(1)}, f32[1,8192]{1,0:T(1,128)}, u32[]{:S(2)}) copy-start(f32[1,8192]{1,0:T(1,128)} %param.23) | copy-start | bytes 98308
  3.1 14.6 %copy-start.13 = (s32[1,1,512]{2,1,0:T(1,128)S(1)}, s32[1,1,512]{2,1,0:T(1,128)}, u32[]{:S(2)}) copy-start(s32[1,1,512]{2,1,0:T(1,128)} %param.29) | copy-start | bytes 6148
  3.1 14.6 %copy-start.14 = (f32[1,8]{1,0:T(1,128)S(1)}, f32[1,8]{1,0:T(1,128)}, u32[]{:S(2)}) copy-start(f32[1,8]{1,0:T(1,128)} %param.26) | copy-start | bytes 100
  3.1 14.6 %copy-start.11 = (s32[1,1,512]{2,1,0:T(1,128)S(1)}, s32[1,1,512]{2,1,0:T(1,128)}, u32[]{:S(2)}) copy-start(s32[1,1,512]{2,1,0:T(1,128)} %param.28) | copy-start | bytes 6148
  3.1 14.6 %copy-start.12 = (s32[1,1,512]{2,1,0:T(1,128)S(1)}, s32[1,1,512]{2,1,0:T(1,128)}, u32[]{:S(2)}) copy-start(s32[1,1,512]{2,1,0:T(1,128)} %param.27) | copy-start | bytes 6148
  3.1 14.7 %copy-start.15 = (f32[7]{0:T(128)S(1)}, f32[7]{0:T(128)}, u32[]{:S(2)}) copy-start(f32[7]{0:T(128)} %param.25) | copy-start | bytes 88
  3.1 15.0 %copy-start.10 = (f32[1,1,2,512]{3,2,1,0:T(2,128)S(1)}, f32[1,1,2,512]{3,2,1,0:T(2,128)}, u32[]{:S(2)}) copy-start(f32[1,1,2,512]{3,2,1,0:T(2,128)} %param.30) | copy-start | bytes 12292
  3.1 15.0 %copy-start.5 = (bf16[256,256]{1,0:T(8,128)(2,1)S(1)}, bf16[256,256]{1,0:T(8,128)(2,1)}, u32[]{:S(2)}) copy-start(bf16[256,256]{1,0:T(8,128)(2,1)} %constant.104.clone) | copy-start | bytes 393220
  3.1 15.0 %copy-start.6 = (bf16[256,256]{1,0:T(8,128)(2,1)S(1)}, bf16[256,256]{1,0:T(8,128)(2,1)}, u32[]{:S(2)}) copy-start(bf16[256,256]{1,0:T(8,128)(2,1)} %constant.103.clone) | copy-start | bytes 393220
  3.1 15.0 %copy-start.7 = (bf16[256,256]{1,0:T(8,128)(2,1)S(1)}, bf16[256,256]{1,0:T(8,128)(2,1)}, u32[]{:S(2)}) copy-start(bf16[256,256]{1,0:T(8,128)(2,1)} %constant.102.clone) | copy-start | bytes 393220
  3.2 15.0 %copy-start.8 = (bf16[256,256]{1,0:T(8,128)(2,1)S(1)}, bf16[256,256]{1,0:T(8,128)(2,1)}, u32[]{:S(2)}) copy-start(bf16[256,256]{1,0:T(8,128)(2,1)} %constant.101.clone) | copy-start | bytes 393220
  3.2 36.4 %all-to-all-start = ((bf16[4,6,16,2048]{3,2,1,0:T(8,128)(2,1)}), bf16[4,6,16,2048]{3,2,1,0:T(8,128)(2,1)S(1)}, u32[]{:S(2)}, u32[]{:S(2)}) async-start(bf16[4,6,16,2048]{3,2,1,0:T(8,128)(2,1)} %gather.1), calls=%async_computation | async-start | bytes 3145728 | tf_op jit(solution)/shard_map/all_to_all | solution.py:459
  14.2 25.4 %copy-start.1 = (f32[64,128]{1,0:T(8,128)S(1)}, f32[64,128]{1,0:T(8,128)}, u32[]{:S(2)}) copy-start(f32[64,128]{1,0:T(8,128)} %constant.106.clone.twist_imag) | copy-start | bytes 98308
  14.2 25.4 %copy-start.2 = (f32[64,128]{1,0:T(8,128)S(1)}, f32[64,128]{1,0:T(8,128)}, u32[]{:S(2)}) copy-start(f32[64,128]{1,0:T(8,128)} %constant.105.clone.twist_real) | copy-start | bytes 98308
  14.2 25.4 %copy-start.4 = (bf16[128,128]{1,0:T(8,128)(2,1)S(1)}, bf16[128,128]{1,0:T(8,128)(2,1)}, u32[]{:S(2)}) copy-start(bf16[128,128]{1,0:T(8,128)(2,1)} %constant.107.clone.first) | copy-start | bytes 98308
  46.6 7.1 %collective-permute-start = (bf16[8,512,128]{2,1,0:T(8,128)(2,1)S(1)}, bf16[8,512,128]{2,1,0:T(8,128)(2,1)S(1)}, u32[]{:S(2)}, u32[]{:S(2)}) collective-permute-start(bf16[8,512,128]{2,1,0:T(8,128)(2,1)S(1)} %get-tuple-element.25), channel_id=1, source_target_pairs={{0,1},{1,0},{2,3},{3,2},{4,5},{5,4},{6,7},{7,6},{8,9},{9,8},{10,11... | collective-permute-start | bytes 3145736 | tf_op jit(solution)/shard_map/ppermute | solution.py:494
  53.7 31.2 %copy-start = (bf16[512,512]{1,0:T(8,128)(2,1)S(1)}, bf16[512,512]{1,0:T(8,128)(2,1)}, u32[]{:S(2)}) copy-start(bf16[512,512]{1,0:T(8,128)(2,1)} %constant.108.clone.table) | copy-start | bytes 1572868
  107.2 39.1 %copy-start.3 = (bf16[128,128]{1,0:T(8,128)(2,1)S(1)}, bf16[128,128]{1,0:T(8,128)(2,1)}, u32[]{:S(2)}) copy-start(bf16[128,128]{1,0:T(8,128)(2,1)} %constant.109.clone.first) | copy-start | bytes 98308
  136.7 9.6 %collective-permute-start.1 = (bf16[8,512,128]{2,1,0:T(8,128)(2,1)S(1)}, bf16[8,512,128]{2,1,0:T(8,128)(2,1)S(1)}, u32[]{:S(2)}, u32[]{:S(2)}) collective-permute-start(bf16[8,512,128]{2,1,0:T(8,128)(2,1)S(1)} %all_to_all.33.mine), channel_id=1, source_target_pairs={{0,1},{1,0},{2,3},{3,2},{4,5},{5,4},{6,7},{7,6},{8,9},{9,8},{10,11... | collective-permute-start | bytes 3145736 | tf_op jit(solution)/shard_map/ppermute | solution.py:539

commit v4 on v3

--- a/solution.py
+++ b/solution.py
@@ -111,11 +111,10 @@
 def gather_kernel(strip, screen, out_ref, blocks, in_sems, out_sems):
     def arrivals(cq):
         rows = pl.ds(cq * COLS, COLS)
-        pairs = [(strip.at[:, rows, :], blocks.at[cq, pl.ds(0, 2)])]
-        for nq in range(LAYERS):
-            pairs.append(
-                (screen.at[rows, pl.ds(nq * QUARTER, QUARTER)], blocks.at[cq, 2 + nq])
-            )
+        pairs = [(screen.at[rows, :], blocks.at[cq, :, pl.ds(0, STRIP_LEN)])]
+        for part in range(2):
+            lanes = pl.ds(STRIP_LEN + part * QUARTER, QUARTER)
+            pairs.append((strip.at[part, rows, :], blocks.at[cq, :, lanes]))
         return [
             pltpu.make_async_copy(source, target, in_sems.at[cq, i])
             for i, (source, target) in enumerate(pairs)
@@ -135,9 +134,13 @@
         departure(cq).wait()
 
 
-def phase_copy(source, target, sems, layer):
-    rows = pl.ds(layer * PHASE_ROWS, PHASE_ROWS)
-    return pltpu.make_async_copy(source.at[:, rows, :], target.at[:, rows, :], sems.at[layer])
+def valid_rows(phases, layer):
+    padded = phases.reshape(2, LAYERS * SUB_ROWS, COL_PITCH, LANES)
+    return padded.at[:, pl.ds(layer * SUB_ROWS, SUB_ROWS), pl.ds(0, COLS), :]
+
+
+def layer_rows(phases, layer):
+    return phases.at[:, pl.ds(layer * SUB_ROWS, SUB_ROWS)]
 
 
 def forward_kernel(
@@ -147,20 +150,21 @@
     table = first[...]
 
     def strip_block(t, carry):
-        lanes = pl.ds(pl.multiple_of(t * LANES, LANES), LANES)
         for nq in range(LAYERS):
             rows = pl.ds(pl.multiple_of((nq * BLOCKS + t) * COL_PITCH, 8), COLS)
             for part in range(2):
-                strip[part, rows, :] = pieces[nq, part, :, lanes].astype(jnp.float32)
+                start = STRIP_LEN + part * QUARTER + t * LANES
+                lanes = pl.ds(pl.multiple_of(start, LANES), LANES)
+                strip[part, rows, :] = pieces[nq, :, lanes].astype(jnp.float32)
         return carry
 
     lax.fori_loop(0, BLOCKS, strip_block, 0, unroll=2)
     for layer in range(LAYERS):
 
         def phase_block(t, carry, layer=layer):
-            lanes = pl.ds(pl.multiple_of(t * LANES, LANES), LANES)
             for nq in range(LAYERS):
-                cosine, sine = phase_parts(pieces[layer, 2 + nq, :, lanes].astype(jnp.float32))
+                lanes = pl.ds(pl.multiple_of(nq * QUARTER + t * LANES, LANES), LANES)
+                cosine, sine = phase_parts(pieces[layer, :, lanes].astype(jnp.float32))
                 rows = pl.ds(
                     pl.multiple_of(layer * PHASE_ROWS + (nq * BLOCKS + t) * COL_PITCH, 8), COLS
                 )
@@ -169,7 +173,9 @@
             return carry
 
         lax.fori_loop(0, BLOCKS, phase_block, 0, unroll=4)
-        phase_copy(phases, phases_out, sems, layer).start()
+        pltpu.make_async_copy(
+            valid_rows(phases, layer), layer_rows(phases_out, layer), sems.at[layer]
+        ).start()
 
         def first_block(pair, carry, layer=layer):
             c = pair * 2
@@ -194,7 +200,7 @@
                 half[1, rows, :] = real * twist_imag[...] + imag * twist_real[...]
             return carry
 
-        lax.fori_loop(0, COLS // 2, first_block, 0, unroll=4)
+        lax.fori_loop(0, COLS // 2, first_block, 0, unroll=8)
 
     weights = second[...]
 
@@ -219,9 +225,11 @@
         other_ref[:, place, :] = both[ZX:]
         return carry
 
-    lax.fori_loop(0, SUB_ROWS // 2, second_block, 0, unroll=8)
+    lax.fori_loop(0, SUB_ROWS // 2, second_block, 0, unroll=16)
     for layer in range(LAYERS):
-        phase_copy(phases, phases_out, sems, layer).wait()
+        pltpu.make_async_copy(
+            valid_rows(phases, layer), layer_rows(phases_out, layer), sems.at[layer]
+        ).wait()
 
 
 def pack_kernel(pieces, table, out_ref, total):
@@ -265,7 +273,9 @@
     out_ref, phases, half, total, sems,
 ):
     for layer in range(LAYERS):
-        phase_copy(phases_in, phases, sems, layer).start()
+        pltpu.make_async_copy(
+            layer_rows(phases_in, layer), valid_rows(phases, layer), sems.at[layer]
+        ).start()
     weights = second[...]
 
     def second_block(pair, carry):
@@ -293,10 +303,12 @@
             half[1, rows, :] = imag * tr - real * ti
         return carry
 
-    lax.fori_loop(0, SUB_ROWS // 2, second_block, 0, unroll=8)
+    lax.fori_loop(0, SUB_ROWS // 2, second_block, 0, unroll=16)
 
     for layer in range(LAYERS):
-        phase_copy(phases_in, phases, sems, layer).wait()
+        pltpu.make_async_copy(
+            layer_rows(phases_in, layer), valid_rows(phases, layer), sems.at[layer]
+        ).wait()
     table = first[...]
 
     def first_block(pair, carry):
@@ -332,7 +344,7 @@
                 total[part, pl.ds(c + h, SUB_ROWS, stride=COL_PITCH), :] = back_gain * sums[2 * h + part]
         return carry
 
-    lax.fori_loop(0, COLS // 2, first_block, 0, unroll=4)
+    lax.fori_loop(0, COLS // 2, first_block, 0, unroll=8)
 
     def leave_block(t, carry):
         lanes = pl.ds(pl.multiple_of(t * LANES, LANES), LANES)
@@ -343,6 +355,18 @@
         return carry
 
     lax.fori_loop(0, BLOCKS, leave_block, 0, unroll=2)
+
+
+def join_kernel(terms, out_ref, total, sems):
+    def departure(cq):
+        rows = pl.ds(cq * COLS, COLS)
+        return pltpu.make_async_copy(total.at[cq], out_ref.at[:, rows, :], sems.at[cq])
+
+    for cq in range(LAYERS):
+        total[cq] = terms[cq].astype(jnp.float32)
+        departure(cq).start()
+    for cq in range(LAYERS):
+        departure(cq).wait()
 
 
 def on_core(kernel, name, out_shape, scratch, inputs, far_in=(), far_out=()):
@@ -367,14 +391,14 @@
 
 
 def gather(strip, screen):
-    blocks = (LAYERS, 2 + LAYERS, COLS, QUARTER)
+    blocks = (LAYERS, COLS, STRIP_LEN + 2 * QUARTER)
     return on_core(
         gather_kernel,
         "gather",
         [pltpu.HBM(blocks, jnp.bfloat16)],
         (
             pltpu.VMEM(blocks, jnp.bfloat16),
-            pltpu.SemaphoreType.DMA((LAYERS, 1 + LAYERS)),
+            pltpu.SemaphoreType.DMA((LAYERS, 3)),
             pltpu.SemaphoreType.DMA((LAYERS,)),
         ),
         2,
@@ -385,14 +409,14 @@
 
 def forward(pieces, factor_real, factor_imag, second):
     blocks = shaped((ZX, SUB_ROWS * Y, LANES), jnp.bfloat16)
-    phases = (2, LAYERS * PHASE_ROWS, LANES)
+    phases = (2, LAYERS * SUB_ROWS, COLS, LANES)
     twist_real, twist_imag = twiddle()
     return on_core(
         forward_kernel,
         "ahead",
         [blocks, blocks, pltpu.HBM(phases, jnp.float32)],
         (
-            pltpu.VMEM(phases, jnp.float32),
+            pltpu.VMEM((2, LAYERS * PHASE_ROWS, LANES), jnp.float32),
             pltpu.VMEM((2, PHASE_ROWS, LANES), jnp.float32),
             pltpu.VMEM((2, SUB_ROWS * LINE_PITCH, LANES), jnp.float32),
             pltpu.SemaphoreType.DMA((LAYERS,)),
@@ -452,7 +476,7 @@
         [weighted_real[:, None] * column_weights, weighted_imag[:, None] * column_weights], axis=1
     )
     adjoint = jnp.dot(row_weights.T, spread_cols, precision=lax.Precision.HIGHEST)
-    return (jnp.stack([residual_real, residual_imag]), adjoint)
+    return ((residual_real, residual_imag), adjoint)
 
 
 def exchange(blocks, axes, groups=None):
@@ -536,15 +560,22 @@
         2,
     )(line, table)[0]
     mine_grids = exchange(copies, "facet", PLANE_GROUPS)
+    mine_grids, residual = lax.optimization_barrier((mine_grids, residual))
     other_grids = lax.ppermute(mine_grids, "facet", CORE_SWAP)
+    other_grids, residual = lax.optimization_barrier((other_grids, jnp.stack(residual)))
     leaving = backward(mine_grids, other_grids, phases, factor_real, factor_imag, second_back)
-    gradient = (
-        exchange(leaving, "layer")
-        .transpose(1, 0, 2, 3)
-        .reshape(1, 2, STRIP_COLS, QUARTER)
-        .astype(jnp.float32)
-    )
-    return (residual[None, None], gradient)
+    gradient = on_core(
+        join_kernel,
+        "join",
+        [pltpu.HBM((2, STRIP_COLS, QUARTER), jnp.float32)],
+        (
+            pltpu.VMEM((LAYERS, 2, COLS, QUARTER), jnp.float32),
+            pltpu.SemaphoreType.DMA((LAYERS,)),
+        ),
+        1,
+        far_out=(0,),
+    )(exchange(leaving, "layer"))[0]
+    return (residual[None, None], gradient[None])
 
 
 def solution(mesh):

time: 171 us -> 168 us (0.982)
  no operation moved by 1% of the time
where the time goes in v4:
time: 168 us
  blocking collectives  97.2 us (58%)
  waiting for transfers between devices  25.2 us (15%)
  starting transfers between devices  23.1 us (14%)
  Pallas kernels  14.2 us (8%)
  other arithmetic  3.36 us (2%)
  local copies, waits for them, and re-layouts  2.06 us (1%)
  between operations  1.71 us (1%)
    all_to_all x5, blocking collectives, exchange(): lax.all_to_all(blocks, axes, split_axis=0, concat_axis=0, tiled=True, axi...  97.2 us
    all_to_all x1, waiting for transfers between devices, exchange(): lax.all_to_all(blocks, axes, split_axis=0, concat_axis=0, tiled=True, axi...  21.3 us
    all_to_all x1, starting transfers between devices, exchange(): lax.all_to_all(blocks, axes, split_axis=0, concat_axis=0, tiled=True, axi...  11 us
    ppermute x1, starting transfers between devices, local(): other_grids = lax.ppermute(mine_grids, 'facet', CORE_SWAP)  7.3 us
    pallas_call x1, Pallas kernels, forward(): on_core(forward_kernel, 'ahead', [blocks, blocks, pltpu.HBM(phases, jnp.f...  6.1 us
    ppermute x1, starting transfers between devices, local(): arrived = lax.ppermute(other, 'facet', CORE_SWAP)  4.8 us
    pallas_call x1, Pallas kernels, backward(): on_core(backward_kernel, 'back', [shaped((LAYERS, 2, COLS, QUARTER), jnp....  4.09 us
  transfers between devices with their start and end apart: 3, of which 3 were waited for; matrix products, arithmetic and copies ran while one was open for 2% of the time, Pallas kernels for 0%

profile of v4, /device:TPU:1, one launch (start us, length us, event | category | flops | bytes accessed | tf_op | source)
XLA Modules:
  0.0 167.8 jit_solution(14600584579717241793)
XLA Ops:
  0.6 2.3 %gather.1 = bf16[4,16,12288]{2,1,0:T(8,128)(2,1)} custom-call(bf16[2,64,2048]{2,1,0:T(8,128)(2,1)} %bitcast.38, bf16[64,8192]{1,0:T(8,128)(2,1)} %bitcast.32), custom_call_target="tpu_custom_call" | custom-call | tf_op jit(solution)/shard_map/gather/pallas_call | solution.py:395
  3.0 11.0 %all-to-all-start = ((bf16[4,16,12288]{2,1,0:T(8,128)(2,1)}), bf16[4,16,12288]{2,1,0:T(8,128)(2,1)S(1)}, u32[]{:S(2)}, u32[]{:S(2)}) async-start(bf16[4,16,12288]{2,1,0:T(8,128)(2,1)} %gather.1), calls=%async_computation | async-start | bytes 3145728 | tf_op jit(solution)/shard_map/all_to_all | solution.py:483
  14.7 0.5 broadcast.167
  15.2 0.7 reduce.3
  16.1 1.1 multiply_bitcast_fusion
  18.1 21.3 %all-to-all-done.pieces = bf16[4,16,12288]{2,1,0:T(8,128)(2,1)S(1)} async-done(((bf16[4,16,12288]{2,1,0:T(8,128)(2,1)}), bf16[4,16,12288]{2,1,0:T(8,128)(2,1)S(1)}, u32[]{:S(2)}, u32[]{:S(2)}) %all-to-all-start) | async-done | bytes 1572896 | tf_op jit(solution)/shard_map/all_to_all | solution.py:483
  39.5 6.1 %ahead.1 = (bf16[8,512,128]{2,1,0:T(8,128)(2,1)S(1)}, bf16[8,512,128]{2,1,0:T(8,128)(2,1)S(1)}, f32[2,256,16,128]{3,2,1,0:T(8,128)}) custom-call(bf16[4,16,12288]{2,1,0:T(8,128)(2,1)S(1)} %all-to-all-done.pieces, f32[64,128]{1,0:T(8,128)S(1)} %copy-done.2, f32[64,128]{1,0:T(8,128)S(1)} %copy-done.1, bf16[128,128]{1,0:T(8,128)(2,1)S(1)} %copy-done.4, ...), custom_call_target="tpu_custom_call" | custom-call | tf_op jit(solution)/shard_map/ahead/pallas_call | solution.py:414
  45.6 4.8 %collective-permute-start = (bf16[8,512,128]{2,1,0:T(8,128)(2,1)S(1)}, bf16[8,512,128]{2,1,0:T(8,128)(2,1)S(1)}, u32[]{:S(2)}, u32[]{:S(2)}) collective-permute-start(bf16[8,512,128]{2,1,0:T(8,128)(2,1)S(1)} %get-tuple-element.31), channel_id=1, source_target_pairs={{0,1},{1,0},{2,3},{3,2},{4,5},{5,4},{6,7},{7,6},{8,9},{9,8},{10,11... | collective-permute-start | bytes 3145736 | tf_op jit(solution)/shard_map/ppermute | solution.py:518
  50.4 2.3 %collective-permute-done = bf16[8,512,128]{2,1,0:T(8,128)(2,1)S(1)} collective-permute-done((bf16[8,512,128]{2,1,0:T(8,128)(2,1)S(1)}, bf16[8,512,128]{2,1,0:T(8,128)(2,1)S(1)}, u32[]{:S(2)}, u32[]{:S(2)}) %collective-permute-start) | collective-permute-done | bytes 1048608 | tf_op jit(solution)/shard_map/ppermute | solution.py:518
  52.9 30.9 %all_to_all.30.pieces = bf16[8,512,128]{2,1,0:T(8,128)(2,1)S(1)} all-to-all(bf16[8,512,128]{2,1,0:T(8,128)(2,1)S(1)} %add_convert_fusion), channel_id=1, replica_groups={{0,2,4,6,8,10,12,14},{1,3,5,7,9,11,13,15},{16,18,20,22,24,26,28,30},{17..., dimensions={0} | all-to-all | bytes 2097152 | tf_op jit(solution)/shard_map/all_to_all | solution.py:483
  83.8 0.4 pack.1
  84.2 19.2 %all_to_all.31 = bf16[32,16,128]{2,1,0:T(8,128)(2,1)S(1)} all-to-all(bf16[32,16,128]{2,1,0:T(8,128)(2,1)S(1)} %pack.1), channel_id=1, replica_groups={{0,128,256,384,16,144,272,400,32,160,288,416,48,176,304,432,64,192,320,..., dimensions={0} | all-to-all | bytes 262144 | tf_op jit(solution)/shard_map/all_to_all | solution.py:483
  103.4 0.4 reshape.132
  104.2 0.4 fusion.20
  104.7 0.4 convolution_convert_fusion
  105.5 14.5 %all_to_all.32.line = bf16[32,16,128]{2,1,0:T(8,128)(2,1)S(1)} all-to-all(bf16[32,16,128]{2,1,0:T(8,128)(2,1)S(1)} %bitcast.37), channel_id=1, replica_groups={{0,128,256,384,16,144,272,400,32,160,288,416,48,176,304,432,64,192,320,..., dimensions={0} | all-to-all | bytes 262144 | tf_op jit(solution)/shard_map/all_to_all | solution.py:483
  120.0 0.4 unpack.1
  120.4 14.7 %all_to_all.33.mine = bf16[8,512,128]{2,1,0:T(8,128)(2,1)S(1)} all-to-all(bf16[8,512,128]{2,1,0:T(8,128)(2,1)S(1)} %unpack.1), channel_id=1, replica_groups={{0,2,4,6,8,10,12,14},{1,3,5,7,9,11,13,15},{16,18,20,22,24,26,28,30},{17..., dimensions={0} | all-to-all | bytes 2097152 | tf_op jit(solution)/shard_map/all_to_all | solution.py:483
  135.1 7.3 %collective-permute-start.1 = (bf16[8,512,128]{2,1,0:T(8,128)(2,1)S(1)}, bf16[8,512,128]{2,1,0:T(8,128)(2,1)S(1)}, u32[]{:S(2)}, u32[]{:S(2)}) collective-permute-start(bf16[8,512,128]{2,1,0:T(8,128)(2,1)S(1)} %all_to_all.33.mine), channel_id=1, source_target_pairs={{0,1},{1,0},{2,3},{3,2},{4,5},{5,4},{6,7},{7,6},{8,9},{9,8},{10,11... | collective-permute-start | bytes 3145736 | tf_op jit(solution)/shard_map/ppermute | solution.py:564
  142.4 0.6 pad_maximum_fusion
  143.0 1.7 collective-permute-done.1.other
  144.6 4.1 %back.1 = bf16[4,2,16,2048]{3,2,1,0:T(8,128)(2,1)S(1)} custom-call(bf16[8,512,128]{2,1,0:T(8,128)(2,1)S(1)} %all_to_all.33.mine, bf16[8,512,128]{2,1,0:T(8,128)(2,1)S(1)} %collective-permute-done.1.other, f32[2,256,16,128]{3,2,1,0:T(8,128)} %get-tuple-element.44.phases_in, f32[64,128]{1,0:T(8,128)S(1)} %copy-done.2, f32[64,128]{1,0:T(8,128)S(1)} %copy-done.1, ...), custom_call_target="tpu_custom_call" | custom-call | tf_op jit(solution)/shard_map/back/pallas_call | solution.py:431
  148.7 18.0 %all_to_all.34.terms = bf16[4,2,16,2048]{3,2,1,0:T(8,128)(2,1)S(1)} all-to-all(bf16[4,2,16,2048]{3,2,1,0:T(8,128)(2,1)S(1)} %back.1), channel_id=1, replica_groups=mesh['layer'=4,'facet'=128] {'layer'}, dimensions={0} | all-to-all | bytes 1048576 | tf_op jit(solution)/shard_map/all_to_all | solution.py:483
  166.7 1.0 join.1
  (57 shorter events, 2.1 us)
Async XLA Ops:
  2.9 12.3 %copy-start.9 = (f32[1,8192]{1,0:T(1,128)S(1)}, f32[1,8192]{1,0:T(1,128)}, u32[]{:S(2)}) copy-start(f32[1,8192]{1,0:T(1,128)} %param.23) | copy-start | bytes 98308
  2.9 14.6 %copy-start.13 = (s32[1,1,512]{2,1,0:T(1,128)S(1)}, s32[1,1,512]{2,1,0:T(1,128)}, u32[]{:S(2)}) copy-start(s32[1,1,512]{2,1,0:T(1,128)} %param.29) | copy-start | bytes 6148
  2.9 14.6 %copy-start.14 = (f32[1,8]{1,0:T(1,128)S(1)}, f32[1,8]{1,0:T(1,128)}, u32[]{:S(2)}) copy-start(f32[1,8]{1,0:T(1,128)} %param.26) | copy-start | bytes 100
  2.9 14.6 %copy-start.11 = (s32[1,1,512]{2,1,0:T(1,128)S(1)}, s32[1,1,512]{2,1,0:T(1,128)}, u32[]{:S(2)}) copy-start(s32[1,1,512]{2,1,0:T(1,128)} %param.28) | copy-start | bytes 6148
  3.0 14.6 %copy-start.12 = (s32[1,1,512]{2,1,0:T(1,128)S(1)}, s32[1,1,512]{2,1,0:T(1,128)}, u32[]{:S(2)}) copy-start(s32[1,1,512]{2,1,0:T(1,128)} %param.27) | copy-start | bytes 6148
  3.0 14.7 %copy-start.15 = (f32[7]{0:T(128)S(1)}, f32[7]{0:T(128)}, u32[]{:S(2)}) copy-start(f32[7]{0:T(128)} %param.25) | copy-start | bytes 88
  3.0 15.0 %copy-start.10 = (f32[1,1,2,512]{3,2,1,0:T(2,128)S(1)}, f32[1,1,2,512]{3,2,1,0:T(2,128)}, u32[]{:S(2)}) copy-start(f32[1,1,2,512]{3,2,1,0:T(2,128)} %param.30) | copy-start | bytes 12292
  3.0 15.0 %copy-start.5 = (bf16[256,256]{1,0:T(8,128)(2,1)S(1)}, bf16[256,256]{1,0:T(8,128)(2,1)}, u32[]{:S(2)}) copy-start(bf16[256,256]{1,0:T(8,128)(2,1)} %constant.104.clone) | copy-start | bytes 393220
  3.0 15.0 %copy-start.6 = (bf16[256,256]{1,0:T(8,128)(2,1)S(1)}, bf16[256,256]{1,0:T(8,128)(2,1)}, u32[]{:S(2)}) copy-start(bf16[256,256]{1,0:T(8,128)(2,1)} %constant.103.clone) | copy-start | bytes 393220
  3.0 15.0 %copy-start.7 = (bf16[256,256]{1,0:T(8,128)(2,1)S(1)}, bf16[256,256]{1,0:T(8,128)(2,1)}, u32[]{:S(2)}) copy-start(bf16[256,256]{1,0:T(8,128)(2,1)} %constant.102.clone) | copy-start | bytes 393220
  3.0 15.0 %copy-start.8 = (bf16[256,256]{1,0:T(8,128)(2,1)S(1)}, bf16[256,256]{1,0:T(8,128)(2,1)}, u32[]{:S(2)}) copy-start(bf16[256,256]{1,0:T(8,128)(2,1)} %constant.101.clone) | copy-start | bytes 393220
  3.0 36.4 %all-to-all-start = ((bf16[4,16,12288]{2,1,0:T(8,128)(2,1)}), bf16[4,16,12288]{2,1,0:T(8,128)(2,1)S(1)}, u32[]{:S(2)}, u32[]{:S(2)}) async-start(bf16[4,16,12288]{2,1,0:T(8,128)(2,1)} %gather.1), calls=%async_computation | async-start | bytes 3145728 | tf_op jit(solution)/shard_map/all_to_all | solution.py:483
  14.0 25.4 %copy-start.1 = (f32[64,128]{1,0:T(8,128)S(1)}, f32[64,128]{1,0:T(8,128)}, u32[]{:S(2)}) copy-start(f32[64,128]{1,0:T(8,128)} %constant.106.clone.twist_imag) | copy-start | bytes 98308
  14.0 25.4 %copy-start.2 = (f32[64,128]{1,0:T(8,128)S(1)}, f32[64,128]{1,0:T(8,128)}, u32[]{:S(2)}) copy-start(f32[64,128]{1,0:T(8,128)} %constant.105.clone.twist_real) | copy-start | bytes 98308
  14.0 25.4 %copy-start.4 = (bf16[128,128]{1,0:T(8,128)(2,1)S(1)}, bf16[128,128]{1,0:T(8,128)(2,1)}, u32[]{:S(2)}) copy-start(bf16[128,128]{1,0:T(8,128)(2,1)} %constant.107.clone.first) | copy-start | bytes 98308
  45.6 7.1 %collective-permute-start = (bf16[8,512,128]{2,1,0:T(8,128)(2,1)S(1)}, bf16[8,512,128]{2,1,0:T(8,128)(2,1)S(1)}, u32[]{:S(2)}, u32[]{:S(2)}) collective-permute-start(bf16[8,512,128]{2,1,0:T(8,128)(2,1)S(1)} %get-tuple-element.31), channel_id=1, source_target_pairs={{0,1},{1,0},{2,3},{3,2},{4,5},{5,4},{6,7},{7,6},{8,9},{9,8},{10,11... | collective-permute-start | bytes 3145736 | tf_op jit(solution)/shard_map/ppermute | solution.py:518
  52.6 31.1 %copy-start = (bf16[512,512]{1,0:T(8,128)(2,1)S(1)}, bf16[512,512]{1,0:T(8,128)(2,1)}, u32[]{:S(2)}) copy-start(bf16[512,512]{1,0:T(8,128)(2,1)} %constant.108.clone.table) | copy-start | bytes 1572868
  105.5 39.2 %copy-start.3 = (bf16[128,128]{1,0:T(8,128)(2,1)S(1)}, bf16[128,128]{1,0:T(8,128)(2,1)}, u32[]{:S(2)}) copy-start(bf16[128,128]{1,0:T(8,128)(2,1)} %constant.109.clone.first) | copy-start | bytes 98308
  135.1 9.6 %collective-permute-start.1 = (bf16[8,512,128]{2,1,0:T(8,128)(2,1)S(1)}, bf16[8,512,128]{2,1,0:T(8,128)(2,1)S(1)}, u32[]{:S(2)}, u32[]{:S(2)}) collective-permute-start(bf16[8,512,128]{2,1,0:T(8,128)(2,1)S(1)} %all_to_all.33.mine), channel_id=1, source_target_pairs={{0,1},{1,0},{2,3},{3,2},{4,5},{5,4},{6,7},{7,6},{8,9},{9,8},{10,11... | collective-permute-start | bytes 3145736 | tf_op jit(solution)/shard_map/ppermute | solution.py:564

commit v5 on v4

--- a/solution.py
+++ b/solution.py
@@ -135,7 +135,7 @@
 
 
 def valid_rows(phases, layer):
-    padded = phases.reshape(2, LAYERS * SUB_ROWS, COL_PITCH, LANES)
+    padded = phases.reshape(2, LAYERS * SUB_ROWS + 1, COL_PITCH, LANES)
     return padded.at[:, pl.ds(layer * SUB_ROWS, SUB_ROWS), pl.ds(0, COLS), :]
 
 
@@ -158,7 +158,7 @@
                 strip[part, rows, :] = pieces[nq, :, lanes].astype(jnp.float32)
         return carry
 
-    lax.fori_loop(0, BLOCKS, strip_block, 0, unroll=2)
+    lax.fori_loop(0, BLOCKS, strip_block, 0, unroll=4)
     for layer in range(LAYERS):
 
         def phase_block(t, carry, layer=layer):
@@ -172,18 +172,21 @@
                 phases[1, rows, :] = sine
             return carry
 
-        lax.fori_loop(0, BLOCKS, phase_block, 0, unroll=4)
+        lax.fori_loop(0, BLOCKS, phase_block, 0, unroll=8)
         pltpu.make_async_copy(
             valid_rows(phases, layer), layer_rows(phases_out, layer), sems.at[layer]
         ).start()
 
-        def first_block(pair, carry, layer=layer):
-            c = pair * 2
+    def first_block(pair, carry):
+        c = pair * 2
+        columns = []
+        for h in range(2):
+            rows = pl.ds(c + h, SUB_ROWS, stride=COL_PITCH)
+            columns.append((strip[0, rows, :], strip[1, rows, :]))
+        for layer in range(LAYERS):
             data = []
-            for h in range(2):
-                column = pl.ds(c + h, SUB_ROWS, stride=COL_PITCH)
+            for h, (real, imag) in enumerate(columns):
                 turn = pl.ds(layer * PHASE_ROWS + c + h, SUB_ROWS, stride=COL_PITCH)
-                real, imag = strip[0, column, :], strip[1, column, :]
                 cosine, sine = phases[0, turn, :], phases[1, turn, :]
                 data.append(
                     jnp.concatenate(
@@ -198,9 +201,9 @@
                 rows = pl.ds(layer * COLS + c + h, SUB_ROWS, stride=LINE_PITCH)
                 half[0, rows, :] = real * twist_real[...] - imag * twist_imag[...]
                 half[1, rows, :] = real * twist_imag[...] + imag * twist_real[...]
-            return carry
-
-        lax.fori_loop(0, COLS // 2, first_block, 0, unroll=8)
+        return carry
+
+    lax.fori_loop(0, COLS // 2, first_block, 0, unroll=2)
 
     weights = second[...]
 
@@ -233,7 +236,7 @@
 
 
 def pack_kernel(pieces, table, out_ref, total):
-    total[...] = jnp.sum(pieces[...].astype(jnp.float32), axis=0)
+    total[: SUB_ROWS * Y, :] = jnp.sum(pieces[...].astype(jnp.float32), axis=0)
     rows = []
     for y in range(Y):
         block = total[pl.ds(y, SUB_ROWS, stride=Y), :]
@@ -263,7 +266,7 @@
             total[pl.ds(r * 16 * Y + y, 16, stride=Y), :] = grids[
                 y * 16 : (y + 1) * 16, r * LANES : (r + 1) * LANES
             ]
-    block = total[...].astype(jnp.bfloat16)
+    block = total[: SUB_ROWS * Y, :].astype(jnp.bfloat16)
     for copy in range(ZX):
         out_ref[copy] = block
 
@@ -416,9 +419,9 @@
         "ahead",
         [blocks, blocks, pltpu.HBM(phases, jnp.float32)],
         (
-            pltpu.VMEM((2, LAYERS * PHASE_ROWS, LANES), jnp.float32),
-            pltpu.VMEM((2, PHASE_ROWS, LANES), jnp.float32),
-            pltpu.VMEM((2, SUB_ROWS * LINE_PITCH, LANES), jnp.float32),
+            pltpu.VMEM((2, LAYERS * PHASE_ROWS + COL_PITCH, LANES), jnp.float32),
+            pltpu.VMEM((2, PHASE_ROWS + COL_PITCH, LANES), jnp.float32),
+            pltpu.VMEM((2, (SUB_ROWS + 1) * LINE_PITCH, LANES), jnp.float32),
             pltpu.SemaphoreType.DMA((LAYERS,)),
         ),
         7,
@@ -433,9 +436,9 @@
         "back",
         [shaped((LAYERS, 2, COLS, QUARTER), jnp.bfloat16)],
         (
-            pltpu.VMEM((2, LAYERS * PHASE_ROWS, LANES), jnp.float32),
-            pltpu.VMEM((2, STRIP_COLS * LINE_PITCH, LANES), jnp.float32),
-            pltpu.VMEM((2, PHASE_ROWS, LANES), jnp.float32),
+            pltpu.VMEM((2, LAYERS * PHASE_ROWS + COL_PITCH, LANES), jnp.float32),
+            pltpu.VMEM((2, (STRIP_COLS + 1) * LINE_PITCH, LANES), jnp.float32),
+            pltpu.VMEM((2, PHASE_ROWS + COL_PITCH, LANES), jnp.float32),
             pltpu.SemaphoreType.DMA((LAYERS,)),
         ),
         9,
@@ -524,7 +527,7 @@
         pack_kernel,
         "pack",
         [shaped((Y * LAYERS, *piece), jnp.bfloat16)],
-        (pltpu.VMEM((SUB_ROWS * Y, LANES), jnp.float32),),
+        (pltpu.VMEM((SUB_ROWS * Y + Y, LANES), jnp.float32),),
         2,
     )(plane_terms, table)[0]
     line_sum = jnp.sum(
@@ -556,7 +559,7 @@
         unpack_kernel,
         "unpack",
         [shaped((ZX, SUB_ROWS * Y, LANES), jnp.bfloat16)],
-        (pltpu.VMEM((SUB_ROWS * Y, LANES), jnp.float32),),
+        (pltpu.VMEM((SUB_ROWS * Y + Y, LANES), jnp.float32),),
         2,
     )(line, table)[0]
     mine_grids = exchange(copies, "facet", PLANE_GROUPS)

time: 168 us -> 168 us (level)
  no operation moved by 1% of the time
where the time goes in v5:
time: 168 us; the launch traced here: 167 us
  blocking collectives  97.2 us (58%)
  waiting for transfers between devices  25.2 us (15%)
  starting transfers between devices  23.1 us (14%)
  Pallas kernels  14 us (8%)
  other arithmetic  3.36 us (2%)
  local copies, waits for them, and re-layouts  2.06 us (1%)
  between operations  1.71 us (1%)
    all_to_all x5, blocking collectives, exchange(): lax.all_to_all(blocks, axes, split_axis=0, concat_axis=0, tiled=True, axi...  97.2 us
    all_to_all x1, waiting for transfers between devices, exchange(): lax.all_to_all(blocks, axes, split_axis=0, concat_axis=0, tiled=True, axi...  21.3 us
    all_to_all x1, starting transfers between devices, exchange(): lax.all_to_all(blocks, axes, split_axis=0, concat_axis=0, tiled=True, axi...  11 us
    ppermute x1, starting transfers between devices, local(): other_grids = lax.ppermute(mine_grids, 'facet', CORE_SWAP)  7.3 us
    pallas_call x1, Pallas kernels, forward(): on_core(forward_kernel, 'ahead', [blocks, blocks, pltpu.HBM(phases, jnp.f...  5.85 us
    ppermute x1, starting transfers between devices, local(): arrived = lax.ppermute(other, 'facet', CORE_SWAP)  4.81 us
    pallas_call x1, Pallas kernels, backward(): on_core(backward_kernel, 'back', [shaped((LAYERS, 2, COLS, QUARTER), jnp....  4.07 us
  transfers between devices with their start and end apart: 3, of which 3 were waited for; matrix products, arithmetic and copies ran while one was open for 2% of the time, Pallas kernels for 0%

profile of v5, /device:TPU:1, one launch (start us, length us, event | category | flops | bytes accessed | tf_op | source)
XLA Modules:
  0.0 167.5 jit_solution(7370553101293154107)
XLA Ops:
  0.6 2.3 %gather.1 = bf16[4,16,12288]{2,1,0:T(8,128)(2,1)} custom-call(bf16[2,64,2048]{2,1,0:T(8,128)(2,1)} %bitcast.38, bf16[64,8192]{1,0:T(8,128)(2,1)} %bitcast.32), custom_call_target="tpu_custom_call" | custom-call | tf_op jit(solution)/shard_map/gather/pallas_call | solution.py:398
  3.0 11.0 %all-to-all-start = ((bf16[4,16,12288]{2,1,0:T(8,128)(2,1)}), bf16[4,16,12288]{2,1,0:T(8,128)(2,1)S(1)}, u32[]{:S(2)}, u32[]{:S(2)}) async-start(bf16[4,16,12288]{2,1,0:T(8,128)(2,1)} %gather.1), calls=%async_computation | async-start | bytes 3145728 | tf_op jit(solution)/shard_map/all_to_all | solution.py:486
  14.7 0.5 broadcast.167
  15.2 0.7 reduce.3
  16.1 1.1 multiply_bitcast_fusion
  18.1 21.3 %all-to-all-done.pieces = bf16[4,16,12288]{2,1,0:T(8,128)(2,1)S(1)} async-done(((bf16[4,16,12288]{2,1,0:T(8,128)(2,1)}), bf16[4,16,12288]{2,1,0:T(8,128)(2,1)S(1)}, u32[]{:S(2)}, u32[]{:S(2)}) %all-to-all-start) | async-done | bytes 1572896 | tf_op jit(solution)/shard_map/all_to_all | solution.py:486
  39.5 5.8 %ahead.1 = (bf16[8,512,128]{2,1,0:T(8,128)(2,1)S(1)}, bf16[8,512,128]{2,1,0:T(8,128)(2,1)S(1)}, f32[2,256,16,128]{3,2,1,0:T(8,128)}) custom-call(bf16[4,16,12288]{2,1,0:T(8,128)(2,1)S(1)} %all-to-all-done.pieces, f32[64,128]{1,0:T(8,128)S(1)} %copy-done.2, f32[64,128]{1,0:T(8,128)S(1)} %copy-done.1, bf16[128,128]{1,0:T(8,128)(2,1)S(1)} %copy-done.4, ...), custom_call_target="tpu_custom_call" | custom-call | tf_op jit(solution)/shard_map/ahead/pallas_call | solution.py:417
  45.3 4.8 %collective-permute-start = (bf16[8,512,128]{2,1,0:T(8,128)(2,1)S(1)}, bf16[8,512,128]{2,1,0:T(8,128)(2,1)S(1)}, u32[]{:S(2)}, u32[]{:S(2)}) collective-permute-start(bf16[8,512,128]{2,1,0:T(8,128)(2,1)S(1)} %get-tuple-element.31), channel_id=1, source_target_pairs={{0,1},{1,0},{2,3},{3,2},{4,5},{5,4},{6,7},{7,6},{8,9},{9,8},{10,11... | collective-permute-start | bytes 3145736 | tf_op jit(solution)/shard_map/ppermute | solution.py:521
  50.1 2.3 %collective-permute-done = bf16[8,512,128]{2,1,0:T(8,128)(2,1)S(1)} collective-permute-done((bf16[8,512,128]{2,1,0:T(8,128)(2,1)S(1)}, bf16[8,512,128]{2,1,0:T(8,128)(2,1)S(1)}, u32[]{:S(2)}, u32[]{:S(2)}) %collective-permute-start) | collective-permute-done | bytes 1048608 | tf_op jit(solution)/shard_map/ppermute | solution.py:521
  52.7 30.9 %all_to_all.30.pieces = bf16[8,512,128]{2,1,0:T(8,128)(2,1)S(1)} all-to-all(bf16[8,512,128]{2,1,0:T(8,128)(2,1)S(1)} %add_convert_fusion), channel_id=1, replica_groups={{0,2,4,6,8,10,12,14},{1,3,5,7,9,11,13,15},{16,18,20,22,24,26,28,30},{17..., dimensions={0} | all-to-all | bytes 2097152 | tf_op jit(solution)/shard_map/all_to_all | solution.py:486
  83.5 0.4 pack.1
  83.9 19.2 %all_to_all.31 = bf16[32,16,128]{2,1,0:T(8,128)(2,1)S(1)} all-to-all(bf16[32,16,128]{2,1,0:T(8,128)(2,1)S(1)} %pack.1), channel_id=1, replica_groups={{0,128,256,384,16,144,272,400,32,160,288,416,48,176,304,432,64,192,320,..., dimensions={0} | all-to-all | bytes 262144 | tf_op jit(solution)/shard_map/all_to_all | solution.py:486
  103.2 0.4 reshape.132
  103.9 0.4 fusion.20
  104.5 0.4 convolution_convert_fusion
  105.3 14.5 %all_to_all.32.line = bf16[32,16,128]{2,1,0:T(8,128)(2,1)S(1)} all-to-all(bf16[32,16,128]{2,1,0:T(8,128)(2,1)S(1)} %bitcast.37), channel_id=1, replica_groups={{0,128,256,384,16,144,272,400,32,160,288,416,48,176,304,432,64,192,320,..., dimensions={0} | all-to-all | bytes 262144 | tf_op jit(solution)/shard_map/all_to_all | solution.py:486
  119.7 0.4 unpack.1
  120.1 14.7 %all_to_all.33.mine = bf16[8,512,128]{2,1,0:T(8,128)(2,1)S(1)} all-to-all(bf16[8,512,128]{2,1,0:T(8,128)(2,1)S(1)} %unpack.1), channel_id=1, replica_groups={{0,2,4,6,8,10,12,14},{1,3,5,7,9,11,13,15},{16,18,20,22,24,26,28,30},{17..., dimensions={0} | all-to-all | bytes 2097152 | tf_op jit(solution)/shard_map/all_to_all | solution.py:486
  134.8 7.3 %collective-permute-start.1 = (bf16[8,512,128]{2,1,0:T(8,128)(2,1)S(1)}, bf16[8,512,128]{2,1,0:T(8,128)(2,1)S(1)}, u32[]{:S(2)}, u32[]{:S(2)}) collective-permute-start(bf16[8,512,128]{2,1,0:T(8,128)(2,1)S(1)} %all_to_all.33.mine), channel_id=1, source_target_pairs={{0,1},{1,0},{2,3},{3,2},{4,5},{5,4},{6,7},{7,6},{8,9},{9,8},{10,11... | collective-permute-start | bytes 3145736 | tf_op jit(solution)/shard_map/ppermute | solution.py:567
  142.1 0.6 pad_maximum_fusion
  142.7 1.7 collective-permute-done.1.other
  144.4 4.1 %back.1 = bf16[4,2,16,2048]{3,2,1,0:T(8,128)(2,1)S(1)} custom-call(bf16[8,512,128]{2,1,0:T(8,128)(2,1)S(1)} %all_to_all.33.mine, bf16[8,512,128]{2,1,0:T(8,128)(2,1)S(1)} %collective-permute-done.1.other, f32[2,256,16,128]{3,2,1,0:T(8,128)} %get-tuple-element.44.phases_in, f32[64,128]{1,0:T(8,128)S(1)} %copy-done.2, f32[64,128]{1,0:T(8,128)S(1)} %copy-done.1, ...), custom_call_target="tpu_custom_call" | custom-call | tf_op jit(solution)/shard_map/back/pallas_call | solution.py:434
  148.5 18.0 %all_to_all.34.terms = bf16[4,2,16,2048]{3,2,1,0:T(8,128)(2,1)S(1)} all-to-all(bf16[4,2,16,2048]{3,2,1,0:T(8,128)(2,1)S(1)} %back.1), channel_id=1, replica_groups=mesh['layer'=4,'facet'=128] {'layer'}, dimensions={0} | all-to-all | bytes 1048576 | tf_op jit(solution)/shard_map/all_to_all | solution.py:486
  166.5 1.0 join.1
  (57 shorter events, 2.1 us)
Async XLA Ops:
  2.9 12.3 %copy-start.9 = (f32[1,8192]{1,0:T(1,128)S(1)}, f32[1,8192]{1,0:T(1,128)}, u32[]{:S(2)}) copy-start(f32[1,8192]{1,0:T(1,128)} %param.23) | copy-start | bytes 98308
  2.9 14.6 %copy-start.13 = (s32[1,1,512]{2,1,0:T(1,128)S(1)}, s32[1,1,512]{2,1,0:T(1,128)}, u32[]{:S(2)}) copy-start(s32[1,1,512]{2,1,0:T(1,128)} %param.29) | copy-start | bytes 6148
  2.9 14.6 %copy-start.14 = (f32[1,8]{1,0:T(1,128)S(1)}, f32[1,8]{1,0:T(1,128)}, u32[]{:S(2)}) copy-start(f32[1,8]{1,0:T(1,128)} %param.26) | copy-start | bytes 100
  2.9 14.6 %copy-start.11 = (s32[1,1,512]{2,1,0:T(1,128)S(1)}, s32[1,1,512]{2,1,0:T(1,128)}, u32[]{:S(2)}) copy-start(s32[1,1,512]{2,1,0:T(1,128)} %param.28) | copy-start | bytes 6148
  3.0 14.6 %copy-start.12 = (s32[1,1,512]{2,1,0:T(1,128)S(1)}, s32[1,1,512]{2,1,0:T(1,128)}, u32[]{:S(2)}) copy-start(s32[1,1,512]{2,1,0:T(1,128)} %param.27) | copy-start | bytes 6148
  3.0 14.7 %copy-start.15 = (f32[7]{0:T(128)S(1)}, f32[7]{0:T(128)}, u32[]{:S(2)}) copy-start(f32[7]{0:T(128)} %param.25) | copy-start | bytes 88
  3.0 15.0 %copy-start.10 = (f32[1,1,2,512]{3,2,1,0:T(2,128)S(1)}, f32[1,1,2,512]{3,2,1,0:T(2,128)}, u32[]{:S(2)}) copy-start(f32[1,1,2,512]{3,2,1,0:T(2,128)} %param.30) | copy-start | bytes 12292
  3.0 15.0 %copy-start.5 = (bf16[256,256]{1,0:T(8,128)(2,1)S(1)}, bf16[256,256]{1,0:T(8,128)(2,1)}, u32[]{:S(2)}) copy-start(bf16[256,256]{1,0:T(8,128)(2,1)} %constant.104.clone) | copy-start | bytes 393220
  3.0 15.0 %copy-start.6 = (bf16[256,256]{1,0:T(8,128)(2,1)S(1)}, bf16[256,256]{1,0:T(8,128)(2,1)}, u32[]{:S(2)}) copy-start(bf16[256,256]{1,0:T(8,128)(2,1)} %constant.103.clone) | copy-start | bytes 393220
  3.0 15.0 %copy-start.7 = (bf16[256,256]{1,0:T(8,128)(2,1)S(1)}, bf16[256,256]{1,0:T(8,128)(2,1)}, u32[]{:S(2)}) copy-start(bf16[256,256]{1,0:T(8,128)(2,1)} %constant.102.clone) | copy-start | bytes 393220
  3.0 15.0 %copy-start.8 = (bf16[256,256]{1,0:T(8,128)(2,1)S(1)}, bf16[256,256]{1,0:T(8,128)(2,1)}, u32[]{:S(2)}) copy-start(bf16[256,256]{1,0:T(8,128)(2,1)} %constant.101.clone) | copy-start | bytes 393220
  3.0 36.4 %all-to-all-start = ((bf16[4,16,12288]{2,1,0:T(8,128)(2,1)}), bf16[4,16,12288]{2,1,0:T(8,128)(2,1)S(1)}, u32[]{:S(2)}, u32[]{:S(2)}) async-start(bf16[4,16,12288]{2,1,0:T(8,128)(2,1)} %gather.1), calls=%async_computation | async-start | bytes 3145728 | tf_op jit(solution)/shard_map/all_to_all | solution.py:486
  14.0 25.4 %copy-start.1 = (f32[64,128]{1,0:T(8,128)S(1)}, f32[64,128]{1,0:T(8,128)}, u32[]{:S(2)}) copy-start(f32[64,128]{1,0:T(8,128)} %constant.106.clone.twist_imag) | copy-start | bytes 98308
  14.0 25.4 %copy-start.2 = (f32[64,128]{1,0:T(8,128)S(1)}, f32[64,128]{1,0:T(8,128)}, u32[]{:S(2)}) copy-start(f32[64,128]{1,0:T(8,128)} %constant.105.clone.twist_real) | copy-start | bytes 98308
  14.0 25.4 %copy-start.4 = (bf16[128,128]{1,0:T(8,128)(2,1)S(1)}, bf16[128,128]{1,0:T(8,128)(2,1)}, u32[]{:S(2)}) copy-start(bf16[128,128]{1,0:T(8,128)(2,1)} %constant.107.clone.first) | copy-start | bytes 98308
  45.3 7.1 %collective-permute-start = (bf16[8,512,128]{2,1,0:T(8,128)(2,1)S(1)}, bf16[8,512,128]{2,1,0:T(8,128)(2,1)S(1)}, u32[]{:S(2)}, u32[]{:S(2)}) collective-permute-start(bf16[8,512,128]{2,1,0:T(8,128)(2,1)S(1)} %get-tuple-element.31), channel_id=1, source_target_pairs={{0,1},{1,0},{2,3},{3,2},{4,5},{5,4},{6,7},{7,6},{8,9},{9,8},{10,11... | collective-permute-start | bytes 3145736 | tf_op jit(solution)/shard_map/ppermute | solution.py:521
  52.4 31.1 %copy-start = (bf16[512,512]{1,0:T(8,128)(2,1)S(1)}, bf16[512,512]{1,0:T(8,128)(2,1)}, u32[]{:S(2)}) copy-start(bf16[512,512]{1,0:T(8,128)(2,1)} %constant.108.clone.table) | copy-start | bytes 1572868
  105.2 39.2 %copy-start.3 = (bf16[128,128]{1,0:T(8,128)(2,1)S(1)}, bf16[128,128]{1,0:T(8,128)(2,1)}, u32[]{:S(2)}) copy-start(bf16[128,128]{1,0:T(8,128)(2,1)} %constant.109.clone.first) | copy-start | bytes 98308
  134.8 9.6 %collective-permute-start.1 = (bf16[8,512,128]{2,1,0:T(8,128)(2,1)S(1)}, bf16[8,512,128]{2,1,0:T(8,128)(2,1)S(1)}, u32[]{:S(2)}, u32[]{:S(2)}) collective-permute-start(bf16[8,512,128]{2,1,0:T(8,128)(2,1)S(1)} %all_to_all.33.mine), channel_id=1, source_target_pairs={{0,1},{1,0},{2,3},{3,2},{4,5},{5,4},{6,7},{7,6},{8,9},{9,8},{10,11... | collective-permute-start | bytes 3145736 | tf_op jit(solution)/shard_map/ppermute | solution.py:567

commit v6 on v5

--- a/solution.py
+++ b/solution.py
@@ -250,6 +250,20 @@
             ]
 
 
+def subgrid_kernel(line, out_ref):
+    sums = [
+        sum(line[y * LAYERS + quarter].astype(jnp.float32) for y in range(Y))
+        for quarter in range(LAYERS)
+    ]
+    for r in range(4):
+        parts = []
+        for p in range(2):
+            for quarter in range(LAYERS):
+                start = r * 2 * COLS + p * COLS
+                parts.append(sums[quarter][:, start : start + COLS])
+        out_ref[r * 16 : (r + 1) * 16, :] = jnp.concatenate(parts, axis=1)
+
+
 def unpack_kernel(line, table, out_ref, total):
     data = jnp.concatenate(
         [
@@ -530,17 +544,9 @@
         (pltpu.VMEM((SUB_ROWS * Y + Y, LANES), jnp.float32),),
         2,
     )(plane_terms, table)[0]
-    line_sum = jnp.sum(
-        exchange(packed, ("layer", "facet"), LINE_GROUPS)
-        .reshape(Y, LAYERS, *piece)
-        .astype(jnp.float32),
-        axis=0,
-    )
-    subgrid = (
-        line_sum.reshape(LAYERS, SUB_ROWS // 4, 4, 2, COLS)
-        .transpose(2, 1, 3, 0, 4)
-        .reshape(SUB_ROWS, 2 * STRIP_COLS)
-    )
+    subgrid = on_core(
+        subgrid_kernel, "subgrid", [shaped((SUB_ROWS, 2 * STRIP_COLS), jnp.float32)], (), 1
+    )(exchange(packed, ("layer", "facet"), LINE_GROUPS))[0]
 
     residual, adjoint = degrid(subgrid, observed_vis, *prepared)
     residual, adjoint = lax.optimization_barrier((residual, adjoint.astype(jnp.bfloat16)))

time: 168 us -> 167 us (level)
  no operation moved by 1% of the time
where the time goes in v6:
time: 167 us
  blocking collectives  97.3 us (58%)
  waiting for transfers between devices  25.2 us (15%)
  starting transfers between devices  23.1 us (14%)
  Pallas kernels  14.1 us (8%)
  other arithmetic  3.34 us (2%)
  between operations  1.69 us (1%)
    all_to_all x5, blocking collectives, exchange(): lax.all_to_all(blocks, axes, split_axis=0, concat_axis=0, tiled=True, axi...  97.3 us
    all_to_all x1, waiting for transfers between devices, exchange(): lax.all_to_all(blocks, axes, split_axis=0, concat_axis=0, tiled=True, axi...  21.3 us
    all_to_all x1, starting transfers between devices, exchange(): lax.all_to_all(blocks, axes, split_axis=0, concat_axis=0, tiled=True, axi...  11 us
    ppermute x1, starting transfers between devices, local(): other_grids = lax.ppermute(mine_grids, 'facet', CORE_SWAP)  7.28 us
    pallas_call x1, Pallas kernels, forward(): on_core(forward_kernel, 'ahead', [blocks, blocks, pltpu.HBM(phases, jnp.f...  5.85 us
    ppermute x1, starting transfers between devices, local(): arrived = lax.ppermute(other, 'facet', CORE_SWAP)  4.81 us
    pallas_call x1, Pallas kernels, backward(): on_core(backward_kernel, 'back', [shaped((LAYERS, 2, COLS, QUARTER), jnp....  4.07 us
  transfers between devices with their start and end apart: 3, of which 3 were waited for; matrix products, arithmetic and copies ran while one was open for 2% of the time, Pallas kernels for 0%

profile of v6, /device:TPU:1, one launch (start us, length us, event | category | flops | bytes accessed | tf_op | source)
XLA Modules:
  0.0 166.9 jit_solution(17392640120689637069)
XLA Ops:
  0.6 2.3 %gather.1 = bf16[4,16,12288]{2,1,0:T(8,128)(2,1)} custom-call(bf16[2,64,2048]{2,1,0:T(8,128)(2,1)} %bitcast.33, bf16[64,8192]{1,0:T(8,128)(2,1)} %bitcast.29), custom_call_target="tpu_custom_call" | custom-call | tf_op jit(solution)/shard_map/gather/pallas_call | solution.py:412
  3.0 11.0 %all-to-all-start = ((bf16[4,16,12288]{2,1,0:T(8,128)(2,1)}), bf16[4,16,12288]{2,1,0:T(8,128)(2,1)S(1)}, u32[]{:S(2)}, u32[]{:S(2)}) async-start(bf16[4,16,12288]{2,1,0:T(8,128)(2,1)} %gather.1), calls=%async_computation | async-start | bytes 3145728 | tf_op jit(solution)/shard_map/all_to_all | solution.py:500
  14.7 0.5 broadcast.167
  15.2 0.7 reduce.3
  16.1 1.1 multiply_bitcast_fusion
  18.1 21.3 %all-to-all-done.pieces = bf16[4,16,12288]{2,1,0:T(8,128)(2,1)S(1)} async-done(((bf16[4,16,12288]{2,1,0:T(8,128)(2,1)}), bf16[4,16,12288]{2,1,0:T(8,128)(2,1)S(1)}, u32[]{:S(2)}, u32[]{:S(2)}) %all-to-all-start) | async-done | bytes 1572896 | tf_op jit(solution)/shard_map/all_to_all | solution.py:500
  39.5 5.8 %ahead.1 = (bf16[8,512,128]{2,1,0:T(8,128)(2,1)S(1)}, bf16[8,512,128]{2,1,0:T(8,128)(2,1)S(1)}, f32[2,256,16,128]{3,2,1,0:T(8,128)}) custom-call(bf16[4,16,12288]{2,1,0:T(8,128)(2,1)S(1)} %all-to-all-done.pieces, f32[64,128]{1,0:T(8,128)S(1)} %copy-done.2, f32[64,128]{1,0:T(8,128)S(1)} %copy-done.1, bf16[128,128]{1,0:T(8,128)(2,1)S(1)} %copy-done.4, ...), custom_call_target="tpu_custom_call" | custom-call | tf_op jit(solution)/shard_map/ahead/pallas_call | solution.py:431
  45.3 4.8 %collective-permute-start = (bf16[8,512,128]{2,1,0:T(8,128)(2,1)S(1)}, bf16[8,512,128]{2,1,0:T(8,128)(2,1)S(1)}, u32[]{:S(2)}, u32[]{:S(2)}) collective-permute-start(bf16[8,512,128]{2,1,0:T(8,128)(2,1)S(1)} %get-tuple-element.31), channel_id=1, source_target_pairs={{0,1},{1,0},{2,3},{3,2},{4,5},{5,4},{6,7},{7,6},{8,9},{9,8},{10,11... | collective-permute-start | bytes 3145736 | tf_op jit(solution)/shard_map/ppermute | solution.py:535
  50.1 2.3 %collective-permute-done = bf16[8,512,128]{2,1,0:T(8,128)(2,1)S(1)} collective-permute-done((bf16[8,512,128]{2,1,0:T(8,128)(2,1)S(1)}, bf16[8,512,128]{2,1,0:T(8,128)(2,1)S(1)}, u32[]{:S(2)}, u32[]{:S(2)}) %collective-permute-start) | collective-permute-done | bytes 1048608 | tf_op jit(solution)/shard_map/ppermute | solution.py:535
  52.4 0.3 add_convert_fusion
  52.7 30.9 %all_to_all.30.pieces = bf16[8,512,128]{2,1,0:T(8,128)(2,1)S(1)} all-to-all(bf16[8,512,128]{2,1,0:T(8,128)(2,1)S(1)} %add_convert_fusion), channel_id=1, replica_groups={{0,2,4,6,8,10,12,14},{1,3,5,7,9,11,13,15},{16,18,20,22,24,26,28,30},{17..., dimensions={0} | all-to-all | bytes 2097152 | tf_op jit(solution)/shard_map/all_to_all | solution.py:500
  83.5 0.4 pack.1
  83.9 19.2 %all_to_all.31.line = bf16[32,16,128]{2,1,0:T(8,128)(2,1)S(1)} all-to-all(bf16[32,16,128]{2,1,0:T(8,128)(2,1)S(1)} %pack.1), channel_id=1, replica_groups={{0,128,256,384,16,144,272,400,32,160,288,416,48,176,304,432,64,192,320,..., dimensions={0} | all-to-all | bytes 262144 | tf_op jit(solution)/shard_map/all_to_all | solution.py:500
  103.3 0.4 fusion.20
  103.8 0.4 convolution_convert_fusion
  104.6 14.5 %all_to_all.32.line = bf16[32,16,128]{2,1,0:T(8,128)(2,1)S(1)} all-to-all(bf16[32,16,128]{2,1,0:T(8,128)(2,1)S(1)} %bitcast.32), channel_id=1, replica_groups={{0,128,256,384,16,144,272,400,32,160,288,416,48,176,304,432,64,192,320,..., dimensions={0} | all-to-all | bytes 262144 | tf_op jit(solution)/shard_map/all_to_all | solution.py:500
  119.1 0.4 unpack.1
  119.5 14.7 %all_to_all.33.mine = bf16[8,512,128]{2,1,0:T(8,128)(2,1)S(1)} all-to-all(bf16[8,512,128]{2,1,0:T(8,128)(2,1)S(1)} %unpack.1), channel_id=1, replica_groups={{0,2,4,6,8,10,12,14},{1,3,5,7,9,11,13,15},{16,18,20,22,24,26,28,30},{17..., dimensions={0} | all-to-all | bytes 2097152 | tf_op jit(solution)/shard_map/all_to_all | solution.py:500
  134.2 7.3 %collective-permute-start.1 = (bf16[8,512,128]{2,1,0:T(8,128)(2,1)S(1)}, bf16[8,512,128]{2,1,0:T(8,128)(2,1)S(1)}, u32[]{:S(2)}, u32[]{:S(2)}) collective-permute-start(bf16[8,512,128]{2,1,0:T(8,128)(2,1)S(1)} %all_to_all.33.mine), channel_id=1, source_target_pairs={{0,1},{1,0},{2,3},{3,2},{4,5},{5,4},{6,7},{7,6},{8,9},{9,8},{10,11... | collective-permute-start | bytes 3145736 | tf_op jit(solution)/shard_map/ppermute | solution.py:573
  141.5 0.6 pad_maximum_fusion
  142.1 1.7 collective-permute-done.1.other
  143.8 4.1 %back.1 = bf16[4,2,16,2048]{3,2,1,0:T(8,128)(2,1)S(1)} custom-call(bf16[8,512,128]{2,1,0:T(8,128)(2,1)S(1)} %all_to_all.33.mine, bf16[8,512,128]{2,1,0:T(8,128)(2,1)S(1)} %collective-permute-done.1.other, f32[2,256,16,128]{3,2,1,0:T(8,128)} %get-tuple-element.44.phases_in, f32[64,128]{1,0:T(8,128)S(1)} %copy-done.2, f32[64,128]{1,0:T(8,128)S(1)} %copy-done.1, ...), custom_call_target="tpu_custom_call" | custom-call | tf_op jit(solution)/shard_map/back/pallas_call | solution.py:448
  147.9 18.0 %all_to_all.34.terms = bf16[4,2,16,2048]{3,2,1,0:T(8,128)(2,1)S(1)} all-to-all(bf16[4,2,16,2048]{3,2,1,0:T(8,128)(2,1)S(1)} %back.1), channel_id=1, replica_groups=mesh['layer'=4,'facet'=128] {'layer'}, dimensions={0} | all-to-all | bytes 1048576 | tf_op jit(solution)/shard_map/all_to_all | solution.py:500
  165.8 1.0 join.1
  (54 shorter events, 1.6 us)
Async XLA Ops:
  2.9 12.3 %copy-start.9 = (f32[1,8192]{1,0:T(1,128)S(1)}, f32[1,8192]{1,0:T(1,128)}, u32[]{:S(2)}) copy-start(f32[1,8192]{1,0:T(1,128)} %param.23) | copy-start | bytes 98308
  2.9 14.6 %copy-start.13 = (s32[1,1,512]{2,1,0:T(1,128)S(1)}, s32[1,1,512]{2,1,0:T(1,128)}, u32[]{:S(2)}) copy-start(s32[1,1,512]{2,1,0:T(1,128)} %param.29) | copy-start | bytes 6148
  2.9 14.6 %copy-start.14 = (f32[1,8]{1,0:T(1,128)S(1)}, f32[1,8]{1,0:T(1,128)}, u32[]{:S(2)}) copy-start(f32[1,8]{1,0:T(1,128)} %param.26) | copy-start | bytes 100
  2.9 14.6 %copy-start.11 = (s32[1,1,512]{2,1,0:T(1,128)S(1)}, s32[1,1,512]{2,1,0:T(1,128)}, u32[]{:S(2)}) copy-start(s32[1,1,512]{2,1,0:T(1,128)} %param.28) | copy-start | bytes 6148
  3.0 14.6 %copy-start.12 = (s32[1,1,512]{2,1,0:T(1,128)S(1)}, s32[1,1,512]{2,1,0:T(1,128)}, u32[]{:S(2)}) copy-start(s32[1,1,512]{2,1,0:T(1,128)} %param.27) | copy-start | bytes 6148
  3.0 14.7 %copy-start.15 = (f32[7]{0:T(128)S(1)}, f32[7]{0:T(128)}, u32[]{:S(2)}) copy-start(f32[7]{0:T(128)} %param.25) | copy-start | bytes 88
  3.0 15.0 %copy-start.10 = (f32[1,1,2,512]{3,2,1,0:T(2,128)S(1)}, f32[1,1,2,512]{3,2,1,0:T(2,128)}, u32[]{:S(2)}) copy-start(f32[1,1,2,512]{3,2,1,0:T(2,128)} %param.30) | copy-start | bytes 12292
  3.0 15.0 %copy-start.5 = (bf16[256,256]{1,0:T(8,128)(2,1)S(1)}, bf16[256,256]{1,0:T(8,128)(2,1)}, u32[]{:S(2)}) copy-start(bf16[256,256]{1,0:T(8,128)(2,1)} %constant.104.clone) | copy-start | bytes 393220
  3.0 15.0 %copy-start.6 = (bf16[256,256]{1,0:T(8,128)(2,1)S(1)}, bf16[256,256]{1,0:T(8,128)(2,1)}, u32[]{:S(2)}) copy-start(bf16[256,256]{1,0:T(8,128)(2,1)} %constant.103.clone) | copy-start | bytes 393220
  3.0 15.0 %copy-start.7 = (bf16[256,256]{1,0:T(8,128)(2,1)S(1)}, bf16[256,256]{1,0:T(8,128)(2,1)}, u32[]{:S(2)}) copy-start(bf16[256,256]{1,0:T(8,128)(2,1)} %constant.102.clone) | copy-start | bytes 393220
  3.0 15.0 %copy-start.8 = (bf16[256,256]{1,0:T(8,128)(2,1)S(1)}, bf16[256,256]{1,0:T(8,128)(2,1)}, u32[]{:S(2)}) copy-start(bf16[256,256]{1,0:T(8,128)(2,1)} %constant.101.clone) | copy-start | bytes 393220
  3.0 36.4 %all-to-all-start = ((bf16[4,16,12288]{2,1,0:T(8,128)(2,1)}), bf16[4,16,12288]{2,1,0:T(8,128)(2,1)S(1)}, u32[]{:S(2)}, u32[]{:S(2)}) async-start(bf16[4,16,12288]{2,1,0:T(8,128)(2,1)} %gather.1), calls=%async_computation | async-start | bytes 3145728 | tf_op jit(solution)/shard_map/all_to_all | solution.py:500
  14.0 25.4 %copy-start.1 = (f32[64,128]{1,0:T(8,128)S(1)}, f32[64,128]{1,0:T(8,128)}, u32[]{:S(2)}) copy-start(f32[64,128]{1,0:T(8,128)} %constant.106.clone.twist_imag) | copy-start | bytes 98308
  14.0 25.4 %copy-start.2 = (f32[64,128]{1,0:T(8,128)S(1)}, f32[64,128]{1,0:T(8,128)}, u32[]{:S(2)}) copy-start(f32[64,128]{1,0:T(8,128)} %constant.105.clone.twist_real) | copy-start | bytes 98308
  14.0 25.4 %copy-start.4 = (bf16[128,128]{1,0:T(8,128)(2,1)S(1)}, bf16[128,128]{1,0:T(8,128)(2,1)}, u32[]{:S(2)}) copy-start(bf16[128,128]{1,0:T(8,128)(2,1)} %constant.107.clone.first) | copy-start | bytes 98308
  45.3 7.1 %collective-permute-start = (bf16[8,512,128]{2,1,0:T(8,128)(2,1)S(1)}, bf16[8,512,128]{2,1,0:T(8,128)(2,1)S(1)}, u32[]{:S(2)}, u32[]{:S(2)}) collective-permute-start(bf16[8,512,128]{2,1,0:T(8,128)(2,1)S(1)} %get-tuple-element.31), channel_id=1, source_target_pairs={{0,1},{1,0},{2,3},{3,2},{4,5},{5,4},{6,7},{7,6},{8,9},{9,8},{10,11... | collective-permute-start | bytes 3145736 | tf_op jit(solution)/shard_map/ppermute | solution.py:535
  52.4 31.1 %copy-start = (bf16[512,512]{1,0:T(8,128)(2,1)S(1)}, bf16[512,512]{1,0:T(8,128)(2,1)}, u32[]{:S(2)}) copy-start(bf16[512,512]{1,0:T(8,128)(2,1)} %constant.108.clone.table) | copy-start | bytes 1572868
  104.6 39.2 %copy-start.3 = (bf16[128,128]{1,0:T(8,128)(2,1)S(1)}, bf16[128,128]{1,0:T(8,128)(2,1)}, u32[]{:S(2)}) copy-start(bf16[128,128]{1,0:T(8,128)(2,1)} %constant.109.clone.first) | copy-start | bytes 98308
  134.2 9.5 %collective-permute-start.1 = (bf16[8,512,128]{2,1,0:T(8,128)(2,1)S(1)}, bf16[8,512,128]{2,1,0:T(8,128)(2,1)S(1)}, u32[]{:S(2)}, u32[]{:S(2)}) collective-permute-start(bf16[8,512,128]{2,1,0:T(8,128)(2,1)S(1)} %all_to_all.33.mine), channel_id=1, source_target_pairs={{0,1},{1,0},{2,3},{3,2},{4,5},{5,4},{6,7},{7,6},{8,9},{9,8},{10,11... | collective-permute-start | bytes 3145736 | tf_op jit(solution)/shard_map/ppermute | solution.py:573
